TPU v7x, 128 devices: a whole 4x4x4 slice. The times are simulated.
128 devices in a mesh: dom: 32 (over y, x, core), sub: 4 (over z).
Axes of the slice: x: 4, y: 4, z: 4, core: 2. Of those that a mesh axis runs over, the one named last changes fastest.
Arguments:
- solution: float32 [8, 8, 8, 65536], P(None, None, None, ('dom', 'sub')), may hold values from -6 to 6
- forcing: float32 [8, 8, 8, 65536], P(None, None, None, ('dom', 'sub')), may hold values from -600 to 600
- metric: float32 [7, 8, 8, 8, 65536], P(None, None, None, None, ('dom', 'sub')), may hold values from -2.5 to 100, as said below
- entity_ids: int32 [26, 65536], P(None, ('dom', 'sub')), may hold values from 0 to 196607, as said below
- new_owner: int32 [65536], P(('dom', 'sub')), may hold values from 0 to 127, as said below
Outputs:
- smoothed: float32 [8, 8, 8, 65536], P(None, None, None, ('dom', 'sub'))
- moved_metric: float32 [7, 8, 8, 8, 65536], P(None, None, None, None, ('dom', 'sub'))
Inputs may be any that keep to these rules, and one draw needn't show every extreme that they name: `new_owner`: an element stays on its device or goes to one of the device's four neighbours: the previous or next device along dom with the same sub index, or the previous or next along sub with the same dom index, indices wrapping around. Two neighbouring devices hand each other equally many elements, at most 64; in every draw some pair of neighbours along dom and some pair along sub hand each other exactly 64. `entity_ids`: face and edge ids come in blocks of 1536 consecutive ids, corner ids in blocks of 512; block b is summed by device b. Every face id is carried by exactly 2 element faces, every edge id by exactly 4 element edges, every corner id by exactly 8 element corners, their shared nodes lining up in the listed order. An id carried by a device's elements lies in the device's own block or in that of the next device along dom, along sub, or along both (indices wrapping around); every device's elements carry exactly 128 faces, 480 edges and 448 corners of the next block along dom, exactly 128 faces, 480 edges and 448 corners of the next block along sub, and exactly 32 edges, 64 corners and no face of the next block along both. metric[0], metric[1], metric[2] and metric[6] are positive; at every node |metric[3]| <= 0.5 sqrt(metric[0] metric[1]), |metric[4]| <= 0.5 sqrt(metric[0] metric[2]), |metric[5]| <= 0.5 sqrt(metric[1] metric[2]).
All inputs are finite; a program needn't handle non-finite values.
Results may differ from a plain program's by a relative error of at most 0.00005.
Values sent between devices are 32-bit elements; how exact they have to be, the bound alone decides.
A program may use at most 128 MiB of HBM per device.

v0:
```python
import jax
import jax.numpy as jnp
import numpy as np
from jax import lax
from jax.sharding import PartitionSpec as P

EX = 4
EY = 4
EZ = 32
MOVE = 64


RELAX = 0.6


def from_behind(value, axis, steps):
    count = lax.axis_size(axis)
    pairs = [(source, (source + steps) % count) for source in range(count)]
    return lax.ppermute(value, axis, pairs)


def padded(shard, sides, width):
    for axis, dim in sides:
        size, length = (lax.axis_size(axis), shard.shape[dim])
        up = [(i, (i + 1) % size) for i in range(size)]
        down = [(j, i) for i, j in up]
        last = lax.slice_in_dim(shard, length - width, length, axis=dim)
        leading = lax.slice_in_dim(shard, 0, width, axis=dim)
        before = lax.ppermute(last, axis, up)
        after = lax.ppermute(leading, axis, down)
        shard = jnp.concatenate([before, shard, after], axis=dim)
    return shard


def derivative_table(order):
    count = order + 1
    points = -np.cos(np.pi * np.arange(count) / order)
    legendre = np.zeros((count, count))
    for sweep in range(80):
        legendre[:, 0] = 1.0
        legendre[:, 1] = points
        for degree in range(2, count):
            legendre[:, degree] = (
                (2 * degree - 1) * points * legendre[:, degree - 1]
                - (degree - 1) * legendre[:, degree - 2]
            ) / degree
        points = points - (points * legendre[:, order] - legendre[:, order - 1]) / (
            count * legendre[:, order]
        )
    legendre[:, 0] = 1.0
    legendre[:, 1] = points
    for degree in range(2, count):
        legendre[:, degree] = (
            (2 * degree - 1) * points * legendre[:, degree - 1]
            - (degree - 1) * legendre[:, degree - 2]
        ) / degree
    values = legendre[:, order]
    identity = np.eye(count)
    spread = points[:, None] - points[None, :] + identity
    table = values[:, None] / values[None, :] / spread
    table = table * (1.0 - identity)
    table[0, 0] = -order * count / 4.0
    table[order, order] = order * count / 4.0
    return jnp.asarray(table, dtype=jnp.float32)


def element_apply(solution, metric, derivative):
    highest = lax.Precision.HIGHEST
    grad_r = jnp.einsum("ai,ijke->ajke", derivative, solution, precision=highest)
    grad_s = jnp.einsum("bj,ijke->ibke", derivative, solution, precision=highest)
    grad_t = jnp.einsum("ck,ijke->ijce", derivative, solution, precision=highest)
    flux_r = metric[0] * grad_r + metric[3] * grad_s + metric[4] * grad_t
    flux_s = metric[3] * grad_r + metric[1] * grad_s + metric[5] * grad_t
    flux_t = metric[4] * grad_r + metric[5] * grad_s + metric[2] * grad_t
    image = jnp.einsum("ai,ajke->ijke", derivative, flux_r, precision=highest)
    image = image + jnp.einsum("bj,ibke->ijke", derivative, flux_s, precision=highest)
    image = image + jnp.einsum("ck,ijce->ijke", derivative, flux_t, precision=highest)
    image = image + metric[6] * solution
    squared = derivative * derivative
    diagonal = jnp.einsum("ai,ajke->ijke", squared, metric[0], precision=highest)
    diagonal = diagonal + jnp.einsum("bj,ibke->ijke", squared, metric[1], precision=highest)
    diagonal = diagonal + jnp.einsum("ck,ijce->ijke", squared, metric[2], precision=highest)
    along = jnp.diagonal(derivative)
    along_i = along[:, None, None, None]
    along_j = along[None, :, None, None]
    along_k = along[None, None, :, None]
    diagonal = (
        diagonal
        + 2.0 * along_i * along_j * metric[3]
        + 2.0 * along_i * along_k * metric[4]
        + 2.0 * along_j * along_k * metric[5]
    )
    diagonal = diagonal + metric[6]
    return (image, diagonal)


def shared_slots(final_index):
    inside = slice(1, final_index)
    end_points = (0, final_index)
    face_slots = [
        (0, inside, inside),
        (final_index, inside, inside),
        (inside, 0, inside),
        (inside, final_index, inside),
        (inside, inside, 0),
        (inside, inside, final_index),
    ]
    edge_slots = [
        (inside, first_end, second_end) for first_end in end_points for second_end in end_points
    ]
    edge_slots = edge_slots + [
        (first_end, inside, second_end) for first_end in end_points for second_end in end_points
    ]
    edge_slots = edge_slots + [
        (first_end, second_end, inside) for first_end in end_points for second_end in end_points
    ]
    corner_slots = [
        (first_end, second_end, third_end)
        for first_end in end_points
        for second_end in end_points
        for third_end in end_points
    ]
    return (face_slots, edge_slots, corner_slots)


def shared_parts(element_cube):
    face_slots, edge_slots, corner_slots = shared_slots(element_cube.shape[0] - 1)
    face_part = jnp.stack([element_cube[slot_index] for slot_index in face_slots])
    edge_part = jnp.stack([element_cube[slot_index] for slot_index in edge_slots])
    corners = jnp.stack([element_cube[slot_index] for slot_index in corner_slots])
    return (face_part, edge_part, corners)


def place_shared(element_cube, face_part, edge_part, corners):
    face_slots, edge_slots, corner_slots = shared_slots(element_cube.shape[0] - 1)
    for number, slot_index in enumerate(face_slots):
        element_cube = element_cube.at[slot_index].set(face_part[number])
    for number, slot_index in enumerate(edge_slots):
        element_cube = element_cube.at[slot_index].set(edge_part[number])
    for number, slot_index in enumerate(corner_slots):
        element_cube = element_cube.at[slot_index].set(corners[number])
    return element_cube


def pack_values(part):
    kind_count = part.shape[0]
    elem_count = part.shape[-1]
    return jnp.moveaxis(part, 0, -2).reshape(-1, kind_count * elem_count)


def unpack_values(values, part_shape):
    kind_count = part_shape[0]
    return jnp.moveaxis(values.reshape(part_shape[1:-1] + (kind_count, part_shape[-1])), -2, 0)


def select_slots(chosen, capacity):
    ranked = jnp.cumsum(chosen.astype(jnp.int32)) - 1
    return jnp.where(chosen, ranked, capacity)


def pack_columns(values, slots, capacity):
    return jnp.zeros((values.shape[0], capacity), jnp.float32).at[:, slots].set(values, mode="drop")


def pack_index(row_index, slots, capacity, hosted):
    return jnp.full((capacity,), hosted, jnp.int32).at[slots].set(row_index, mode="drop")


def add_rows(totals, values, row_index):
    return totals.at[:, row_index].add(values, mode="drop")


def read_rows(totals, row_index):
    return jnp.take(totals, jnp.clip(row_index, 0, totals.shape[1] - 1), axis=1)


def outgoing_rows(state, source):
    return jnp.take(state, source, axis=1).T


def arrival_rows(dom_got, sub_got, move_cap):
    return jnp.concatenate(
        [dom_got[:move_cap], dom_got[3 * move_cap :], sub_got[:move_cap], sub_got[3 * move_cap :]],
        axis=0,
    )


def land_rows(state, arrived, landing):
    return state.at[:, landing].set(arrived.T, mode="drop")


def on_device(solution, forcing, metric, entity_ids, new_owner):
    dom_count = lax.axis_size("dom")
    sub_count = lax.axis_size("sub")
    dom_index = lax.axis_index("dom")
    sub_index = lax.axis_index("sub")
    own_index = dom_index * sub_count + sub_index
    dom_ahead = (dom_index + 1) % dom_count
    dom_behind = (dom_index + dom_count - 1) % dom_count
    sub_ahead = (sub_index + 1) % sub_count
    sub_behind = (sub_index + sub_count - 1) % sub_count
    next_dom = dom_ahead * sub_count + sub_index
    prev_dom = dom_behind * sub_count + sub_index
    next_sub = dom_index * sub_count + sub_ahead
    prev_sub = dom_index * sub_count + sub_behind
    next_both = dom_ahead * sub_count + sub_ahead
    elem_count = solution.shape[-1]
    metric_rows = metric.reshape(-1, elem_count)
    departed = new_owner != own_index
    column = jnp.full((elem_count,), 4 * MOVE, jnp.int32)
    count_list = []
    for direction, target in enumerate((prev_dom, next_dom, prev_sub, next_sub)):
        chosen = departed & (new_owner == target)
        ranked = jnp.cumsum(chosen.astype(jnp.int32)) - 1
        column = jnp.where(chosen, direction * MOVE + ranked, column)
        count_list.append(jnp.sum(chosen.astype(jnp.int32)))
    source = (
        jnp.zeros((4 * MOVE,), jnp.int32)
        .at[column]
        .set(jnp.arange(elem_count, dtype=jnp.int32), mode="drop")
    )
    counts = jnp.stack(count_list)
    offsets = jnp.cumsum(counts) - counts
    hole_rank = jnp.cumsum(departed.astype(jnp.int32)) - 1
    hole_slot = (
        jnp.zeros((elem_count,), jnp.int32)
        .at[jnp.where(departed, hole_rank, elem_count)]
        .set(jnp.arange(elem_count, dtype=jnp.int32), mode="drop")
    )
    arrive_index = jnp.arange(4 * MOVE, dtype=jnp.int32)
    arrive_dir = arrive_index // MOVE
    arrive_pos = arrive_index % MOVE
    filled = arrive_pos < counts[arrive_dir]
    landing = jnp.where(
        filled, hole_slot[jnp.clip(offsets[arrive_dir] + arrive_pos, 0, elem_count - 1)], elem_count
    )
    derivative = derivative_table(solution.shape[0] - 1)
    image, diagonal = element_apply(solution, metric, derivative)
    stacked_pair = jnp.stack([image, diagonal], axis=3)
    parts = shared_parts(stacked_pair)
    blocks = (3 * elem_count, 3 * elem_count, elem_count)
    id_ranges = ((0, 6), (6, 18), (18, 26))
    dom_caps = (EY * EZ, EZ * (4 * EY - 1), EZ * (4 * EY - 2))
    sub_caps = (EX * EZ, EZ * (4 * EX - 1), EZ * (4 * EX - 2))
    both_caps = (0, EZ, 2 * EZ)
    totals_list, owner_list, index_list = ([], [], [])
    dom_slots, dom_out, dom_rows = ([], [], [])
    sub_slots, sub_out, sub_rows = ([], [], [])
    both_slots, both_out, both_rows = ([None], [None], [None])
    for kind_index in range(3):
        start_row, stop_row = id_ranges[kind_index]
        id_list = entity_ids[start_row:stop_row].reshape(-1)
        hosted = blocks[kind_index]
        owner_dev = id_list // hosted
        row_index = id_list % hosted
        values = pack_values(parts[kind_index])
        totals = jnp.zeros((values.shape[0], hosted), jnp.float32)
        totals = add_rows(totals, values, jnp.where(owner_dev == own_index, row_index, hosted))
        totals_list.append(totals)
        owner_list.append(owner_dev)
        index_list.append(row_index)
        slot_dom = select_slots(owner_dev == next_dom, dom_caps[kind_index])
        dom_slots.append(slot_dom)
        dom_out.append(pack_columns(values, slot_dom, dom_caps[kind_index]))
        dom_rows.append(pack_index(row_index, slot_dom, dom_caps[kind_index], hosted))
        slot_sub = select_slots(owner_dev == next_sub, sub_caps[kind_index])
        sub_slots.append(slot_sub)
        sub_out.append(pack_columns(values, slot_sub, sub_caps[kind_index]))
        sub_rows.append(pack_index(row_index, slot_sub, sub_caps[kind_index], hosted))
        if kind_index > 0:
            slot_both = select_slots(owner_dev == next_both, both_caps[kind_index])
            both_slots.append(slot_both)
            both_out.append(pack_columns(values, slot_both, both_caps[kind_index]))
            both_rows.append(pack_index(row_index, slot_both, both_caps[kind_index], hosted))
    got_dom = from_behind(
        (
            dom_out[0],
            dom_out[1],
            dom_out[2],
            both_out[1],
            both_out[2],
            dom_rows[0],
            dom_rows[1],
            dom_rows[2],
            both_rows[1],
            both_rows[2],
        ),
        "dom",
        1,
    )
    for kind_index in range(3):
        totals_list[kind_index] = add_rows(
            totals_list[kind_index], got_dom[kind_index], got_dom[5 + kind_index]
        )
    got_sub = from_behind(
        (
            sub_out[0],
            sub_out[1],
            sub_out[2],
            got_dom[3],
            got_dom[4],
            sub_rows[0],
            sub_rows[1],
            sub_rows[2],
            got_dom[8],
            got_dom[9],
        ),
        "sub",
        1,
    )
    for kind_index in range(3):
        totals_list[kind_index] = add_rows(
            totals_list[kind_index], got_sub[kind_index], got_sub[5 + kind_index]
        )
    totals_list[1] = add_rows(totals_list[1], got_sub[3], got_sub[8])
    totals_list[2] = add_rows(totals_list[2], got_sub[4], got_sub[9])
    back_sub = from_behind(
        (
            read_rows(totals_list[0], got_sub[5]),
            read_rows(totals_list[1], got_sub[6]),
            read_rows(totals_list[2], got_sub[7]),
            read_rows(totals_list[1], got_sub[8]),
            read_rows(totals_list[2], got_sub[9]),
        ),
        "sub",
        -1,
    )
    back_dom = from_behind(
        (
            read_rows(totals_list[0], got_dom[5]),
            read_rows(totals_list[1], got_dom[6]),
            read_rows(totals_list[2], got_dom[7]),
            back_sub[3],
            back_sub[4],
        ),
        "dom",
        -1,
    )
    merged_parts = []
    for kind_index in range(3):
        owner_dev = owner_list[kind_index]
        merged = read_rows(totals_list[kind_index], index_list[kind_index])
        from_dom = jnp.take(
            back_dom[kind_index],
            jnp.clip(dom_slots[kind_index], 0, dom_caps[kind_index] - 1),
            axis=1,
        )
        merged = jnp.where((owner_dev == next_dom)[None, :], from_dom, merged)
        from_sub = jnp.take(
            back_sub[kind_index],
            jnp.clip(sub_slots[kind_index], 0, sub_caps[kind_index] - 1),
            axis=1,
        )
        merged = jnp.where((owner_dev == next_sub)[None, :], from_sub, merged)
        if kind_index > 0:
            from_both = jnp.take(
                back_dom[2 + kind_index],
                jnp.clip(both_slots[kind_index], 0, both_caps[kind_index] - 1),
                axis=1,
            )
            merged = jnp.where((owner_dev == next_both)[None, :], from_both, merged)
        merged_parts.append(unpack_values(merged, parts[kind_index].shape))
    assembled = place_shared(stacked_pair, merged_parts[0], merged_parts[1], merged_parts[2])
    relaxed = solution + RELAX * (forcing - assembled[:, :, :, 0]) / assembled[:, :, :, 1]
    relaxed_rows = relaxed.reshape(-1, elem_count)
    field_rows = relaxed_rows.shape[0]
    moving = jnp.concatenate([relaxed_rows, metric_rows], axis=0)
    leaving_rows = outgoing_rows(moving, source)
    moved_dom = padded(leaving_rows[: 2 * MOVE], (("dom", 0),), MOVE)
    moved_sub = padded(leaving_rows[2 * MOVE :], (("sub", 0),), MOVE)
    landed = land_rows(moving, arrival_rows(moved_dom, moved_sub, MOVE), landing)
    smoothed = landed[:field_rows].reshape(solution.shape)
    moved_metric = landed[field_rows:].reshape(metric.shape)
    return (smoothed, moved_metric)


def solution(mesh):
    placed = (
        P(None, None, None, ("dom", "sub")),
        P(None, None, None, ("dom", "sub")),
        P(None, None, None, None, ("dom", "sub")),
        P(None, ("dom", "sub")),
        P(("dom", "sub")),
    )
    return jax.shard_map(
        on_device,
        mesh=mesh,
        in_specs=placed,
        out_specs=(P(None, None, None, ("dom", "sub")), P(None, None, None, None, ("dom", "sub"))),
        check_vma=False,
    )
```

profile of v0, /device:TPU:0, one launch (start us, length us, event | category | flops | bytes accessed | tf_op | source)
XLA Modules:
  0.0 821.0 jit_solution(15832955976892037090)
XLA Ops:
  6.1 16.0 %scatter_custom_fusion.17 = s32[64]{0:T(128)} fusion(s32[4096]{0:T(1024)S(1)} %bitcast.639, s32[4096]{0:T(1024)S(1)} %get-tuple-element.336, s32[]{:T(128)} %constant.1248.clone.1), kind=kCustom, calls=%fused_computation.552 | custom fusion | bytes 260 | tf_op jit(solution)/shard_map/scatter | solution.py:166
  22.0 16.0 %scatter_custom_fusion.19 = s32[448]{0:T(512)} fusion(s32[4096]{0:T(1024)S(1)} %bitcast.635, s32[4096]{0:T(1024)S(1)} %get-tuple-element.336, s32[]{:T(128)} %constant.1248.clone.1), kind=kCustom, calls=%fused_computation.541 | custom fusion | bytes 1796 | tf_op jit(solution)/shard_map/scatter | solution.py:166
  39.8 16.0 %scatter_custom_fusion.22 = s32[448]{0:T(512)} fusion(s32[4096]{0:T(1024)S(1)} %bitcast.637, s32[4096]{0:T(1024)S(1)} %get-tuple-element.336, s32[]{:T(128)} %constant.1248.clone.1), kind=kCustom, calls=%fused_computation.539 | custom fusion | bytes 1796 | tf_op jit(solution)/shard_map/scatter | solution.py:166
  61.8 12.3 %scatter_custom_fusion.4 = s32[128]{0:T(128)} fusion(s32[3072]{0:T(1024)S(1)} %bitcast.641, s32[3072]{0:T(1024)S(1)} %add_select_fusion.6, s32[]{:T(128)} %constant.1226.clone.1), kind=kCustom, calls=%fused_computation.556 | custom fusion | bytes 516 | tf_op jit(solution)/shard_map/scatter | solution.py:166
  82.6 23.4 %scatter_custom_fusion.7 = s32[32]{0:T(128)} fusion(s32[6144]{0:T(1024)S(1)} %bitcast.632, s32[6144]{0:T(1024)S(1)} %add_select_fusion, s32[]{:T(128)} %constant.1226.clone.1), kind=kCustom, calls=%fused_computation.554 | custom fusion | bytes 132 | tf_op jit(solution)/shard_map/scatter | solution.py:166
  153.2 12.5 %scatter_custom_fusion.1 = s32[128]{0:T(128)} fusion(s32[3072]{0:T(1024)S(1)} %bitcast.644, s32[3072]{0:T(1024)} %copy-done.73, s32[]{:T(128)} %constant.1226.clone.1), kind=kCustom, calls=%fused_computation.558 | custom fusion | bytes 1024 | tf_op jit(solution)/shard_map/scatter | solution.py:166
  193.0 11.9 %scatter_custom_fusion.25 = f32[2,64]{0,1:T(8,128)} fusion(s32[4096]{0:T(1024)} %bitcast.640, f32[4096,2]{1,0:T(8,128)} %bitcast.588, f32[]{:T(128)} %constant.1234.clone.1), kind=kCustom, calls=%fused_computation.377 | custom fusion | bytes 1024 | tf_op jit(solution)/shard_map/scatter | solution.py:162
  204.9 11.6 %scatter_custom_fusion.23 = f32[2,448]{0,1:T(8,128)} fusion(s32[4096]{0:T(1024)} %bitcast.638, f32[4096,2]{1,0:T(8,128)} %bitcast.589, f32[]{:T(128)} %constant.1234.clone.1), kind=kCustom, calls=%fused_computation.224 | custom fusion | bytes 4096 | tf_op jit(solution)/shard_map/scatter | solution.py:162
  216.5 11.6 %scatter_custom_fusion.20 = f32[2,448]{0,1:T(8,128)} fusion(s32[4096]{0:T(1024)} %bitcast.636, f32[4096,2]{1,0:T(8,128)} %bitcast.590, f32[]{:T(128)} %constant.1234.clone.1), kind=kCustom, calls=%fused_computation.226 | custom fusion | bytes 4096 | tf_op jit(solution)/shard_map/scatter | solution.py:162
  228.0 23.7 %scatter_custom_fusion.12 = s32[480]{0:T(512)} fusion(s32[6144]{0:T(1024)} %bitcast.630, s32[6144]{0:T(1024)} %copy-done.61, s32[]{:T(128)} %constant.1226.clone.1), kind=kCustom, calls=%fused_computation.543 | custom fusion | bytes 2432 | tf_op jit(solution)/shard_map/scatter | solution.py:166
  255.5 16.4 %scatter_custom_fusion.15 = f32[12,32]{0,1:T(8,128)} fusion(s32[6144]{0:T(1024)} %bitcast.633, f32[6144,12]{1,0:T(8,128)} %copy.818, f32[]{:T(128)} %constant.1234.clone.1), kind=kCustom, calls=%fused_computation.426 | custom fusion | bytes 2048 | tf_op jit(solution)/shard_map/scatter | solution.py:162
  271.9 16.5 %scatter_custom_fusion.13 = f32[12,480]{0,1:T(8,128)} fusion(s32[6144]{0:T(1024)} %bitcast.631, f32[6144,12]{1,0:T(8,128)} %copy.818, f32[]{:T(128)} %constant.1234.clone.1), kind=kCustom, calls=%fused_computation.220 | custom fusion | bytes 23552 | tf_op jit(solution)/shard_map/scatter | solution.py:162
  288.5 23.7 %scatter_custom_fusion.9 = s32[480]{0:T(512)} fusion(s32[6144]{0:T(1024)} %bitcast.628, s32[6144]{0:T(1024)} %copy-done.61, s32[]{:T(128)} %constant.1226.clone.1), kind=kCustom, calls=%fused_computation.545 | custom fusion | bytes 2432 | tf_op jit(solution)/shard_map/scatter | solution.py:166
  312.1 16.7 %scatter_custom_fusion.10 = f32[12,480]{0,1:T(8,128)} fusion(s32[6144]{0:T(1024)} %bitcast.629, f32[6144,12]{1,0:T(8,128)} %copy.818, f32[]{:T(128)} %constant.1234.clone.1), kind=kCustom, calls=%fused_computation.222 | custom fusion | bytes 23552 | tf_op jit(solution)/shard_map/scatter | solution.py:162
  338.6 17.5 %scatter_custom_fusion = f32[72,1536]{0,1:T(8,128)S(1)} fusion(s32[3072]{0:T(1024)} %bitcast.643, f32[3072,72]{1,0:T(8,128)} %copy.788, f32[]{:T(128)} %constant.1234.clone.1), kind=kCustom, calls=%fused_computation.178 | custom fusion | flops 221184 | bytes 442880 | tf_op jit(solution)/shard_map/scatter-add | solution.py:170
  358.1 22.7 %scatter_custom_fusion.18 = f32[2,512]{0,1:T(8,128)S(1)} fusion(s32[4096]{0:T(1024)} %bitcast.634, f32[4096,2]{1,0:T(8,128)} %bitcast.591, f32[]{:T(128)} %constant.1234.clone.1), kind=kCustom, calls=%fused_computation.218 | custom fusion | flops 8192 | bytes 4608 | tf_op jit(solution)/shard_map/scatter-add | solution.py:170
  382.6 33.7 %scatter_custom_fusion.8 = f32[12,1536]{0,1:T(8,128)S(1)} fusion(s32[6144]{0:T(1024)} %bitcast.627, f32[6144,12]{1,0:T(8,128)} %copy.818, f32[]{:T(128)} %constant.1234.clone.1), kind=kCustom, calls=%fused_computation.176 | custom fusion | flops 73728 | bytes 74240 | tf_op jit(solution)/shard_map/scatter-add | solution.py:170
  469.7 14.1 %gather_fusion.7 = f32[4096,2]{1,0:T(8,128)} fusion(f32[2,512]{0,1:T(8,128)S(1)} %scatter_custom_fusion.26, s32[4096]{0:T(1024)S(1)} %copy-done.35), kind=kCustom, calls=%fused_computation.19 | custom fusion | bytes 81920 | tf_op jit(solution)/shard_map/jit(_take)/gather | solution.py:174
  484.5 14.1 %gather_fusion.6 = f32[4096,2]{1,0:T(8,128)} fusion(f32[2,64]{0,1:T(8,128)S(1)} %collective-permute-done.27, s32[4096]{0:T(1024)S(1)} %get-tuple-element.516), kind=kCustom, calls=%fused_computation.18 | custom fusion | bytes 81920 | tf_op jit(solution)/shard_map/jit(_take)/gather | solution.py:356
  498.6 14.1 %gather_fusion.21 = f32[4096,2]{1,0:T(8,128)} fusion(f32[2,448]{0,1:T(8,128)S(1)} %collective-permute-done.29, s32[4096]{0:T(1024)S(1)} %copy-done.34), kind=kCustom, calls=%fused_computation.11.clone | custom fusion | bytes 81920 | tf_op jit(solution)/shard_map/jit(_take)/gather | solution.py:343
  515.3 14.1 %gather_fusion.19 = f32[4096,2]{1,0:T(8,128)} fusion(f32[2,448]{0,1:T(8,128)S(1)} %collective-permute-done.28, s32[4096]{0:T(1024)S(1)} %copy-done.33), kind=kCustom, calls=%fused_computation.5.clone | custom fusion | bytes 81920 | tf_op jit(solution)/shard_map/jit(_take)/gather | solution.py:349
  529.4 9.2 %fusion.11 = f32[2,4096]{0,1:T(8,128)} fusion(f32[4096,2]{1,0:T(8,128)} %gather_fusion.21, f32[4096,2]{1,0:T(8,128)} %gather_fusion.19, f32[4096,2]{1,0:T(8,128)} %gather_fusion.7, f32[4096,2]{1,0:T(8,128)} %gather_fusion.6, pred[4096]{0:T(1024)(128)(4,1)} %get-tuple-element.467, pred[4096]{0:T(1024)(128)(4,1)} %get-tuple-element.337, ...), kind=kLoop, calls=%fused_computation.119 | loop fusion | flops 57344 | bytes 192512 | tf_op jit(solution)/shard_map/jit(_where)/select_n | solution.py:361
  560.3 22.0 %gather_fusion.4 = f32[6144,12]{1,0:T(8,128)} fusion(f32[12,1536]{0,1:T(8,128)} %copy-done.2, s32[6144]{0:T(1024)S(1)} %get-tuple-element.511), kind=kCustom, calls=%fused_computation.16 | custom fusion | bytes 614400 | tf_op jit(solution)/shard_map/jit(_take)/gather | solution.py:174
  582.3 20.9 %gather_fusion.3 = f32[6144,12]{1,0:T(8,128)} fusion(f32[12,32]{0,1:T(8,128)S(1)} %collective-permute-done.15, s32[6144]{0:T(1024)S(1)} %get-tuple-element.512), kind=kCustom, calls=%fused_computation.15 | custom fusion | bytes 614400 | tf_op jit(solution)/shard_map/jit(_take)/gather | solution.py:356
  610.1 10.8 %gather_fusion.1 = f32[3072,72]{1,0:T(8,128)} fusion(f32[72,1536]{0,1:T(8,128)S(1)} %scatter_custom_fusion.6, s32[3072]{0:T(1024)S(1)} %copy-done.43), kind=kCustom, calls=%fused_computation.13 | custom fusion | bytes 1781760 | tf_op jit(solution)/shard_map/jit(_take)/gather | solution.py:174
  620.9 20.9 %gather_fusion.17 = f32[6144,12]{1,0:T(8,128)} fusion(f32[12,480]{0,1:T(8,128)S(1)} %collective-permute-done.17, s32[6144]{0:T(1024)S(1)} %get-tuple-element.510), kind=kCustom, calls=%fused_computation.9.clone | custom fusion | bytes 614400 | tf_op jit(solution)/shard_map/jit(_take)/gather | solution.py:343
  641.9 20.9 %gather_fusion.15 = f32[6144,12]{1,0:T(8,128)} fusion(f32[12,480]{0,1:T(8,128)S(1)} %collective-permute-done.16, s32[6144]{0:T(1024)S(1)} %get-tuple-element.509), kind=kCustom, calls=%fused_computation.3.clone | custom fusion | bytes 614400 | tf_op jit(solution)/shard_map/jit(_take)/gather | solution.py:349
  662.8 10.3 %fusion.9 = f32[12,6144]{0,1:T(8,128)} fusion(f32[6144,12]{1,0:T(8,128)} %gather_fusion.17, f32[6144,12]{1,0:T(8,128)} %gather_fusion.15, f32[6144,12]{1,0:T(8,128)} %gather_fusion.4, f32[6144,12]{1,0:T(8,128)} %gather_fusion.3, pred[6144]{0:T(1024)(128)(4,1)S(1)} %copy-done.60, pred[6144]{0:T(1024)(128)(4,1)S(1)} %copy-done.59, ...), kind=kLoop, calls=%fused_computation.116 | loop fusion | flops 516096 | bytes 1517568 | tf_op jit(solution)/shard_map/jit(_where)/select_n | solution.py:361
  681.5 10.8 %gather_fusion.13 = f32[3072,72]{1,0:T(8,128)} fusion(f32[72,128]{0,1:T(8,128)S(1)} %collective-permute-done.5, s32[3072]{0:T(1024)S(1)} %copy-done.42), kind=kCustom, calls=%fused_computation.7.clone | custom fusion | bytes 1781760 | tf_op jit(solution)/shard_map/jit(_take)/gather | solution.py:343
  692.4 10.8 %gather_fusion.11 = f32[3072,72]{1,0:T(8,128)} fusion(f32[72,128]{0,1:T(8,128)S(1)} %collective-permute-done.4, s32[3072]{0:T(1024)S(1)} %copy-done.41), kind=kCustom, calls=%fused_computation.1.clone | custom fusion | bytes 1781760 | tf_op jit(solution)/shard_map/jit(_take)/gather | solution.py:349
  750.7 9.2 %gather_fusion.9 = f32[256,4096]{1,0:T(8,128)} fusion(f32[4096,512]{0,1:T(8,128)} %pad_maximum_fusion.1, s32[1024]{0:T(1024)} %pad_clamp_fusion), kind=kCustom, calls=%fused_computation.21 | custom fusion | bytes 8389632 | tf_op jit(solution)/shard_map/jit(_take)/gather | solution.py:178
  792.5 10.5 %scatter_custom_fusion.29 = f32[4096,512]{0,1:T(8,128)} fusion(f32[4096,512]{0,1:T(8,128)} %pad_maximum_fusion.1, s32[256]{0:T(256)S(1)} %bitcast.648, f32[64,4096]{1,0:T(8,128)} %collective-permute-done.33, f32[]{:T(128)} %constant.1293, f32[64,4096]{1,0:T(8,128)S(1)} %collective-permute-done.32, f32[64,4096]{1,0:T(8,128)S(1)} %collective-permute-done.31, ...), kind=kCustom, calls=%fused_computation.106 | custom fusion | flops 3145728 | bytes 12583424 | tf_op jit(solution)/shard_map/scatter | solution.py:189
  (509 shorter events, 303.1 us)
Async XLA Ops:
  22.0 398.1 %collective-permute-start.18 = (s32[64]{0:T(128)}, s32[64]{0:T(128)}, u32[]{:S(2)}, u32[]{:S(2)}) collective-permute-start(s32[64]{0:T(128)} %scatter_custom_fusion.17), channel_id=1, source_target_pairs={{0,4},{4,8},{8,12},{12,16},{16,20},{20,24},{24,28},{28,32},{32,36}... | collective-permute-start | bytes 776 | tf_op jit(solution)/shard_map/ppermute | solution.py:19
  38.1 394.8 %collective-permute-start.20 = (s32[448]{0:T(512)}, s32[448]{0:T(512)}, u32[]{:S(2)}, u32[]{:S(2)}) collective-permute-start(s32[448]{0:T(512)} %scatter_custom_fusion.19), channel_id=1, source_target_pairs={{0,4},{4,8},{8,12},{12,16},{16,20},{20,24},{24,28},{28,32},{32,36}... | collective-permute-start | bytes 5384 | tf_op jit(solution)/shard_map/ppermute | solution.py:19
  55.8 379.4 %collective-permute-start.22 = (s32[448]{0:T(512)}, s32[448]{0:T(512)}, u32[]{:S(2)}, u32[]{:S(2)}) collective-permute-start(s32[448]{0:T(512)} %scatter_custom_fusion.22), channel_id=1, source_target_pairs={{0,1},{1,2},{2,3},{3,0},{4,5},{5,6},{6,7},{7,4},{8,9},{9,10},{10,1... | collective-permute-start | bytes 5384 | tf_op jit(solution)/shard_map/ppermute | solution.py:19
  74.1 352.5 %collective-permute-start.2 = (s32[128]{0:T(128)}, s32[128]{0:T(128)}, u32[]{:S(2)}, u32[]{:S(2)}) collective-permute-start(s32[128]{0:T(128)} %scatter_custom_fusion.4), channel_id=1, source_target_pairs={{0,1},{1,2},{2,3},{3,0},{4,5},{5,6},{6,7},{7,4},{8,9},{9,10},{10,1... | collective-permute-start | bytes 1544 | tf_op jit(solution)/shard_map/ppermute | solution.py:19
  106.0 274.9 %collective-permute-start.6 = (s32[32]{0:T(128)}, s32[32]{0:T(128)}, u32[]{:S(2)}, u32[]{:S(2)}) collective-permute-start(s32[32]{0:T(128)} %scatter_custom_fusion.7), channel_id=1, source_target_pairs={{0,4},{4,8},{8,12},{12,16},{16,20},{20,24},{24,28},{28,32},{32,36}... | collective-permute-start | bytes 392 | tf_op jit(solution)/shard_map/ppermute | solution.py:19
  380.9 35.4 %collective-permute-start.7 = (s32[32]{0:T(128)}, s32[32]{0:T(128)}, u32[]{:S(2)}, u32[]{:S(2)}) collective-permute-start(s32[32]{0:T(128)} %collective-permute-done.6), channel_id=1, source_target_pairs={{0,1},{1,2},{2,3},{3,0},{4,5},{5,6},{6,7},{7,4},{8,9},{9,10},{10,1... | collective-permute-start | bytes 392 | tf_op jit(solution)/shard_map/ppermute | solution.py:19
  416.3 13.5 %collective-permute-start = (s32[128]{0:T(128)}, s32[128]{0:T(128)S(1)}, u32[]{:S(2)}, u32[]{:S(2)}) collective-permute-start(s32[128]{0:T(128)} %scatter_custom_fusion.1), channel_id=1, source_target_pairs={{0,4},{4,8},{8,12},{12,16},{16,20},{20,24},{24,28},{28,32},{32,36}... | collective-permute-start | bytes 1544 | tf_op jit(solution)/shard_map/ppermute | solution.py:19
  425.0 14.8 %collective-permute-start.8 = (s32[480]{0:T(512)}, s32[480]{0:T(512)S(1)}, u32[]{:S(2)}, u32[]{:S(2)}) collective-permute-start(s32[480]{0:T(512)} %scatter_custom_fusion.9), channel_id=1, source_target_pairs={{0,4},{4,8},{8,12},{12,16},{16,20},{20,24},{24,28},{28,32},{32,36}... | collective-permute-start | bytes 5768 | tf_op jit(solution)/shard_map/ppermute | solution.py:19
  426.6 14.4 %collective-permute-start.10 = (s32[480]{0:T(512)}, s32[480]{0:T(512)S(1)}, u32[]{:S(2)}, u32[]{:S(2)}) collective-permute-start(s32[480]{0:T(512)} %scatter_custom_fusion.12), channel_id=1, source_target_pairs={{0,1},{1,2},{2,3},{3,0},{4,5},{5,6},{6,7},{7,4},{8,9},{9,10},{10,1... | collective-permute-start | bytes 5768 | tf_op jit(solution)/shard_map/ppermute | solution.py:19
  429.8 173.4 %collective-permute-start.1 = (f32[72,128]{0,1:T(8,128)}, f32[72,128]{0,1:T(8,128)}, u32[]{:S(2)}, u32[]{:S(2)}) collective-permute-start(f32[72,128]{0,1:T(8,128)} %scatter_custom_fusion.2), channel_id=1, source_target_pairs={{0,4},{4,8},{8,12},{12,16},{16,20},{20,24},{24,28},{28,32},{32,36}... | collective-permute-start | bytes 110600 | tf_op jit(solution)/shard_map/ppermute | solution.py:19
  432.8 8.1 collective-permute-start.24
  435.2 8.8 %collective-permute-start.21 = (f32[2,448]{0,1:T(8,128)S(1)}, f32[2,448]{0,1:T(8,128)S(1)}, u32[]{:S(2)}, u32[]{:S(2)}) collective-permute-start(f32[2,448]{0,1:T(8,128)S(1)} %copy-done.9), channel_id=1, source_target_pairs={{0,4},{4,8},{8,12},{12,16},{16,20},{20,24},{24,28},{28,32},{32,36}... | collective-permute-start | bytes 10760 | tf_op jit(solution)/shard_map/ppermute | solution.py:19
  439.8 9.5 %collective-permute-start.23 = (f32[2,448]{0,1:T(8,128)S(1)}, f32[2,448]{0,1:T(8,128)}, u32[]{:S(2)}, u32[]{:S(2)}) collective-permute-start(f32[2,448]{0,1:T(8,128)S(1)} %copy-done.8), channel_id=1, source_target_pairs={{0,1},{1,2},{2,3},{3,0},{4,5},{5,6},{6,7},{7,4},{8,9},{9,10},{10,1... | collective-permute-start | bytes 10760 | tf_op jit(solution)/shard_map/ppermute | solution.py:19
  441.0 71.8 %collective-permute-start.12 = (f32[12,32]{0,1:T(8,128)}, f32[12,32]{0,1:T(8,128)}, u32[]{:S(2)}, u32[]{:S(2)}) collective-permute-start(f32[12,32]{0,1:T(8,128)} %scatter_custom_fusion.15), channel_id=1, source_target_pairs={{0,4},{4,8},{8,12},{12,16},{16,20},{20,24},{24,28},{28,32},{32,36}... | collective-permute-start | bytes 4616 | tf_op jit(solution)/shard_map/ppermute | solution.py:19
  441.0 11.7 %collective-permute-start.25 = (f32[2,64]{0,1:T(8,128)}, f32[2,64]{0,1:T(8,128)S(1)}, u32[]{:S(2)}, u32[]{:S(2)}) collective-permute-start(f32[2,64]{0,1:T(8,128)} %collective-permute-done.24), channel_id=1, source_target_pairs={{0,1},{1,2},{2,3},{3,0},{4,5},{5,6},{6,7},{7,4},{8,9},{9,10},{10,1... | collective-permute-start | bytes 1544 | tf_op jit(solution)/shard_map/ppermute | solution.py:19
  455.9 12.6 %collective-permute-start.26 = (f32[2,64]{0,1:T(8,128)}, f32[2,64]{0,1:T(8,128)}, u32[]{:S(2)}, u32[]{:S(2)}) collective-permute-start(f32[2,64]{0,1:T(8,128)} %select_bitcast_fusion.6), channel_id=1, source_target_pairs={{0,3},{1,0},{2,1},{3,2},{4,7},{5,4},{6,5},{7,6},{8,11},{9,8},{10,9... | collective-permute-start | bytes 1544 | tf_op jit(solution)/shard_map/ppermute | solution.py:19
  462.5 51.1 %collective-permute-start.28 = (f32[2,448]{0,1:T(8,128)}, f32[2,448]{0,1:T(8,128)S(1)}, u32[]{:S(2)}, u32[]{:S(2)}) collective-permute-start(f32[2,448]{0,1:T(8,128)} %select_bitcast_fusion.3), channel_id=1, source_target_pairs={{0,3},{1,0},{2,1},{3,2},{4,7},{5,4},{6,5},{7,6},{8,11},{9,8},{10,9... | collective-permute-start | bytes 10760 | tf_op jit(solution)/shard_map/ppermute | solution.py:19
  464.3 34.3 %collective-permute-start.29 = (f32[2,448]{0,1:T(8,128)}, f32[2,448]{0,1:T(8,128)S(1)}, u32[]{:S(2)}, u32[]{:S(2)}) collective-permute-start(f32[2,448]{0,1:T(8,128)} %select_bitcast_fusion.2), channel_id=1, source_target_pairs={{0,124},{4,0},{8,4},{12,8},{16,12},{20,16},{24,20},{28,24},{32,28}... | collective-permute-start | bytes 10760 | tf_op jit(solution)/shard_map/ppermute | solution.py:19
  468.5 15.3 %collective-permute-start.27 = (f32[2,64]{0,1:T(8,128)}, f32[2,64]{0,1:T(8,128)S(1)}, u32[]{:S(2)}, u32[]{:S(2)}) collective-permute-start(f32[2,64]{0,1:T(8,128)} %collective-permute-done.26), channel_id=1, source_target_pairs={{0,124},{4,0},{8,4},{12,8},{16,12},{20,16},{24,20},{28,24},{32,28}... | collective-permute-start | bytes 1544 | tf_op jit(solution)/shard_map/ppermute | solution.py:19
  483.8 121.3 %collective-permute-start.3 = (f32[72,128]{0,1:T(8,128)}, f32[72,128]{0,1:T(8,128)}, u32[]{:S(2)}, u32[]{:S(2)}) collective-permute-start(f32[72,128]{0,1:T(8,128)} %scatter_custom_fusion.5), channel_id=1, source_target_pairs={{0,1},{1,2},{2,3},{3,0},{4,5},{5,6},{6,7},{7,4},{8,9},{9,10},{10,1... | collective-permute-start | bytes 110600 | tf_op jit(solution)/shard_map/ppermute | solution.py:19
  498.6 42.9 %collective-permute-start.9 = (f32[12,480]{0,1:T(8,128)}, f32[12,480]{0,1:T(8,128)S(1)}, u32[]{:S(2)}, u32[]{:S(2)}) collective-permute-start(f32[12,480]{0,1:T(8,128)} %scatter_custom_fusion.10), channel_id=1, source_target_pairs={{0,4},{4,8},{8,12},{12,16},{16,20},{20,24},{24,28},{28,32},{32,36}... | collective-permute-start | bytes 69128 | tf_op jit(solution)/shard_map/ppermute | solution.py:19
  512.7 32.5 %collective-permute-start.11 = (f32[12,480]{0,1:T(8,128)}, f32[12,480]{0,1:T(8,128)S(1)}, u32[]{:S(2)}, u32[]{:S(2)}) collective-permute-start(f32[12,480]{0,1:T(8,128)} %scatter_custom_fusion.13), channel_id=1, source_target_pairs={{0,1},{1,2},{2,3},{3,0},{4,5},{5,6},{6,7},{7,4},{8,9},{9,10},{10,1... | collective-permute-start | bytes 69128 | tf_op jit(solution)/shard_map/ppermute | solution.py:19
  513.6 35.3 %collective-permute-start.13 = (f32[12,32]{0,1:T(8,128)}, f32[12,32]{0,1:T(8,128)S(1)}, u32[]{:S(2)}, u32[]{:S(2)}) collective-permute-start(f32[12,32]{0,1:T(8,128)} %collective-permute-done.12), channel_id=1, source_target_pairs={{0,1},{1,2},{2,3},{3,0},{4,5},{5,6},{6,7},{7,4},{8,9},{9,10},{10,1... | collective-permute-start | bytes 4616 | tf_op jit(solution)/shard_map/ppermute | solution.py:19
  554.9 87.0 %collective-permute-start.16 = (f32[12,480]{0,1:T(8,128)S(1)}, f32[12,480]{0,1:T(8,128)S(1)}, u32[]{:S(2)}, u32[]{:S(2)}) collective-permute-start(f32[12,480]{0,1:T(8,128)S(1)} %select_bitcast_fusion.1), channel_id=1, source_target_pairs={{0,3},{1,0},{2,1},{3,2},{4,7},{5,4},{6,5},{7,6},{8,11},{9,8},{10,9... | collective-permute-start | bytes 69128 | tf_op jit(solution)/shard_map/ppermute | solution.py:19
  556.1 26.2 %collective-permute-start.15 = (f32[12,32]{0,1:T(8,128)S(1)}, f32[12,32]{0,1:T(8,128)S(1)}, u32[]{:S(2)}, u32[]{:S(2)}) collective-permute-start(f32[12,32]{0,1:T(8,128)S(1)} %collective-permute-done.14), channel_id=1, source_target_pairs={{0,124},{4,0},{8,4},{12,8},{16,12},{20,16},{24,20},{28,24},{32,28}... | collective-permute-start | bytes 4616 | tf_op jit(solution)/shard_map/ppermute | solution.py:19
  560.2 60.7 %collective-permute-start.17 = (f32[12,480]{0,1:T(8,128)S(1)}, f32[12,480]{0,1:T(8,128)S(1)}, u32[]{:S(2)}, u32[]{:S(2)}) collective-permute-start(f32[12,480]{0,1:T(8,128)S(1)} %select_bitcast_fusion), channel_id=1, source_target_pairs={{0,124},{4,0},{8,4},{12,8},{16,12},{20,16},{24,20},{28,24},{32,28}... | collective-permute-start | bytes 69128 | tf_op jit(solution)/shard_map/ppermute | solution.py:19
  608.6 83.8 %collective-permute-start.4 = (f32[72,128]{0,1:T(8,128)S(1)}, f32[72,128]{0,1:T(8,128)S(1)}, u32[]{:S(2)}, u32[]{:S(2)}) collective-permute-start(f32[72,128]{0,1:T(8,128)S(1)} %select_bitcast_fusion.5), channel_id=1, source_target_pairs={{0,3},{1,0},{2,1},{3,2},{4,7},{5,4},{6,5},{7,6},{8,11},{9,8},{10,9... | collective-permute-start | bytes 110600 | tf_op jit(solution)/shard_map/ppermute | solution.py:19
  610.0 71.5 %collective-permute-start.5 = (f32[72,128]{0,1:T(8,128)S(1)}, f32[72,128]{0,1:T(8,128)S(1)}, u32[]{:S(2)}, u32[]{:S(2)}) collective-permute-start(f32[72,128]{0,1:T(8,128)S(1)} %select_bitcast_fusion.4), channel_id=1, source_target_pairs={{0,124},{4,0},{8,4},{12,8},{16,12},{20,16},{24,20},{28,24},{32,28}... | collective-permute-start | bytes 110600 | tf_op jit(solution)/shard_map/ppermute | solution.py:19
  764.7 24.0 %collective-permute-start.30 = (f32[64,4096]{1,0:T(8,128)}, f32[64,4096]{1,0:T(8,128)S(1)}, u32[]{:S(2)}, u32[]{:S(2)}) collective-permute-start(f32[64,4096]{1,0:T(8,128)} %get-tuple-element.386), channel_id=1, source_target_pairs={{0,4},{4,8},{8,12},{12,16},{16,20},{20,24},{24,28},{28,32},{32,36}... | collective-permute-start | bytes 3145736 | tf_op jit(solution)/shard_map/ppermute | solution.py:29
  765.2 27.0 %collective-permute-start.32 = (f32[64,4096]{1,0:T(8,128)}, f32[64,4096]{1,0:T(8,128)S(1)}, u32[]{:S(2)}, u32[]{:S(2)}) collective-permute-start(f32[64,4096]{1,0:T(8,128)} %get-tuple-element.387), channel_id=1, source_target_pairs={{0,1},{1,2},{2,3},{3,0},{4,5},{5,6},{6,7},{7,4},{8,9},{9,10},{10,1... | collective-permute-start | bytes 3145736 | tf_op jit(solution)/shard_map/ppermute | solution.py:29
  765.9 26.2 %collective-permute-start.31 = (f32[64,4096]{1,0:T(8,128)}, f32[64,4096]{1,0:T(8,128)S(1)}, u32[]{:S(2)}, u32[]{:S(2)}) collective-permute-start(f32[64,4096]{1,0:T(8,128)} %get-tuple-element.388), channel_id=1, source_target_pairs={{4,0},{8,4},{12,8},{16,12},{20,16},{24,20},{28,24},{32,28},{36,32}... | collective-permute-start | bytes 3145736 | tf_op jit(solution)/shard_map/ppermute | solution.py:30
  770.2 22.3 %collective-permute-start.33 = (f32[64,4096]{1,0:T(8,128)}, f32[64,4096]{1,0:T(8,128)}, u32[]{:S(2)}, u32[]{:S(2)}) collective-permute-start(f32[64,4096]{1,0:T(8,128)} %get-tuple-element.389), channel_id=1, source_target_pairs={{1,0},{2,1},{3,2},{0,3},{5,4},{6,5},{7,6},{4,7},{9,8},{10,9},{11,1... | collective-permute-start | bytes 3145736 | tf_op jit(solution)/shard_map/ppermute | solution.py:30
  (86 other events, 3246.7 us)
where the time goes:
time: 834 us; the launch traced here: 821 us
  local copies, waits for them, and re-layouts  535 us (64%)
  other arithmetic  206 us (25%)
  starting transfers between devices  40 us (5%)
  matrix products  28.7 us (3%)
  waiting for transfers between devices  8.74 us (1%)
    scatter x8, local copies, waits for them, and re-layouts, pack_index(): jnp.full((capacity,), hosted, jnp.int32).at[slots]  144 us
    scatter x8, local copies, waits for them, and re-layouts, pack_columns(): jnp.zeros((values.shape[0], capacity), jnp.float32).at[:, slots]  103 us
    scatter-add x11, other arithmetic, add_rows(): return totals.at[:, row_index].add(values, mode='drop')  94.6 us
    gather x11, local copies, waits for them, and re-layouts, read_rows(): return jnp.take(totals, jnp.clip(row_index, 0, totals.shape[1] - 1), axis=1)  54.8 us
    gather x3, local copies, waits for them, and re-layouts, on_device(): jnp.take(back_dom[kind_index], jnp.clip(dom_slots[kind_index], 0, dom_cap...  45.8 us
    gather x3, local copies, waits for them, and re-layouts, on_device(): jnp.take(back_sub[kind_index], jnp.clip(sub_slots[kind_index], 0, sub_cap...  45.8 us
    gather x2, local copies, waits for them, and re-layouts, on_device(): jnp.take(back_dom[2 + kind_index], jnp.clip(both_slots[kind_index], 0, bo...  34.9 us
    ppermute x30, starting transfers between devices, from_behind(): return lax.ppermute(value, axis, pairs)  32 us
  transfers between devices with their start and end apart: 34, of which 5 were waited for; matrix products, arithmetic and copies ran while one was open for 79% of the time, Pallas kernels for 0%

commit v1 on v0

v1 whole, which is shorter than its diff:
```python
import functools

import jax
import jax.numpy as jnp
import numpy as np
from jax import lax
from jax.experimental import pallas as pl
from jax.experimental.pallas import tpu as pltpu
from jax.sharding import PartitionSpec as P

N = 8
E = 512
NODES = N * N * N
EX = 4
EY = 4
EZ = 32
MOVE = 64
RELAX = 0.6
F_BLOCK, E_BLOCK, C_BLOCK = 3 * E, 3 * E, E
F_KEYS, E_KEYS, C_KEYS = 1792, 2560, 1536
E_HI, C_HI = E_KEYS // 256, C_KEYS // 256
MSG = 224
BOTH = 24
INTERPRET = False

f32, bf16, i32 = jnp.float32, jnp.bfloat16, jnp.int32


def derivative_table(order):
    count = order + 1
    points = -np.cos(np.pi * np.arange(count) / order)
    legendre = np.zeros((count, count))
    for sweep in range(80):
        legendre[:, 0] = 1.0
        legendre[:, 1] = points
        for degree in range(2, count):
            legendre[:, degree] = (
                (2 * degree - 1) * points * legendre[:, degree - 1]
                - (degree - 1) * legendre[:, degree - 2]
            ) / degree
        points = points - (points * legendre[:, order] - legendre[:, order - 1]) / (
            count * legendre[:, order]
        )
    legendre[:, 0] = 1.0
    legendre[:, 1] = points
    for degree in range(2, count):
        legendre[:, degree] = (
            (2 * degree - 1) * points * legendre[:, degree - 1]
            - (degree - 1) * legendre[:, degree - 2]
        ) / degree
    values = legendre[:, order]
    identity = np.eye(count)
    spread = points[:, None] - points[None, :] + identity
    table = values[:, None] / values[None, :] / spread
    table = table * (1.0 - identity)
    table[0, 0] = -order * count / 4.0
    table[order, order] = order * count / 4.0
    return table.astype(np.float32)


TABLE = derivative_table(N - 1)
SQUARED = TABLE * TABLE
ALONG = [float(v) for v in np.diagonal(TABLE)]


def row_of(i, j, k):
    return (i * N + j) * N + k


EDGE_ROWS = (
    [(row_of(0, a, b), N * N) for a in (0, 7) for b in (0, 7)]
    + [(row_of(a, 0, b), N) for a in (0, 7) for b in (0, 7)]
    + [(row_of(a, b, 0), 1) for a in (0, 7) for b in (0, 7)]
)
CORNER_ROWS = [row_of(a, b, c) for a in (0, 7) for b in (0, 7) for c in (0, 7)]


def split3(x):
    hi = x.astype(bf16)
    rest = x - hi.astype(f32)
    mid = rest.astype(bf16)
    low = (rest - mid.astype(f32)).astype(bf16)
    return hi, mid, low


def stack3(x):
    return jnp.concatenate(split3(x), axis=0)


def sum3(x):
    m = x.shape[0] // 3
    return x[0:m] + x[m : 2 * m] + x[2 * m : 3 * m]


def dot_nn(a, b):
    return lax.dot_general(a, b, (((1,), (0,)), ((), ())), preferred_element_type=f32)


def dot_nt(a, b):
    return lax.dot_general(a, b, (((1,), (1,)), ((), ())), preferred_element_type=f32)


def small_row(key, count):
    ok = (key >= 0) & (key < count)
    return jnp.where(ok, key, -1).astype(f32).astype(bf16)


def iota_rows(count, lanes):
    return lax.broadcasted_iota(i32, (count, lanes), 0).astype(f32).astype(bf16)


def onehot(row, count):
    lanes = row.shape[1]
    io = iota_rows(count, 128)
    one, zero = jnp.ones((count, 128), bf16), jnp.zeros((count, 128), bf16)
    cols = [
        jnp.where(io == jnp.broadcast_to(row[:, g : g + 128], (count, 128)), one, zero)
        for g in range(0, lanes, 128)
    ]
    return cols[0] if len(cols) == 1 else jnp.concatenate(cols, axis=1)


def prefix_matrix():
    a = lax.broadcasted_iota(i32, (E, E), 0)
    b = lax.broadcasted_iota(i32, (E, E), 1)
    return jnp.where(a <= b, 1.0, 0.0).astype(bf16)


def ranks(mask, tri):
    m = mask.shape[0]
    flags = jnp.where(mask, 1.0, 0.0)
    within = dot_nn(flags.astype(bf16), tri) - 1.0
    if m > 1:
        before = jnp.zeros((1, 1), f32)
        offs = [before]
        for r in range(m - 1):
            before = before + jnp.sum(flags[r : r + 1], axis=1, keepdims=True)
            offs.append(before)
        within = within + jnp.concatenate(offs, axis=0)
    return within.astype(i32)


def move_rows(owner, devs, tri):
    own = devs[0]
    departed = owner != own
    leave = jnp.full((1, E), -1, i32)
    arrive = jnp.full((1, E), -1, i32)
    flags = [departed] + [departed & (owner == devs[d]) for d in range(1, 5)]
    stacked = jnp.concatenate([jnp.where(f, 1.0, 0.0) for f in flags] + [jnp.zeros((3, E), f32)], axis=0)
    pre = dot_nn(stacked.astype(bf16), tri)
    hole = pre[0:1] - 1.0
    start = jnp.zeros((1, 1), f32)
    for d in range(4):
        chosen = flags[d + 1]
        rank = pre[d + 1 : d + 2] - 1.0
        leave = jnp.where(chosen, d * MOVE + rank.astype(i32), leave)
        count = pre[d + 1 : d + 2, E - 1 : E]
        pos = hole - start
        inside = departed & (pos >= 0.0) & (pos < count)
        arrive = jnp.where(inside, d * MOVE + pos.astype(i32), arrive)
        start = start + count
    return departed, leave, arrive


def swapped(col):
    return jnp.where(col >= 0, col ^ MOVE, -1)


def lane_low(rows):
    return lax.broadcasted_iota(i32, (rows, 128), 1) < MOVE


def pack_block(x, pa, pb):
    half = NODES // 2
    ya = sum3(dot_nt(stack3(x[0:half]), pa))
    yb = sum3(dot_nt(stack3(x[half:]), pb))
    low = lane_low(half)
    out = []
    for g in (0, 128):
        a, b = ya[:, g : g + 128], yb[:, g : g + 128]
        out.append(jnp.where(low, a, b))
        out.append(jnp.where(low, b, a))
    return out


def land_block(x, got, pa, pb, departed):
    half = NODES // 2
    low = lane_low(half)
    zl, zh = [], []
    for g in (0, 2):
        zl.append(jnp.where(low, got[g + 1], got[g]))
        zh.append(jnp.where(low, got[g], got[g + 1]))
    zl = jnp.concatenate(zl, axis=1)
    zh = jnp.concatenate(zh, axis=1)
    yl = sum3(dot_nn(stack3(zl), pb))
    yh = sum3(dot_nn(stack3(zh), pa))
    keep = jnp.logical_not(departed)
    return jnp.where(keep, x[0:half], yl), jnp.where(keep, x[half:], yh)


def pack_kernel(devs, owner_ref, met_ref, o0, o1, o2, o3, pa, pb):
    @pl.when(pl.program_id(0) == 0)
    def _():
        _, leave, _ = move_rows(owner_ref[...], [devs[d] for d in range(5)], prefix_matrix())
        pa[...] = onehot(small_row(leave, 256), 256)
        pb[...] = onehot(small_row(swapped(leave), 256), 256)

    out = pack_block(met_ref[0].reshape(NODES, E), pa[...], pb[...])
    for ref, val in zip((o0, o1, o2, o3), out):
        ref[...] = val


def pack_metric(devs, owner, metric):
    half = NODES // 2
    return pl.pallas_call(
        pack_kernel,
        grid=(7,),
        in_specs=[
            pl.BlockSpec(memory_space=pltpu.SMEM),
            pl.BlockSpec((1, E), lambda m: (0, 0)),
            pl.BlockSpec((1, N, N, N, E), lambda m: (m, 0, 0, 0, 0)),
        ],
        out_specs=[pl.BlockSpec((half, 128), lambda m: (m, 0))] * 4,
        out_shape=[jax.ShapeDtypeStruct((7 * half, 128), f32)] * 4,
        scratch_shapes=[pltpu.VMEM((256, E), bf16)] * 2,
        interpret=INTERPRET,
        name="pack",
    )(devs, owner, metric)


def contract_i(src, table, put):
    for j in range(N):
        xs = [src(i, j) for i in range(N)]
        for a in range(N):
            put(a, j, sum(float(table[a, i]) * xs[i] for i in range(N) if table[a, i] != 0.0))


def contract_j(src, table, put):
    for i in range(N):
        xs = [src(i, j) for j in range(N)]
        for b in range(N):
            put(i, b, sum(float(table[b, j]) * xs[j] for j in range(N) if table[b, j] != 0.0))


def key_rows(ids, block, devs, dom_base, both_base, sub_base, tri):
    rel, inside = [], []
    for d in (0, 2, 4, 5):
        r = ids - devs[d] * block
        rel.append(r)
        inside.append((r >= 0) & (r < block))
    key = jnp.where(inside[0], rel[0], -1)
    key = jnp.where(inside[1], dom_base + ranks(inside[1], tri), key)
    key = jnp.where(inside[2], sub_base + ranks(inside[2], tri), key)
    if both_base is not None:
        key = jnp.where(inside[3], both_base + ranks(inside[3], tri), key)
    row = jnp.where(inside[0], rel[0], jnp.where(inside[1], rel[1], jnp.where(inside[2], rel[2], rel[3])))
    return key, row.astype(f32)


def tile(ref, r):
    return ref[pl.ds(r * N, N), :]


def apply_kernel(
    devs, ids, sol, met, kmat, im_out, dg_out, key_out, tf, te, tc, md, ms,
    vf, ve, vc, rix, ga, gb, gc, of, le, ol, acc_e,
):
    c = pl.program_id(0)

    @pl.when(c == 0)
    def _():
        tri = prefix_matrix()
        dv = [devs[d] for d in range(6)]
        k, r = key_rows(ids[0:6], F_BLOCK, dv, 1536, None, 1664, tri)
        key_out[0:6, :] = k
        rix[0:6, :] = r
        k, r = key_rows(ids[6:18], E_BLOCK, dv, 1536, 2016, 2048, tri)
        key_out[6:18, :] = k
        rix[6:18, :] = r
        k, r = key_rows(ids[18:26], C_BLOCK, dv, 512, 960, 1024, tri)
        key_out[18:26, :] = k
        rix[18:26, :] = r

    im, dg = im_out.at[0], dg_out.at[0]
    fwd, bwd = kmat.at[0], kmat.at[1]
    half = NODES // 2

    def kdot(m, x):
        return lax.dot_general(
            m, x, (((1,), (0,)), ((), ())),
            precision=lax.Precision.HIGHEST, preferred_element_type=f32,
        )

    def put_a(i, j, v):
        ga[pl.ds((i * N + j) * N, N), :] = v

    def put_b(i, j, v):
        gb[pl.ds((i * N + j) * N, N), :] = v

    contract_i(lambda i, j: sol[i, j], TABLE, put_a)
    contract_j(lambda i, j: sol[i, j], TABLE, put_b)
    for h in range(2):
        x = sol[h * 4 : h * 4 + 4].reshape(half, 128)
        gc[h * half : (h + 1) * half, :] = kdot(fwd[...], x)

    for i in range(N):
        for j in range(N):
            r = i * N + j
            a, b, t = tile(ga, r), tile(gb, r), tile(gc, r)
            m3, m4, m5 = met[3, i, j], met[4, i, j], met[5, i, j]
            ga[pl.ds(r * N, N), :] = met[0, i, j] * a + m3 * b + m4 * t
            gb[pl.ds(r * N, N), :] = m3 * a + met[1, i, j] * b + m5 * t
            gc[pl.ds(r * N, N), :] = m4 * a + m5 * b + met[2, i, j] * t

    for h in range(2):
        im[h * half : (h + 1) * half, :] = kdot(bwd[...], gc[h * half : (h + 1) * half, :])

    def add_im(i, j, v):
        im[pl.ds((i * N + j) * N, N), :] += v

    contract_i(lambda i, j: tile(ga, i * N + j), TABLE.T, add_im)

    def add_im_last(i, j, v):
        im[pl.ds((i * N + j) * N, N), :] += v + met[6, i, j] * sol[i, j]

    contract_j(lambda i, j: tile(gb, i * N + j), TABLE.T, add_im_last)

    sq = kmat.at[2]
    for h in range(2):
        x = met[2, h * 4 : h * 4 + 4].reshape(half, 128)
        dg[h * half : (h + 1) * half, :] = kdot(sq[...], x)

    def add_dg(i, j, v):
        dg[pl.ds((i * N + j) * N, N), :] += v

    contract_i(lambda i, j: met[0, i, j], SQUARED.T, add_dg)
    kk = lax.broadcasted_iota(i32, (N, 128), 0)
    dk = jnp.where(kk == 0, ALONG[0], jnp.where(kk == N - 1, ALONG[N - 1], 0.0))

    def add_dg_last(i, j, v):
        v = v + met[6, i, j]
        if ALONG[i] * ALONG[j] != 0.0:
            v = v + (2.0 * ALONG[i] * ALONG[j]) * met[3, i, j]
        if ALONG[i] != 0.0:
            v = v + (2.0 * ALONG[i]) * dk * met[4, i, j]
        if ALONG[j] != 0.0:
            v = v + (2.0 * ALONG[j]) * dk * met[5, i, j]
        dg[pl.ds((i * N + j) * N, N), :] += v

    contract_j(lambda i, j: met[1, i, j], SQUARED.T, add_dg_last)

    lanes = pl.ds(pl.multiple_of(c * 128, 128), 128)

    def face(ref, f):
        if f < 2:
            base = 0 if f == 0 else 448
            return ref[base : base + 64, :]
        if f < 4:
            j = 0 if f == 2 else 7
            return jnp.concatenate([ref[pl.ds((i * N + j) * N, N), :] for i in range(N)], axis=0)
        return ref[pl.ds(0 if f == 4 else 7, 64, stride=N), :]

    top = lax.broadcasted_iota(i32, (N, 128), 0) == 0
    for f in range(6):
        at = pl.ds(pl.multiple_of(f * E + c * 128, 128), 128)
        a, b = face(im, f), face(dg, f)
        mark = jnp.broadcast_to(rix[f : f + 1, lanes], (N, 128))
        a = jnp.concatenate([jnp.where(top, mark, a[0:N]), a[N:]], axis=0)
        for s, (p, q) in enumerate(zip(split3(a), split3(b))):
            vf[s * 128 : s * 128 + 64, at] = p
            vf[s * 128 + 64 : s * 128 + 128, at] = q
    for e in range(12):
        at = pl.ds(pl.multiple_of(e * E + c * 128, 128), 128)
        start, stride = EDGE_ROWS[e]
        rows = pl.ds(start, N) if stride == 1 else pl.ds(start, N, stride=stride)
        a, b = im[rows, :], dg[rows, :]
        mark = jnp.broadcast_to(rix[6 + e : 7 + e, lanes], (N, 128))
        x = jnp.concatenate([jnp.where(top, mark, a), b], axis=0)
        for s, p in enumerate(split3(x)):
            ve[s * 16 : s * 16 + 16, at] = p
    for q in range(8):
        at = pl.ds(pl.multiple_of(q * E + c * 128, 128), 128)
        r = CORNER_ROWS[q]
        vc[0:1, at] = im[r : r + 1, :]
        vc[1:2, at] = dg[r : r + 1, :]
        vc[2:3, at] = rix[18 + q : 19 + q, lanes]
        vc[3:8, at] = jnp.zeros((5, 128), f32)

    @pl.when(c == 3)
    def _():
        def face_block(n, carry):
            for f in range(6):
                of[:, f * E : (f + 1) * E] = onehot(small_row(key_out[f : f + 1, :] - n * 256, 256), 256)
            acc = dot_nt(vf[...], of[...])
            tf[:, pl.ds(pl.multiple_of(n * 256, 256), 256)] = sum3(acc)
            return carry

        lax.fori_loop(0, F_KEYS // 256, face_block, 0)

        for e in range(12):
            at = slice(e * E, (e + 1) * E)
            key = key_out[6 + e : 7 + e, :]
            hi = small_row(key >> 8, E_HI)
            ol[:, at] = onehot(small_row(key & 255, 256), 256)
            for g in range(4):
                ag = slice(e * E + g * 128, e * E + (g + 1) * 128)
                hb = jnp.broadcast_to(hi[:, g * 128 : (g + 1) * 128], (16, 128))
                zero = jnp.zeros((16, 128), bf16)
                parts = [ve[s * 16 : s * 16 + 16, ag] for s in range(3)]
                for h in range(E_HI):
                    m = hb == jnp.full((16, 128), float(h), bf16)
                    for s in range(3):
                        le[(s * E_HI + h) * 16 : (s * E_HI + h + 1) * 16, ag] = jnp.where(m, parts[s], zero)
        acc_e[...] = dot_nt(le[...], ol[...])
        for h in range(E_HI):
            te[h] = sum(acc_e[(s * E_HI + h) * 16 : (s * E_HI + h + 1) * 16, :] for s in range(3))

        full = E * 8
        for q in range(8):
            at = slice(q * E, (q + 1) * E)
            ol[:, at] = onehot(small_row(key_out[18 + q : 19 + q, :] & 255, 256), 256)
        hi = jnp.concatenate([key_out[18 + q : 19 + q, :] >> 8 for q in range(8)], axis=1)
        x = vc[...]
        big = jnp.concatenate(
            [jnp.where(jnp.broadcast_to(hi, (8, full)) == h, x, 0.0) for h in range(C_HI)], axis=0
        )
        acc = sum3(dot_nt(stack3(big), ol[:, 0:full]))
        for h in range(C_HI):
            tc[h] = acc[h * 8 : (h + 1) * 8]

        md[0:128, :] = tf[:, 1536:1664]
        ms[0:128, :] = tf[:, 1664:1792]
        for g in range(4):
            er, cr = msg_rows(g)
            half_lanes = slice((g % 2) * 128, (g % 2) * 128 + 128)
            md[er : er + 16, :] = te[6 + g // 2, :, half_lanes]
            ms[er : er + 16, :] = te[8 + g // 2, :, half_lanes]
            md[cr : cr + 8, :] = tc[2 + g // 2, :, half_lanes]
            ms[cr : cr + 8, :] = tc[4 + g // 2, :, half_lanes]


def msg_rows(g):
    if g < 3:
        return 128 + 16 * g, 176 + 8 * g
    return 200, 216


def apply_scatter(devs, ids, solution, metric):
    eye = np.eye(NODES // 2 // N, dtype=np.float32)
    kmat = np.stack([np.kron(eye, TABLE), np.kron(eye, TABLE.T), np.kron(eye, SQUARED.T)])
    chunk = lambda c: (c, 0, 0)
    whole2 = lambda c: (0, 0)
    whole3 = lambda c: (0, 0, 0)
    return pl.pallas_call(
        apply_kernel,
        grid=(4,),
        in_specs=[
            pl.BlockSpec(memory_space=pltpu.SMEM),
            pl.BlockSpec((26, E), whole2),
            pl.BlockSpec((N, N, N, 128), lambda c: (0, 0, 0, c)),
            pl.BlockSpec((7, N, N, N, 128), lambda c: (0, 0, 0, 0, c)),
            pl.BlockSpec((3, 256, 256), whole3),
        ],
        out_specs=[
            pl.BlockSpec((1, NODES, 128), chunk),
            pl.BlockSpec((1, NODES, 128), chunk),
            pl.BlockSpec((26, E), whole2),
            pl.BlockSpec((128, F_KEYS), whole2),
            pl.BlockSpec((E_HI, 16, 256), whole3),
            pl.BlockSpec((C_HI, 8, 256), whole3),
            pl.BlockSpec((MSG, 128), whole2),
            pl.BlockSpec((MSG, 128), whole2),
        ],
        out_shape=[
            jax.ShapeDtypeStruct((4, NODES, 128), f32),
            jax.ShapeDtypeStruct((4, NODES, 128), f32),
            jax.ShapeDtypeStruct((26, E), i32),
            jax.ShapeDtypeStruct((128, F_KEYS), f32),
            jax.ShapeDtypeStruct((E_HI, 16, 256), f32),
            jax.ShapeDtypeStruct((C_HI, 8, 256), f32),
            jax.ShapeDtypeStruct((MSG, 128), f32),
            jax.ShapeDtypeStruct((MSG, 128), f32),
        ],
        scratch_shapes=[
            pltpu.VMEM((384, 6 * E), bf16),
            pltpu.VMEM((48, 12 * E), bf16),
            pltpu.VMEM((8, 8 * E), f32),
            pltpu.VMEM((26, E), f32),
            pltpu.VMEM((NODES, 128), f32),
            pltpu.VMEM((NODES, 128), f32),
            pltpu.VMEM((NODES, 128), f32),
            pltpu.VMEM((256, 6 * E), bf16),
            pltpu.VMEM((3 * E_HI * 16, 12 * E), bf16),
            pltpu.VMEM((256, 12 * E), bf16),
            pltpu.VMEM((3 * E_HI * 16, 256), f32),
        ],
        compiler_params=pltpu.CompilerParams(vmem_limit_bytes=56 << 20),
        interpret=INTERPRET,
        name="apply",
    )(devs, ids, solution, metric, kmat)


def owner_kernel(tf, te, tc, gd, gs, gboth, tf2, te2, tc2, rd, rs, rb):
    vals = jnp.concatenate([gd[0:128, :], gs[0:128, :]], axis=1)
    key = vals[0:1, :].astype(i32)
    vs = stack3(vals)
    ret = jnp.zeros((384, 256), f32)
    for n in range(F_BLOCK // 256):
        o = onehot(small_row(key - n * 256, 256), 256)
        total = tf[:, n * 256 : (n + 1) * 256] + sum3(dot_nt(vs, o))
        tf2[:, n * 256 : (n + 1) * 256] = total
        ret = ret + dot_nn(stack3(total), o)
    ret = sum3(ret)
    rd[0:128, :] = ret[:, 0:128]
    rs[0:128, :] = ret[:, 128:256]

    lane = lax.broadcasted_iota(i32, (1, 128), 1)

    def lines(rows, id_row, total_ref, total_out, his, cut, at):
        vals, keys = [], []
        for src in (gd, gs):
            for g in range(4):
                r = msg_rows(g)[at]
                v = src[r : r + rows, :]
                k = v[id_row : id_row + 1].astype(i32)
                if src is gd and g == 3:
                    k = jnp.where(lane >= cut, -1, k)
                vals.append(v)
                keys.append(k)
        r = msg_rows(3)[at] - (MSG - BOTH)
        v = gboth[r : r + rows, :]
        keys.append(jnp.where(lane < cut, -1, v[id_row : id_row + 1].astype(i32)))
        vals.append(v)
        x = jnp.concatenate(vals, axis=1)
        key = jnp.concatenate(keys, axis=1)
        hi = key >> 8
        o = onehot(small_row(key & 255, 256), 256)
        big = jnp.concatenate([jnp.where(jnp.broadcast_to(hi, x.shape) == h, x, 0.0) for h in range(his)], axis=0)
        acc = sum3(dot_nt(stack3(big), o))
        totals = jnp.concatenate([total_ref[h] for h in range(his)], axis=0) + acc
        for h in range(his):
            total_out[h] = totals[h * rows : (h + 1) * rows]
        y = sum3(dot_nn(stack3(totals), o))
        back = jnp.zeros_like(x)
        for h in range(his):
            back = jnp.where(jnp.broadcast_to(hi, x.shape) == h, y[h * rows : (h + 1) * rows], back)
        for n, dst in enumerate((rd, rs)):
            for g in range(4):
                p = msg_rows(g)[at]
                dst[p : p + rows, :] = back[:, (n * 4 + g) * 128 : (n * 4 + g + 1) * 128]
        rb[r : r + rows, :] = back[:, 1024:1152]

    lines(16, 0, te, te2, E_BLOCK // 256, 96, 0)
    lines(8, 2, tc, tc2, C_BLOCK // 256, 64, 1)


def owner_sums(tf, te, tc, got_dom, got_sub, got_both):
    return pl.pallas_call(
        owner_kernel,
        out_shape=[
            jax.ShapeDtypeStruct((128, F_BLOCK), f32),
            jax.ShapeDtypeStruct((E_BLOCK // 256, 16, 256), f32),
            jax.ShapeDtypeStruct((C_BLOCK // 256, 8, 256), f32),
            jax.ShapeDtypeStruct((MSG, 128), f32),
            jax.ShapeDtypeStruct((MSG, 128), f32),
            jax.ShapeDtypeStruct((BOTH, 128), f32),
        ],
        interpret=INTERPRET,
        name="owner",
    )(tf, te, tc, got_dom, got_sub, got_both)


def relax_kernel(
    devs, owner, keys, tf, te, tc, rd, rs, rb, im_in, dg_in, sol, forc,
    out, o0, o1, o2, o3, im, dg, tfs, of, gf, ge, gc, rel,
):
    im[...] = im_in[...]
    dg[...] = dg_in[...]
    for s, p in enumerate(split3(tf[...])):
        tfs[s * 128 : (s + 1) * 128, 0:1536] = p
    for s, p in enumerate(split3(rd[0:128, :])):
        tfs[s * 128 : (s + 1) * 128, 1536:1664] = p
    for s, p in enumerate(split3(rs[0:128, :])):
        tfs[s * 128 : (s + 1) * 128, 1664:1792] = p

    def face_gather(f, carry):
        key = keys[pl.ds(f, 1), :]
        for n in range(F_KEYS // 256):
            of[n * 256 : (n + 1) * 256, :] = onehot(small_row(key - n * 256, 256), 256)
        gf[f] = sum3(dot_nn(tfs[...], of[...]))
        return carry

    lax.fori_loop(0, 6, face_gather, 0)

    lane = lax.broadcasted_iota(i32, (1, 128), 1)

    def table(own, his, rows, at, cut):
        blocks = [own[h] for h in range(his)]
        for src in (rd, rs):
            for g in (0, 2):
                pair = []
                for q in (g, g + 1):
                    r = msg_rows(q)[at]
                    v = src[r : r + rows, :]
                    if src is rd and q == 3:
                        b = r - (MSG - BOTH)
                        v = jnp.where(jnp.broadcast_to(lane, (rows, 128)) >= cut, rb[b : b + rows, :], v)
                    pair.append(v)
                blocks.append(jnp.concatenate(pair, axis=1))
        return stack3(jnp.concatenate(blocks, axis=0))

    def line_gather(tab, first, count, his, rows, dst):
        def one(q, carry):
            key = keys[pl.ds(first + q, 1), :]
            hi = key >> 8
            y = sum3(dot_nn(tab, onehot(small_row(key & 255, 256), 256)))
            back = jnp.zeros((rows, E), f32)
            for h in range(his):
                back = jnp.where(jnp.broadcast_to(hi, (rows, E)) == h, y[h * rows : (h + 1) * rows], back)
            dst[q] = back
            return carry

        lax.fori_loop(0, count, one, 0)

    line_gather(table(te, 6, 16, 0, 96), 6, 12, E_HI, 16, ge)
    line_gather(table(tc, 2, 8, 1, 64), 18, 8, C_HI, 8, gc)

    for c in range(4):
        at = slice(c * 128, (c + 1) * 128)
        for ref, base in ((im.at[c], 0), (dg.at[c], 1)):
            for f in range(6):
                v = gf[f, base * 64 : base * 64 + 64, at]
                if f < 2:
                    start = 0 if f == 0 else 448
                    ref[start : start + 64, :] = v
                elif f < 4:
                    j = 0 if f == 2 else 7
                    for i in range(N):
                        ref[pl.ds((i * N + j) * N, N), :] = v[i * N : (i + 1) * N]
                else:
                    ref[pl.ds(0 if f == 4 else 7, 64, stride=N), :] = v
            for e in range(12):
                start, stride = EDGE_ROWS[e]
                rows = pl.ds(start, N) if stride == 1 else pl.ds(start, N, stride=stride)
                ref[rows, :] = ge[e, base * 8 : base * 8 + 8, at]
            for q in range(8):
                r = CORNER_ROWS[q]
                ref[r : r + 1, :] = gc[q, base : base + 1, at]
        s = sol[:, :, :, at].reshape(NODES, 128)
        v = s + RELAX * (forc[:, :, :, at].reshape(NODES, 128) - im[c]) / dg[c]
        rel[:, at] = v
    out[...] = rel[...].reshape(N, N, N, E)
    _, leave, _ = move_rows(owner[...], [devs[d] for d in range(5)], prefix_matrix())
    pa = onehot(small_row(leave, 256), 256)
    pb = onehot(small_row(swapped(leave), 256), 256)
    for ref, val in zip((o0, o1, o2, o3), pack_block(rel[...], pa, pb)):
        ref[...] = val


def gather_relax(devs, owner, keys, tf, te, tc, rd, rs, rb, im, dg, solution, forcing):
    half = NODES // 2
    vm = pl.BlockSpec(memory_space=pltpu.VMEM)
    return pl.pallas_call(
        relax_kernel,
        in_specs=[pl.BlockSpec(memory_space=pltpu.SMEM)] + [vm] * 12,
        out_shape=[jax.ShapeDtypeStruct((N, N, N, E), f32)] + [jax.ShapeDtypeStruct((half, 128), f32)] * 4,
        scratch_shapes=[
            pltpu.VMEM((4, NODES, 128), f32),
            pltpu.VMEM((4, NODES, 128), f32),
            pltpu.VMEM((384, F_KEYS), bf16),
            pltpu.VMEM((F_KEYS, E), bf16),
            pltpu.VMEM((6, 128, E), f32),
            pltpu.VMEM((12, 16, E), f32),
            pltpu.VMEM((8, 8, E), f32),
            pltpu.VMEM((NODES, E), f32),
        ],
        compiler_params=pltpu.CompilerParams(vmem_limit_bytes=48 << 20),
        interpret=INTERPRET,
        name="relax",
    )(devs, owner, keys, tf, te, tc, rd, rs, rb, im, dg, solution, forcing)


def land_kernel(devs, owner_ref, x_ref, a0, a1, a2, a3, out, pa, pb, dep):
    @pl.when(pl.program_id(0) == 0)
    def _():
        departed, _, arrive = move_rows(owner_ref[...], [devs[d] for d in range(5)], prefix_matrix())
        pa[...] = onehot(small_row(arrive, 256), 256)
        pb[...] = onehot(small_row(swapped(arrive), 256), 256)
        dep[...] = jnp.broadcast_to(jnp.where(departed, 1.0, 0.0), (8, E))

    departed = dep[0:1, :] > 0.5
    got = [a[...] for a in (a0, a1, a2, a3)]
    shape = x_ref.shape
    lo, hi = land_block(x_ref[...].reshape(NODES, E), got, pa[...], pb[...], departed)
    half = shape[:-4] + (N // 2, N, N, E)
    if len(shape) == 5:
        out[0, 0:4] = lo.reshape(half[1:])
        out[0, 4:8] = hi.reshape(half[1:])
    else:
        out[0:4] = lo.reshape(half)
        out[4:8] = hi.reshape(half)


def land(devs, owner, x, got, name):
    half = NODES // 2
    parts = x.shape[0] if x.ndim == 5 else 1
    if x.ndim == 5:
        spec = pl.BlockSpec((1, N, N, N, E), lambda m: (m, 0, 0, 0, 0))
    else:
        spec = pl.BlockSpec((N, N, N, E), lambda m: (0, 0, 0, 0))
    return pl.pallas_call(
        land_kernel,
        grid=(parts,),
        in_specs=[
            pl.BlockSpec(memory_space=pltpu.SMEM),
            pl.BlockSpec((1, E), lambda m: (0, 0)),
            spec,
        ]
        + [pl.BlockSpec((half, 128), lambda m: (m, 0))] * 4,
        out_specs=spec,
        out_shape=jax.ShapeDtypeStruct(x.shape, f32),
        scratch_shapes=[pltpu.VMEM((256, E), bf16)] * 2 + [pltpu.VMEM((8, E), f32)],
        interpret=INTERPRET,
        name=name,
    )(devs, owner, x, *got)


def shift(value, axis, steps):
    count = lax.axis_size(axis)
    return lax.ppermute(value, axis, [(s, (s + steps) % count) for s in range(count)])


def shift_both(value, steps):
    a, b = lax.axis_size("dom"), lax.axis_size("sub")
    pairs = [(d * b + s, (d + steps) % a * b + (s + steps) % b) for d in range(a) for s in range(b)]
    return lax.ppermute(value, ("dom", "sub"), pairs)


def exchange(sent):
    return [
        shift(sent[1], "dom", 1),
        shift(sent[0], "dom", -1),
        shift(sent[3], "sub", 1),
        shift(sent[2], "sub", -1),
    ]


def on_device(solution, forcing, metric, entity_ids, new_owner):
    a, b = lax.axis_size("dom"), lax.axis_size("sub")
    d, s = lax.axis_index("dom"), lax.axis_index("sub")
    da, db = (d + 1) % a, (d + a - 1) % a
    sa, sb = (s + 1) % b, (s + b - 1) % b
    devs = jnp.stack([d * b + s, db * b + s, da * b + s, d * b + sb, d * b + sa, da * b + sa]).astype(i32)
    owner = new_owner.reshape(1, E)

    sent = pack_metric(devs, owner, metric)
    im, dg, keys, tf, te, tc, md, ms = apply_scatter(devs, entity_ids, solution, metric)
    gd = shift(md, "dom", 1)
    gs = shift(ms, "sub", 1)
    gb = shift_both(md[MSG - BOTH :], 1)
    tf, te, tc, rd, rs, rb = owner_sums(tf, te, tc, gd, gs, gb)
    rd = shift(rd, "dom", -1)
    rs = shift(rs, "sub", -1)
    rb = shift_both(rb, -1)
    relaxed, *moved = gather_relax(
        devs, owner, keys, tf, te, tc, rd, rs, rb, im, dg, solution, forcing
    )
    moved_metric = land(devs, owner, metric, exchange(sent), "land_metric")
    smoothed = land(devs, owner, relaxed, exchange(moved), "land_field")
    return smoothed, moved_metric


def solution(mesh):
    cols = ("dom", "sub")
    placed = (
        P(None, None, None, cols),
        P(None, None, None, cols),
        P(None, None, None, None, cols),
        P(None, cols),
        P(cols),
    )
    return jax.shard_map(
        on_device,
        mesh=mesh,
        in_specs=placed,
        out_specs=(P(None, None, None, cols), P(None, None, None, None, cols)),
        check_vma=False,
    )
```

time: 834 us -> 127 us (0.15); the launches traced: 821 us -> 127 us
  local copies, waits for them, and re-layouts: 535 us -> 6.31 us
  other arithmetic: 206 us -> 0 us
  Pallas kernels: 0 us -> 61.7 us
  matrix products: 28.7 us -> 0 us
  waiting for transfers between devices: 8.74 us -> 36.9 us
  starting transfers between devices: 40 us -> 20.9 us
    scatter x44 -> x0, local copies, waits for them, and re-layouts: 273 us -> none  [the longest x8 144 us: pack_index(): jnp.full((capacity,), hosted, jnp.int32).at[slots]]
    gather x23 -> x0, local copies, waits for them, and re-layouts: 194 us -> none  [the longest x11 54.8 us: read_rows(): return jnp.take(totals, jnp.clip(row_index, 0, totals.shape[1] - 1), axis=1)]
    scatter-add x11 -> x0, other arithmetic: 94.6 us -> none  [add_rows(): return totals.at[:, row_index].add(values, mode='drop')]
    pallas_call x0 -> x6, Pallas kernels: none -> 61.7 us  [the longest x1 20.7 us: apply_scatter(): pl.pallas_call(apply_kernel, grid=(4,), in_specs=[pl.BlockSpec(memory_spa...]
    select_n x32 -> x0, other arithmetic: 53.7 us -> none  [the longest x2 19.5 us: on_device(): merged = jnp.where((owner_dev == next_both)[None, :], from_both, merged)]
    dot_general x9 -> x0, matrix products: 28.7 us -> none  [the longest x1 7.11 us: element_apply(): image = jnp.einsum('ai,ajke->ijke', derivative, flux_r, precision=highest)]
    ppermute x34 -> x14, waiting for transfers between devices: 8.74 us -> 36.9 us  [the longest x12 33.6 us: shift(): lax.ppermute(value, axis, [(s, (s + steps) % count) for s in range(count)])]
    slice x8 -> x1, local copies, waits for them, and re-layouts: 25.5 us -> 0.71 us  [on_device(): gb = shift_both(md[MSG - BOTH:], 1)]
  transfers between devices with their start and end apart: 34 -> 14, of which waited for: 5 -> 8; matrix products, arithmetic and copies ran while one was open for 79% -> 1% of each run, Pallas kernels for 0% -> 23%
where the time goes in v1:
time: 127 us
  Pallas kernels  61.7 us (49%)
  waiting for transfers between devices  36.9 us (29%)
  starting transfers between devices  20.9 us (16%)
  local copies, waits for them, and re-layouts  6.31 us (5%)
    ppermute x12, waiting for transfers between devices, shift(): lax.ppermute(value, axis, [(s, (s + steps) % count) for s in range(count)])  33.6 us
    pallas_call x1, Pallas kernels, apply_scatter(): pl.pallas_call(apply_kernel, grid=(4,), in_specs=[pl.BlockSpec(memory_spa...  20.7 us
    ppermute x12, starting transfers between devices, shift(): lax.ppermute(value, axis, [(s, (s + steps) % count) for s in range(count)])  19.7 us
    pallas_call x2, Pallas kernels, land(): pl.pallas_call(land_kernel, grid=(parts,), in_specs=[pl.BlockSpec(memory_...  14.8 us
    pallas_call x1, Pallas kernels, gather_relax(): pl.pallas_call(relax_kernel, in_specs=[pl.BlockSpec(memory_space=pltpu.SM...  13.3 us
    pallas_call x1, Pallas kernels, pack_metric(): pl.pallas_call(pack_kernel, grid=(7,), in_specs=[pl.BlockSpec(memory_spac...  9.18 us
    unnamed x34, local copies, waits for them, and re-layouts  5.03 us
    pallas_call x1, Pallas kernels, owner_sums(): pl.pallas_call(owner_kernel, out_shape=[jax.ShapeDtypeStruct((128, F_BLOC...  3.75 us
  transfers between devices with their start and end apart: 14, of which 8 were waited for; matrix products, arithmetic and copies ran while one was open for 1% of the time, Pallas kernels for 23%

profile of v1, /device:TPU:0, one launch (start us, length us, event | category | flops | bytes accessed | tf_op | source)
XLA Modules:
  0.0 126.7 jit_solution(14149422041072271405)
XLA Ops:
  0.7 0.6 stack.27.devs
  1.3 20.7 %apply.1 = (f32[4,512,128]{2,1,0:T(8,128)}, f32[4,512,128]{2,1,0:T(8,128)}, s32[26,512]{1,0:T(8,128)}, f32[128,1792]{1,0:T(8,128)}, f32[10,16,256]{2,1,0:T(8,128...) custom-call(s32[6]{0:T(128)} %stack.27.devs, s32[26,512]{1,0:T(8,128)} %ids.1, ...), custom_call_target="tpu_custom_call" | custom-call | tf_op jit(solution)/shard_map/apply/pallas_call | solution.py:454
  22.0 2.1 %collective-permute-start.1 = (f32[224,128]{1,0:T(8,128)}, f32[224,128]{1,0:T(8,128)S(1)}, u32[]{:S(2)}, u32[]{:S(2)}) collective-permute-start(f32[224,128]{1,0:T(8,128)} %get-tuple-element.30), channel_id=1, source_target_pairs={{0,1},{1,2},{2,3},{3,0},{4,5},{5,6},{6,7},{7,4},{8,9},{9,10},{10,1... | collective-permute-start | bytes 344072 | tf_op jit(solution)/shard_map/ppermute | solution.py:730
  24.1 0.7 slice.3
  24.8 1.1 collective-permute-start.2
  25.9 9.2 %pack.1 = (f32[1792,128]{1,0:T(8,128)}, f32[1792,128]{1,0:T(8,128)}, f32[1792,128]{1,0:T(8,128)}, f32[1792,128]{1,0:T(8,128)}) custom-call(s32[6]{0:T(128)} %stack.27.devs, s32[1,512]{1,0:T(1,128)} %bitcast.7, f32[7,8,8,8,512]{4,3,2,1,0:T(8,128)} %x_ref.1), custom_call_target="tpu_custom_call" | custom-call | tf_op jit(solution)/shard_map/pack/pallas_call | solution.py:215
  35.1 1.9 %collective-permute-start.10 = (f32[1792,128]{1,0:T(8,128)}, f32[1792,128]{1,0:T(8,128)}, u32[]{:S(2)}, u32[]{:S(2)}) collective-permute-start(f32[1792,128]{1,0:T(8,128)} %get-tuple-element.44), channel_id=1, source_target_pairs={{0,4},{4,8},{8,12},{12,16},{16,20},{20,24},{24,28},{28,32},{32,36}... | collective-permute-start | bytes 2752520 | tf_op jit(solution)/shard_map/ppermute | solution.py:730
  36.9 3.5 %collective-permute-start.11 = (f32[1792,128]{1,0:T(8,128)}, f32[1792,128]{1,0:T(8,128)}, u32[]{:S(2)}, u32[]{:S(2)}) collective-permute-start(f32[1792,128]{1,0:T(8,128)} %get-tuple-element.45), channel_id=1, source_target_pairs={{0,124},{4,0},{8,4},{12,8},{16,12},{20,16},{24,20},{28,24},{32,28}... | collective-permute-start | bytes 2752520 | tf_op jit(solution)/shard_map/ppermute | solution.py:730
  40.5 1.6 %collective-permute-start.12 = (f32[1792,128]{1,0:T(8,128)}, f32[1792,128]{1,0:T(8,128)}, u32[]{:S(2)}, u32[]{:S(2)}) collective-permute-start(f32[1792,128]{1,0:T(8,128)} %get-tuple-element.46), channel_id=1, source_target_pairs={{0,1},{1,2},{2,3},{3,0},{4,5},{5,6},{6,7},{7,4},{8,9},{9,10},{10,1... | collective-permute-start | bytes 2752520 | tf_op jit(solution)/shard_map/ppermute | solution.py:730
  42.1 1.6 %collective-permute-start.13 = (f32[1792,128]{1,0:T(8,128)}, f32[1792,128]{1,0:T(8,128)}, u32[]{:S(2)}, u32[]{:S(2)}) collective-permute-start(f32[1792,128]{1,0:T(8,128)} %get-tuple-element.47), channel_id=1, source_target_pairs={{0,3},{1,0},{2,1},{3,2},{4,7},{5,4},{6,5},{7,6},{8,11},{9,8},{10,9... | collective-permute-start | bytes 2752520 | tf_op jit(solution)/shard_map/ppermute | solution.py:730
  43.7 9.2 %collective-permute-done.gd = f32[224,128]{1,0:T(8,128)S(1)} collective-permute-done((f32[224,128]{1,0:T(8,128)}, f32[224,128]{1,0:T(8,128)S(1)}, u32[]{:S(2)}, u32[]{:S(2)}) %collective-permute-start) | collective-permute-done | bytes 114720 | tf_op jit(solution)/shard_map/ppermute | solution.py:730
  52.9 0.6 copy-done.15
  53.6 3.7 %owner.1 = (f32[128,1536]{1,0:T(8,128)}, f32[6,16,256]{2,1,0:T(8,128)}, f32[2,8,256]{2,1,0:T(8,128)}, f32[224,128]{1,0:T(8,128)}, f32[224,128]{1,0:T(8,128)}, /*index=5*/f32[24,128]{1,0:T(8,128)}) custom-call(f32[128,1792]{1,0:T(8,128)} %get-tuple-element.26.tf, f32[10,16,256]{2,1,0:T(8,128)} %get-tuple-element.27.te, f32[6,8,256]{2,1,0:T(8,128)} %get-tuple-element.28.tc, ...), custom_call_target="tpu_custom_call" | custom-call | tf_op jit(solution)/shard_map/owner/pallas_call | solution.py:558
  57.4 3.3 %collective-permute-done.5.rb = f32[24,128]{1,0:T(8,128)S(1)} collective-permute-done((f32[24,128]{1,0:T(8,128)}, f32[24,128]{1,0:T(8,128)S(1)}, u32[]{:S(2)}, u32[]{:S(2)}) %collective-permute-start.5) | collective-permute-done | bytes 12320 | tf_op jit(solution)/shard_map/ppermute | solution.py:736
  60.8 4.2 %collective-permute-start.3 = (f32[224,128]{1,0:T(8,128)}, f32[224,128]{1,0:T(8,128)S(1)}, u32[]{:S(2)}, u32[]{:S(2)}) collective-permute-start(f32[224,128]{1,0:T(8,128)} %get-tuple-element.34), channel_id=1, source_target_pairs={{0,124},{4,0},{8,4},{12,8},{16,12},{20,16},{24,20},{28,24},{32,28}... | collective-permute-start | bytes 344072 | tf_op jit(solution)/shard_map/ppermute | solution.py:730
  65.0 2.7 %collective-permute-done.3.rd = f32[224,128]{1,0:T(8,128)S(1)} collective-permute-done((f32[224,128]{1,0:T(8,128)}, f32[224,128]{1,0:T(8,128)S(1)}, u32[]{:S(2)}, u32[]{:S(2)}) %collective-permute-start.3) | collective-permute-done | bytes 114720 | tf_op jit(solution)/shard_map/ppermute | solution.py:730
  67.7 1.8 %collective-permute-start.4 = (f32[224,128]{1,0:T(8,128)}, f32[224,128]{1,0:T(8,128)S(1)}, u32[]{:S(2)}, u32[]{:S(2)}) collective-permute-start(f32[224,128]{1,0:T(8,128)} %get-tuple-element.35), channel_id=1, source_target_pairs={{0,3},{1,0},{2,1},{3,2},{4,7},{5,4},{6,5},{7,6},{8,11},{9,8},{10,9... | collective-permute-start | bytes 344072 | tf_op jit(solution)/shard_map/ppermute | solution.py:730
  69.5 3.2 %collective-permute-done.4.rs = f32[224,128]{1,0:T(8,128)S(1)} collective-permute-done((f32[224,128]{1,0:T(8,128)}, f32[224,128]{1,0:T(8,128)S(1)}, u32[]{:S(2)}, u32[]{:S(2)}) %collective-permute-start.4) | collective-permute-done | bytes 114720 | tf_op jit(solution)/shard_map/ppermute | solution.py:730
  72.7 1.1 copy-done.4
  73.9 0.9 copy-done.5
  74.8 0.7 copy-done.9
  75.5 13.3 %relax.1 = (f32[8,8,8,512]{3,2,1,0:T(8,128)S(1)}, f32[256,128]{1,0:T(8,128)S(1)}, f32[256,128]{1,0:T(8,128)S(1)}, f32[256,128]{1,0:T(8,128)S(1)}, f32[256,128]{1,0:T(8,128)S(1)}) custom-call(s32[6]{0:T(128)S(1)} %copy-done.8, s32[1,512]{1,0:T(1,128)S(1)} %bitcast.10, s32[26,512]{1,0:T(8,128)S(1)} %copy-done.6, f32[128,1536]{1,0:T(8,128)S(1)} %copy-done.4, ...), custom_call_target="tpu_custom_call" | custom-call | tf_op jit(solution)/shard_map/relax/pallas_call | solution.py:663
  88.8 1.0 copy-done.1
  89.8 7.7 %collective-permute-done.6.a0 = f32[256,128]{1,0:T(8,128)S(1)} collective-permute-done((f32[256,128]{1,0:T(8,128)S(1)}, f32[256,128]{1,0:T(8,128)S(1)}, u32[]{:S(2)}, u32[]{:S(2)}) %collective-permute-start.6) | collective-permute-done | bytes 131104 | tf_op jit(solution)/shard_map/ppermute | solution.py:730
  97.5 2.5 %collective-permute-done.7.a1 = f32[256,128]{1,0:T(8,128)S(1)} collective-permute-done((f32[256,128]{1,0:T(8,128)S(1)}, f32[256,128]{1,0:T(8,128)S(1)}, u32[]{:S(2)}, u32[]{:S(2)}) %collective-permute-start.7) | collective-permute-done | bytes 131104 | tf_op jit(solution)/shard_map/ppermute | solution.py:730
  100.0 0.9 collective-permute-start.8
  100.9 5.3 %collective-permute-done.8.a2 = f32[256,128]{1,0:T(8,128)S(1)} collective-permute-done((f32[256,128]{1,0:T(8,128)S(1)}, f32[256,128]{1,0:T(8,128)S(1)}, u32[]{:S(2)}, u32[]{:S(2)}) %collective-permute-start.8) | collective-permute-done | bytes 131104 | tf_op jit(solution)/shard_map/ppermute | solution.py:730
  106.2 1.9 %collective-permute-start.9 = (f32[256,128]{1,0:T(8,128)S(1)}, f32[256,128]{1,0:T(8,128)S(1)}, u32[]{:S(2)}, u32[]{:S(2)}) collective-permute-start(f32[256,128]{1,0:T(8,128)S(1)} %get-tuple-element.43), channel_id=1, source_target_pairs={{0,3},{1,0},{2,1},{3,2},{4,7},{5,4},{6,5},{7,6},{8,11},{9,8},{10,9... | collective-permute-start | bytes 393224 | tf_op jit(solution)/shard_map/ppermute | solution.py:730
  108.1 3.0 %collective-permute-done.9.a3 = f32[256,128]{1,0:T(8,128)S(1)} collective-permute-done((f32[256,128]{1,0:T(8,128)S(1)}, f32[256,128]{1,0:T(8,128)S(1)}, u32[]{:S(2)}, u32[]{:S(2)}) %collective-permute-start.9) | collective-permute-done | bytes 131104 | tf_op jit(solution)/shard_map/ppermute | solution.py:730
  111.2 0.7 copy-done.13
  111.8 3.2 %land_field.1 = f32[8,8,8,512]{3,2,1,0:T(8,128)} custom-call(s32[6]{0:T(128)} %stack.27.devs, s32[1,512]{1,0:T(1,128)} %bitcast.8, f32[8,8,8,512]{3,2,1,0:T(8,128)} %copy-done.1, f32[256,128]{1,0:T(8,128)} %copy-done.10, f32[256,128]{1,0:T(8,128)} %copy-done.11, f32[256,128]{1,0:T(8,128)} %copy-done.12, f32[256,128]{1,0:T(8,128)} %copy-done.13), custom_call_target="tpu_custom_call" | custom-call | tf_op jit(solution)/shard_map/land_field/pallas_call | solution.py:711
  115.1 11.6 %land_metric.1 = f32[7,8,8,8,512]{4,3,2,1,0:T(8,128)} custom-call(s32[6]{0:T(128)} %stack.27.devs, s32[1,512]{1,0:T(1,128)} %bitcast.9, f32[7,8,8,8,512]{4,3,2,1,0:T(8,128)} %x_ref.1, f32[1792,128]{1,0:T(8,128)} %collective-permute-done.10.a0, f32[1792,128]{1,0:T(8,128)} %collective-permute-done.11.a1, f32[1792,128]{1,0:T(8,128)} %collective-permute-done.12.a2, ...), custom_call_target="tpu_custom_call" | custom-call | tf_op jit(solution)/shard_map/land_metric/pallas_call | solution.py:711
  (38 shorter events, 0.2 us)
Async XLA Ops:
  1.2 71.5 %copy-start = (f32[8,8,8,512]{3,2,1,0:T(8,128)S(1)}, f32[8,8,8,512]{3,2,1,0:T(8,128)}, u32[]{:S(2)}) copy-start(f32[8,8,8,512]{3,2,1,0:T(8,128)} %sol.3) | copy-start | bytes 3145732
  1.2 71.5 %copy-start.7 = (s32[512]{0:T(512)S(1)}, s32[512]{0:T(512)}, u32[]{:S(2)}) copy-start(s32[512]{0:T(512)} %param.10) | copy-start | bytes 6148
  1.3 71.5 %copy-start.8 = (s32[6]{0:T(128)S(1)}, s32[6]{0:T(128)}, u32[]{:S(2)}) copy-start(s32[6]{0:T(128)} %stack.27.devs) | copy-start | bytes 76
  22.0 50.7 %copy-start.2 = (f32[4,512,128]{2,1,0:T(8,128)S(1)}, f32[4,512,128]{2,1,0:T(8,128)}, u32[]{:S(2)}) copy-start(f32[4,512,128]{2,1,0:T(8,128)} %get-tuple-element.37.im_in) | copy-start | bytes 3145732
  22.0 50.7 %copy-start.3 = (f32[4,512,128]{2,1,0:T(8,128)S(1)}, f32[4,512,128]{2,1,0:T(8,128)}, u32[]{:S(2)}) copy-start(f32[4,512,128]{2,1,0:T(8,128)} %get-tuple-element.38.dg_in) | copy-start | bytes 3145732
  22.0 50.7 %copy-start.6 = (s32[26,512]{1,0:T(8,128)S(1)}, s32[26,512]{1,0:T(8,128)}, u32[]{:S(2)}) copy-start(s32[26,512]{1,0:T(8,128)} %get-tuple-element.25.keys) | copy-start | bytes 159748
  22.0 21.7 %collective-permute-start.1 = (f32[224,128]{1,0:T(8,128)}, f32[224,128]{1,0:T(8,128)S(1)}, u32[]{:S(2)}, u32[]{:S(2)}) collective-permute-start(f32[224,128]{1,0:T(8,128)} %get-tuple-element.30), channel_id=1, source_target_pairs={{0,1},{1,2},{2,3},{3,0},{4,5},{5,6},{6,7},{7,4},{8,9},{9,10},{10,1... | collective-permute-start | bytes 344072 | tf_op jit(solution)/shard_map/ppermute | solution.py:730
  24.8 17.3 %collective-permute-start.2 = (f32[24,128]{1,0:T(8,128)S(1)}, f32[24,128]{1,0:T(8,128)S(1)}, u32[]{:S(2)}, u32[]{:S(2)}) collective-permute-start(f32[24,128]{1,0:T(8,128)S(1)} %slice.3), channel_id=1, source_target_pairs={{0,5},{1,6},{2,7},{3,4},{4,9},{5,10},{6,11},{7,8},{8,13},{9,14},{1... | collective-permute-start | bytes 36872 | tf_op jit(solution)/shard_map/ppermute | solution.py:736
  35.1 80.0 %collective-permute-start.10 = (f32[1792,128]{1,0:T(8,128)}, f32[1792,128]{1,0:T(8,128)}, u32[]{:S(2)}, u32[]{:S(2)}) collective-permute-start(f32[1792,128]{1,0:T(8,128)} %get-tuple-element.44), channel_id=1, source_target_pairs={{0,4},{4,8},{8,12},{12,16},{16,20},{20,24},{24,28},{28,32},{32,36}... | collective-permute-start | bytes 2752520 | tf_op jit(solution)/shard_map/ppermute | solution.py:730
  36.9 78.1 %collective-permute-start.11 = (f32[1792,128]{1,0:T(8,128)}, f32[1792,128]{1,0:T(8,128)}, u32[]{:S(2)}, u32[]{:S(2)}) collective-permute-start(f32[1792,128]{1,0:T(8,128)} %get-tuple-element.45), channel_id=1, source_target_pairs={{0,124},{4,0},{8,4},{12,8},{16,12},{20,16},{24,20},{28,24},{32,28}... | collective-permute-start | bytes 2752520 | tf_op jit(solution)/shard_map/ppermute | solution.py:730
  40.5 74.6 %collective-permute-start.12 = (f32[1792,128]{1,0:T(8,128)}, f32[1792,128]{1,0:T(8,128)}, u32[]{:S(2)}, u32[]{:S(2)}) collective-permute-start(f32[1792,128]{1,0:T(8,128)} %get-tuple-element.46), channel_id=1, source_target_pairs={{0,1},{1,2},{2,3},{3,0},{4,5},{5,6},{6,7},{7,4},{8,9},{9,10},{10,1... | collective-permute-start | bytes 2752520 | tf_op jit(solution)/shard_map/ppermute | solution.py:730
  42.1 10.8 %copy-start.16 = (f32[24,128]{1,0:T(8,128)}, f32[24,128]{1,0:T(8,128)S(1)}, u32[]{:S(2)}) copy-start(f32[24,128]{1,0:T(8,128)S(1)} %collective-permute-done.2.gboth) | copy-start | bytes 36868
  42.1 73.0 %collective-permute-start.13 = (f32[1792,128]{1,0:T(8,128)}, f32[1792,128]{1,0:T(8,128)}, u32[]{:S(2)}, u32[]{:S(2)}) collective-permute-start(f32[1792,128]{1,0:T(8,128)} %get-tuple-element.47), channel_id=1, source_target_pairs={{0,3},{1,0},{2,1},{3,2},{4,7},{5,4},{6,5},{7,6},{8,11},{9,8},{10,9... | collective-permute-start | bytes 2752520 | tf_op jit(solution)/shard_map/ppermute | solution.py:730
  43.7 9.2 %copy-start.14 = (f32[224,128]{1,0:T(8,128)}, f32[224,128]{1,0:T(8,128)S(1)}, u32[]{:S(2)}) copy-start(f32[224,128]{1,0:T(8,128)S(1)} %collective-permute-done.1.gs) | copy-start | bytes 344068
  43.7 9.2 %collective-permute-start = (f32[224,128]{1,0:T(8,128)}, f32[224,128]{1,0:T(8,128)S(1)}, u32[]{:S(2)}, u32[]{:S(2)}) collective-permute-start(f32[224,128]{1,0:T(8,128)} %get-tuple-element.29), channel_id=1, source_target_pairs={{0,4},{4,8},{8,12},{12,16},{16,20},{20,24},{24,28},{28,32},{32,36}... | collective-permute-start | bytes 344072 | tf_op jit(solution)/shard_map/ppermute | solution.py:730
  52.9 0.6 copy-start.15
  57.3 3.5 %collective-permute-start.5 = (f32[24,128]{1,0:T(8,128)}, f32[24,128]{1,0:T(8,128)S(1)}, u32[]{:S(2)}, u32[]{:S(2)}) collective-permute-start(f32[24,128]{1,0:T(8,128)} %get-tuple-element.36), channel_id=1, source_target_pairs={{0,127},{1,124},{2,125},{3,126},{4,3},{5,0},{6,1},{7,2},{8,7},{9,4... | collective-permute-start | bytes 36872 | tf_op jit(solution)/shard_map/ppermute | solution.py:736
  60.8 6.9 %collective-permute-start.3 = (f32[224,128]{1,0:T(8,128)}, f32[224,128]{1,0:T(8,128)S(1)}, u32[]{:S(2)}, u32[]{:S(2)}) collective-permute-start(f32[224,128]{1,0:T(8,128)} %get-tuple-element.34), channel_id=1, source_target_pairs={{0,124},{4,0},{8,4},{12,8},{16,12},{20,16},{24,20},{28,24},{32,28}... | collective-permute-start | bytes 344072 | tf_op jit(solution)/shard_map/ppermute | solution.py:730
  67.7 5.0 %collective-permute-start.4 = (f32[224,128]{1,0:T(8,128)}, f32[224,128]{1,0:T(8,128)S(1)}, u32[]{:S(2)}, u32[]{:S(2)}) collective-permute-start(f32[224,128]{1,0:T(8,128)} %get-tuple-element.35), channel_id=1, source_target_pairs={{0,3},{1,0},{2,1},{3,2},{4,7},{5,4},{6,5},{7,6},{8,11},{9,8},{10,9... | collective-permute-start | bytes 344072 | tf_op jit(solution)/shard_map/ppermute | solution.py:730
  72.7 1.1 copy-start.4
  73.9 0.9 copy-start.5
  74.8 0.7 copy-start.9
  88.8 1.0 copy-start.1
  89.8 7.7 %collective-permute-start.6 = (f32[256,128]{1,0:T(8,128)S(1)}, f32[256,128]{1,0:T(8,128)S(1)}, u32[]{:S(2)}, u32[]{:S(2)}) collective-permute-start(f32[256,128]{1,0:T(8,128)S(1)} %get-tuple-element.40), channel_id=1, source_target_pairs={{0,4},{4,8},{8,12},{12,16},{16,20},{20,24},{24,28},{28,32},{32,36}... | collective-permute-start | bytes 393224 | tf_op jit(solution)/shard_map/ppermute | solution.py:730
  97.5 13.7 %copy-start.10 = (f32[256,128]{1,0:T(8,128)}, f32[256,128]{1,0:T(8,128)S(1)}, u32[]{:S(2)}) copy-start(f32[256,128]{1,0:T(8,128)S(1)} %collective-permute-done.6.a0) | copy-start | bytes 393220
  97.5 2.5 %collective-permute-start.7 = (f32[256,128]{1,0:T(8,128)S(1)}, f32[256,128]{1,0:T(8,128)S(1)}, u32[]{:S(2)}, u32[]{:S(2)}) collective-permute-start(f32[256,128]{1,0:T(8,128)S(1)} %get-tuple-element.41), channel_id=1, source_target_pairs={{0,124},{4,0},{8,4},{12,8},{16,12},{20,16},{24,20},{28,24},{32,28}... | collective-permute-start | bytes 393224 | tf_op jit(solution)/shard_map/ppermute | solution.py:730
  100.0 11.2 %copy-start.11 = (f32[256,128]{1,0:T(8,128)}, f32[256,128]{1,0:T(8,128)S(1)}, u32[]{:S(2)}) copy-start(f32[256,128]{1,0:T(8,128)S(1)} %collective-permute-done.7.a1) | copy-start | bytes 393220
  100.0 6.2 %collective-permute-start.8 = (f32[256,128]{1,0:T(8,128)S(1)}, f32[256,128]{1,0:T(8,128)S(1)}, u32[]{:S(2)}, u32[]{:S(2)}) collective-permute-start(f32[256,128]{1,0:T(8,128)S(1)} %get-tuple-element.42), channel_id=1, source_target_pairs={{0,1},{1,2},{2,3},{3,0},{4,5},{5,6},{6,7},{7,4},{8,9},{9,10},{10,1... | collective-permute-start | bytes 393224 | tf_op jit(solution)/shard_map/ppermute | solution.py:730
  106.2 5.0 %copy-start.12 = (f32[256,128]{1,0:T(8,128)}, f32[256,128]{1,0:T(8,128)S(1)}, u32[]{:S(2)}) copy-start(f32[256,128]{1,0:T(8,128)S(1)} %collective-permute-done.8.a2) | copy-start | bytes 393220
  106.2 5.0 %collective-permute-start.9 = (f32[256,128]{1,0:T(8,128)S(1)}, f32[256,128]{1,0:T(8,128)S(1)}, u32[]{:S(2)}, u32[]{:S(2)}) collective-permute-start(f32[256,128]{1,0:T(8,128)S(1)} %get-tuple-element.43), channel_id=1, source_target_pairs={{0,3},{1,0},{2,1},{3,2},{4,7},{5,4},{6,5},{7,6},{8,11},{9,8},{10,9... | collective-permute-start | bytes 393224 | tf_op jit(solution)/shard_map/ppermute | solution.py:730
  111.2 0.7 copy-start.13

commit v2 on v1

--- a/solution.py
+++ b/solution.py
@@ -500,7 +500,7 @@
     )(devs, ids, solution, metric, kmat)
 
 
-def owner_kernel(tf, te, tc, gd, gs, gboth, tf2, te2, tc2, rd, rs, rb):
+def owner_sums(tf, te, tc, gd, gs, gboth, tf2, te2, tc2, rd, rs, rb):
     vals = jnp.concatenate([gd[0:128, :], gs[0:128, :]], axis=1)
     key = vals[0:1, :].astype(i32)
     vs = stack3(vals)
@@ -554,28 +554,7 @@
     lines(8, 2, tc, tc2, C_BLOCK // 256, 64, 1)
 
 
-def owner_sums(tf, te, tc, got_dom, got_sub, got_both):
-    return pl.pallas_call(
-        owner_kernel,
-        out_shape=[
-            jax.ShapeDtypeStruct((128, F_BLOCK), f32),
-            jax.ShapeDtypeStruct((E_BLOCK // 256, 16, 256), f32),
-            jax.ShapeDtypeStruct((C_BLOCK // 256, 8, 256), f32),
-            jax.ShapeDtypeStruct((MSG, 128), f32),
-            jax.ShapeDtypeStruct((MSG, 128), f32),
-            jax.ShapeDtypeStruct((BOTH, 128), f32),
-        ],
-        interpret=INTERPRET,
-        name="owner",
-    )(tf, te, tc, got_dom, got_sub, got_both)
-
-
-def relax_kernel(
-    devs, owner, keys, tf, te, tc, rd, rs, rb, im_in, dg_in, sol, forc,
-    out, o0, o1, o2, o3, im, dg, tfs, of, gf, ge, gc, rel,
-):
-    im[...] = im_in[...]
-    dg[...] = dg_in[...]
+def gather_shared(keys, tf, te, tc, rd, rs, rb, tfs, of, gf, ge, gc):
     for s, p in enumerate(split3(tf[...])):
         tfs[s * 128 : (s + 1) * 128, 0:1536] = p
     for s, p in enumerate(split3(rd[0:128, :])):
@@ -625,6 +604,7 @@
     line_gather(table(te, 6, 16, 0, 96), 6, 12, E_HI, 16, ge)
     line_gather(table(tc, 2, 8, 1, 64), 18, 8, C_HI, 8, gc)
 
+def place_relax(im, dg, gf, ge, gc, sol, forc, rel):
     for c in range(4):
         at = slice(c * 128, (c + 1) * 128)
         for ref, base in ((im.at[c], 0), (dg.at[c], 1)):
@@ -649,35 +629,118 @@
         s = sol[:, :, :, at].reshape(NODES, 128)
         v = s + RELAX * (forc[:, :, :, at].reshape(NODES, 128) - im[c]) / dg[c]
         rel[:, at] = v
-    out[...] = rel[...].reshape(N, N, N, E)
-    _, leave, _ = move_rows(owner[...], [devs[d] for d in range(5)], prefix_matrix())
+
+MESH = pl.DeviceIdType.MESH
+
+
+def exchange_kernel(
+    owner, keys, tf, te, tc, md, ms, im_in, dg_in, sol_in, forc_in,
+    out, a0, a1, a2, a3,
+    gd, gs, gb, tf2, te2, tc2, sd, ss, sb, rd, rs, rb,
+    im, dg, sol, forc, tfs, of, gf, ge, gc, rel, p0, p1, p2, p3,
+    local_sem, send_sem, recv_sem,
+):
+    na, nb = lax.axis_size("dom"), lax.axis_size("sub")
+    d, s = lax.axis_index("dom"), lax.axis_index("sub")
+    dn, dp = lax.rem(d + 1, na), lax.rem(d + na - 1, na)
+    sn, sp = lax.rem(s + 1, nb), lax.rem(s + nb - 1, nb)
+    prev_dom, next_dom, prev_sub, next_sub = (dp, s), (dn, s), (d, sp), (d, sn)
+    prev_both, next_both = (dp, sp), (dn, sn)
+    loads = [
+        pltpu.make_async_copy(src, dst, local_sem.at[n])
+        for n, (src, dst) in enumerate(((im_in, im), (dg_in, dg), (sol_in, sol), (forc_in, forc)))
+    ]
+    for copy in loads:
+        copy.start()
+
+    barrier = pltpu.get_barrier_semaphore()
+    for peer in (prev_dom, next_dom, prev_sub, next_sub, prev_both, next_both):
+        pl.semaphore_signal(barrier, inc=1, device_id=peer, device_id_type=MESH)
+    pl.semaphore_wait(barrier, 6)
+
+    def send(n, src, dst, peer):
+        copy = pltpu.make_async_remote_copy(
+            src_ref=src, dst_ref=dst, send_sem=send_sem.at[n], recv_sem=recv_sem.at[n],
+            device_id=peer, device_id_type=MESH,
+        )
+        copy.start()
+        return copy
+
+    first = [
+        send(0, ms, gs, next_sub),
+        send(1, md, gd, next_dom),
+        send(2, md.at[pl.ds(MSG - BOTH, BOTH)], gb, next_both),
+    ]
+    for copy in first:
+        copy.wait()
+    owner_sums(tf, te, tc, gd, gs, gb, tf2, te2, tc2, sd, ss, sb)
+    second = [
+        send(3, ss, rs, prev_sub),
+        send(4, sd, rd, prev_dom),
+        send(5, sb, rb, prev_both),
+    ]
+    for copy in second:
+        copy.wait()
+    gather_shared(keys, tf2, te2, tc2, rd, rs, rb, tfs, of, gf, ge, gc)
+    for copy in loads:
+        copy.wait()
+    place_relax(im, dg, gf, ge, gc, sol, forc, rel)
+    devs = [x * nb + y for x, y in ((d, s), prev_dom, next_dom, prev_sub, next_sub)]
+    _, leave, _ = move_rows(owner[...], devs, prefix_matrix())
     pa = onehot(small_row(leave, 256), 256)
     pb = onehot(small_row(swapped(leave), 256), 256)
-    for ref, val in zip((o0, o1, o2, o3), pack_block(rel[...], pa, pb)):
+    for ref, val in zip((p0, p1, p2, p3), pack_block(rel[...], pa, pb)):
         ref[...] = val
-
-
-def gather_relax(devs, owner, keys, tf, te, tc, rd, rs, rb, im, dg, solution, forcing):
+    third = [
+        send(6, p2, a3, prev_sub),
+        send(7, p3, a2, next_sub),
+        send(8, p0, a1, prev_dom),
+        send(9, p1, a0, next_dom),
+    ]
+    out[...] = rel[...].reshape(N, N, N, E)
+    for copy in third:
+        copy.wait()
+
+
+def exchange_relax(owner, keys, tf, te, tc, md, ms, im, dg, solution, forcing):
     half = NODES // 2
     vm = pl.BlockSpec(memory_space=pltpu.VMEM)
+    hbm = pl.BlockSpec(memory_space=pl.ANY)
+    msg, both = pltpu.VMEM((MSG, 128), f32), pltpu.VMEM((BOTH, 128), f32)
     return pl.pallas_call(
-        relax_kernel,
-        in_specs=[pl.BlockSpec(memory_space=pltpu.SMEM)] + [vm] * 12,
+        exchange_kernel,
+        in_specs=[vm] * 7 + [hbm] * 4,
         out_shape=[jax.ShapeDtypeStruct((N, N, N, E), f32)] + [jax.ShapeDtypeStruct((half, 128), f32)] * 4,
         scratch_shapes=[
+            msg, msg, both,
+            pltpu.VMEM((128, F_BLOCK), f32),
+            pltpu.VMEM((E_BLOCK // 256, 16, 256), f32),
+            pltpu.VMEM((C_BLOCK // 256, 8, 256), f32),
+            msg, msg, both, msg, msg, both,
             pltpu.VMEM((4, NODES, 128), f32),
             pltpu.VMEM((4, NODES, 128), f32),
+            pltpu.VMEM((N, N, N, E), f32),
+            pltpu.VMEM((N, N, N, E), f32),
             pltpu.VMEM((384, F_KEYS), bf16),
             pltpu.VMEM((F_KEYS, E), bf16),
             pltpu.VMEM((6, 128, E), f32),
             pltpu.VMEM((12, 16, E), f32),
             pltpu.VMEM((8, 8, E), f32),
             pltpu.VMEM((NODES, E), f32),
+            pltpu.VMEM((half, 128), f32),
+            pltpu.VMEM((half, 128), f32),
+            pltpu.VMEM((half, 128), f32),
+            pltpu.VMEM((half, 128), f32),
+            pltpu.SemaphoreType.DMA((4,)),
+            pltpu.SemaphoreType.DMA((10,)),
+            pltpu.SemaphoreType.DMA((10,)),
         ],
-        compiler_params=pltpu.CompilerParams(vmem_limit_bytes=48 << 20),
-        interpret=INTERPRET,
-        name="relax",
-    )(devs, owner, keys, tf, te, tc, rd, rs, rb, im, dg, solution, forcing)
+        compiler_params=pltpu.CompilerParams(
+            vmem_limit_bytes=48 << 20, collective_id=0, has_side_effects=True
+        ),
+        interpret=pltpu.InterpretParams() if INTERPRET else False,
+        name="exchange",
+    )(owner, keys, tf, te, tc, md, ms, im, dg, solution, forcing)
 
 
 def land_kernel(devs, owner_ref, x_ref, a0, a1, a2, a3, out, pa, pb, dep):
@@ -730,12 +793,6 @@
     return lax.ppermute(value, axis, [(s, (s + steps) % count) for s in range(count)])
 
 
-def shift_both(value, steps):
-    a, b = lax.axis_size("dom"), lax.axis_size("sub")
-    pairs = [(d * b + s, (d + steps) % a * b + (s + steps) % b) for d in range(a) for s in range(b)]
-    return lax.ppermute(value, ("dom", "sub"), pairs)
-
-
 def exchange(sent):
     return [
         shift(sent[1], "dom", 1),
@@ -754,19 +811,12 @@
     owner = new_owner.reshape(1, E)
 
     sent = pack_metric(devs, owner, metric)
-    im, dg, keys, tf, te, tc, md, ms = apply_scatter(devs, entity_ids, solution, metric)
-    gd = shift(md, "dom", 1)
-    gs = shift(ms, "sub", 1)
-    gb = shift_both(md[MSG - BOTH :], 1)
-    tf, te, tc, rd, rs, rb = owner_sums(tf, te, tc, gd, gs, gb)
-    rd = shift(rd, "dom", -1)
-    rs = shift(rs, "sub", -1)
-    rb = shift_both(rb, -1)
-    relaxed, *moved = gather_relax(
-        devs, owner, keys, tf, te, tc, rd, rs, rb, im, dg, solution, forcing
-    )
-    moved_metric = land(devs, owner, metric, exchange(sent), "land_metric")
-    smoothed = land(devs, owner, relaxed, exchange(moved), "land_field")
+    arrived = exchange(sent)
+    later, *sent = lax.optimization_barrier((devs, *sent))
+    im, dg, keys, tf, te, tc, md, ms = apply_scatter(later, entity_ids, solution, metric)
+    relaxed, *moved = exchange_relax(owner, keys, tf, te, tc, md, ms, im, dg, solution, forcing)
+    moved_metric = land(devs, owner, metric, arrived, "land_metric")
+    smoothed = land(devs, owner, relaxed, moved, "land_field")
     return smoothed, moved_metric
 
 

time: 127 us -> 104 us (0.82)
  waiting for transfers between devices: 36.9 us -> 0.01 us
  Pallas kernels: 61.7 us -> 80.6 us
  starting transfers between devices: 20.9 us -> 8.8 us
  local copies, waits for them, and re-layouts: 6.31 us -> 13.3 us
    ppermute x12 -> x4, waiting for transfers between devices: 33.6 us -> 0.01 us  [shift(): lax.ppermute(value, axis, [(s, (s + steps) % count) for s in range(count)])]
    pallas_call x2 -> x1, Pallas kernels: 17.1 us -> 36 us  [exchange_relax(): pl.pallas_call(exchange_kernel, in_specs=[vm] * 7 + [hbm] * 4, out_shape=...]
    ppermute x12 -> x4, starting transfers between devices: 19.7 us -> 8.8 us  [shift(): lax.ppermute(value, axis, [(s, (s + steps) % count) for s in range(count)])]
    unnamed x34, local copies, waits for them, and re-layouts: 5.03 us -> 12.7 us
    ppermute x2 -> x0, waiting for transfers between devices: 3.34 us -> none  [shift_both(): return lax.ppermute(value, ('dom', 'sub'), pairs)]
  transfers between devices with their start and end apart: 14 -> 4, of which waited for: 8 -> 0; matrix products, arithmetic and copies ran while one was open for 1% -> 0% of each run, Pallas kernels for 23% -> 58%
where the time goes in v2:
time: 104 us; the launch traced here: 103 us
  Pallas kernels  80.6 us (77%)
  local copies, waits for them, and re-layouts  13.3 us (13%)
  starting transfers between devices  8.8 us (8%)
    pallas_call x1, Pallas kernels, exchange_relax(): pl.pallas_call(exchange_kernel, in_specs=[vm] * 7 + [hbm] * 4, out_shape=...  36 us
    pallas_call x1, Pallas kernels, apply_scatter(): pl.pallas_call(apply_kernel, grid=(4,), in_specs=[pl.BlockSpec(memory_spa...  20.6 us
    pallas_call x2, Pallas kernels, land(): pl.pallas_call(land_kernel, grid=(parts,), in_specs=[pl.BlockSpec(memory_...  14.8 us
    unnamed x34, local copies, waits for them, and re-layouts  12.7 us
    pallas_call x1, Pallas kernels, pack_metric(): pl.pallas_call(pack_kernel, grid=(7,), in_specs=[pl.BlockSpec(memory_spac...  9.23 us
    ppermute x4, starting transfers between devices, shift(): lax.ppermute(value, axis, [(s, (s + steps) % count) for s in range(count)])  8.8 us
  transfers between devices with their start and end apart: 4, of which 0 were waited for; matrix products, arithmetic and copies ran while one was open for 0% of the time, Pallas kernels for 58%

profile of v2, /device:TPU:0, one launch (start us, length us, event | category | flops | bytes accessed | tf_op | source)
XLA Modules:
  0.0 103.5 jit_solution(18055319246367736940)
XLA Ops:
  0.7 0.6 stack.27.devs
  1.2 9.2 %pack.1 = (f32[1792,128]{1,0:T(8,128)}, f32[1792,128]{1,0:T(8,128)}, f32[1792,128]{1,0:T(8,128)}, f32[1792,128]{1,0:T(8,128)}) custom-call(s32[6]{0:T(128)} %stack.27.devs, s32[1,512]{1,0:T(1,128)} %bitcast.7, f32[7,8,8,8,512]{4,3,2,1,0:T(8,128)} %x_ref.1), custom_call_target="tpu_custom_call" | custom-call | tf_op jit(solution)/shard_map/pack/pallas_call | solution.py:215
  10.5 4.8 %collective-permute-start.1 = (f32[1792,128]{1,0:T(8,128)}, f32[1792,128]{1,0:T(8,128)S(1)}, u32[]{:S(2)}, u32[]{:S(2)}) collective-permute-start(f32[1792,128]{1,0:T(8,128)} %get-tuple-element.20), channel_id=1, source_target_pairs={{0,124},{4,0},{8,4},{12,8},{16,12},{20,16},{24,20},{28,24},{32,28}... | collective-permute-start | bytes 2752520 | tf_op jit(solution)/shard_map/ppermute | solution.py:793
  15.2 0.0 collective-permute-start
  15.2 4.0 %collective-permute-start.3 = (f32[1792,128]{1,0:T(8,128)}, f32[1792,128]{1,0:T(8,128)}, u32[]{:S(2)}, u32[]{:S(2)}) collective-permute-start(f32[1792,128]{1,0:T(8,128)} %get-tuple-element.22), channel_id=1, source_target_pairs={{0,3},{1,0},{2,1},{3,2},{4,7},{5,4},{6,5},{7,6},{8,11},{9,8},{10,9... | collective-permute-start | bytes 2752520 | tf_op jit(solution)/shard_map/ppermute | solution.py:793
  19.3 0.0 collective-permute-start.2
  19.3 20.6 %apply.1 = (f32[4,512,128]{2,1,0:T(8,128)}, f32[4,512,128]{2,1,0:T(8,128)}, s32[26,512]{1,0:T(8,128)}, f32[128,1792]{1,0:T(8,128)}, f32[10,16,256]{2,1,0:T(8,128...) custom-call(s32[6]{0:T(128)} %stack.27.devs, s32[26,512]{1,0:T(8,128)} %ids.1, ...), custom_call_target="tpu_custom_call" | custom-call | tf_op jit(solution)/shard_map/apply/pallas_call | solution.py:454
  39.9 0.0 copy-done
  39.9 0.0 copy-start.1
  39.9 1.2 %copy-done.1 = f32[4,512,128]{2,1,0:T(8,128)S(1)} copy-done((f32[4,512,128]{2,1,0:T(8,128)S(1)}, f32[4,512,128]{2,1,0:T(8,128)}, u32[]{:S(2)}) %copy-start.1) | copy-done | bytes 1048600
  41.2 1.2 %copy-done.2 = f32[4,512,128]{2,1,0:T(8,128)S(1)} copy-done((f32[4,512,128]{2,1,0:T(8,128)S(1)}, f32[4,512,128]{2,1,0:T(8,128)}, u32[]{:S(2)}) %copy-start.2) | copy-done | bytes 1048600
  42.4 1.2 %copy-done.4 = f32[128,1792]{1,0:T(8,128)S(1)} copy-done((f32[128,1792]{1,0:T(8,128)S(1)}, f32[128,1792]{1,0:T(8,128)}, u32[]{:S(2)}) %copy-start.4) | copy-done | bytes 917528
  43.6 0.9 copy-done.5
  44.5 0.9 copy-done.10
  45.4 0.9 copy-done.11
  46.3 0.8 copy-done.12
  47.1 0.8 copy-done.13
  47.9 36.0 %exchange.1 = (f32[8,8,8,512]{3,2,1,0:T(8,128)S(1)}, f32[256,128]{1,0:T(8,128)S(1)}, f32[256,128]{1,0:T(8,128)S(1)}, f32[256,128]{1,0:T(8,128)S(1)}, f32[256,128]{1,0:T(8,128)S(1)}) custom-call(s32[1,512]{1,0:T(1,128)S(1)} %bitcast.10, s32[26,512]{1,0:T(8,128)S(1)} %copy-done.12, f32[128,1792]{1,0:T(8,128)S(1)} %copy-done.4, f32[10,16,256]{2,1,0:T(8,128)S(1)} %copy-done.5, ...), custom_call_target="tpu_custom_call" | custom-call | tf_op jit(solution)/shard_map/exchange/pallas_call | solution.py:710
  83.9 0.0 copy-start.3
  83.9 1.0 copy-done.3
  84.9 0.7 copy-done.6
  85.5 0.7 copy-done.7
  86.2 0.6 copy-done.8
  86.8 0.6 copy-done.9
  87.5 3.2 %land_field.1 = f32[8,8,8,512]{3,2,1,0:T(8,128)} custom-call(s32[6]{0:T(128)} %stack.27.devs, s32[1,512]{1,0:T(1,128)} %bitcast.8, f32[8,8,8,512]{3,2,1,0:T(8,128)} %copy-done.3, f32[256,128]{1,0:T(8,128)} %copy-done.6, f32[256,128]{1,0:T(8,128)} %copy-done.7, f32[256,128]{1,0:T(8,128)} %copy-done.8, f32[256,128]{1,0:T(8,128)} %copy-done.9), custom_call_target="tpu_custom_call" | custom-call | tf_op jit(solution)/shard_map/land_field/pallas_call | solution.py:774
  90.7 0.0 collective-permute-done.1.a1
  90.7 0.0 collective-permute-done.a0
  90.7 0.0 collective-permute-done.3.a3
  90.7 0.0 collective-permute-done.2.a2
  90.7 0.9 copy-done.15
  91.7 0.3 copy-done.16
  91.9 11.5 %land_metric.1 = f32[7,8,8,8,512]{4,3,2,1,0:T(8,128)} custom-call(s32[6]{0:T(128)} %stack.27.devs, s32[1,512]{1,0:T(1,128)} %bitcast.9, f32[7,8,8,8,512]{4,3,2,1,0:T(8,128)} %x_ref.1, f32[1792,128]{1,0:T(8,128)} %copy-done.16, f32[1792,128]{1,0:T(8,128)} %copy-done.15, f32[1792,128]{1,0:T(8,128)} %collective-permute-done.2.a2, ...), custom_call_target="tpu_custom_call" | custom-call | tf_op jit(solution)/shard_map/land_metric/pallas_call | solution.py:774
  (16 shorter events, 0.0 us)
Async XLA Ops:
  1.2 38.7 %copy-start = (f32[8,8,8,512]{3,2,1,0:T(8,128)S(1)}, f32[8,8,8,512]{3,2,1,0:T(8,128)}, u32[]{:S(2)}) copy-start(f32[8,8,8,512]{3,2,1,0:T(8,128)} %sol_in.1) | copy-start | bytes 3145732
  1.2 38.7 %copy-start.14 = (s32[512]{0:T(512)S(1)}, s32[512]{0:T(512)}, u32[]{:S(2)}) copy-start(s32[512]{0:T(512)} %param.10) | copy-start | bytes 6148
  10.5 80.2 %collective-permute-start.1 = (f32[1792,128]{1,0:T(8,128)}, f32[1792,128]{1,0:T(8,128)S(1)}, u32[]{:S(2)}, u32[]{:S(2)}) collective-permute-start(f32[1792,128]{1,0:T(8,128)} %get-tuple-element.20), channel_id=1, source_target_pairs={{0,124},{4,0},{8,4},{12,8},{16,12},{20,16},{24,20},{28,24},{32,28}... | collective-permute-start | bytes 2752520 | tf_op jit(solution)/shard_map/ppermute | solution.py:793
  15.2 75.5 %collective-permute-start = (f32[1792,128]{1,0:T(8,128)}, f32[1792,128]{1,0:T(8,128)S(1)}, u32[]{:S(2)}, u32[]{:S(2)}) collective-permute-start(f32[1792,128]{1,0:T(8,128)} %get-tuple-element.21), channel_id=1, source_target_pairs={{0,4},{4,8},{8,12},{12,16},{16,20},{20,24},{24,28},{28,32},{32,36}... | collective-permute-start | bytes 2752520 | tf_op jit(solution)/shard_map/ppermute | solution.py:793
  15.2 75.5 %collective-permute-start.3 = (f32[1792,128]{1,0:T(8,128)}, f32[1792,128]{1,0:T(8,128)}, u32[]{:S(2)}, u32[]{:S(2)}) collective-permute-start(f32[1792,128]{1,0:T(8,128)} %get-tuple-element.22), channel_id=1, source_target_pairs={{0,3},{1,0},{2,1},{3,2},{4,7},{5,4},{6,5},{7,6},{8,11},{9,8},{10,9... | collective-permute-start | bytes 2752520 | tf_op jit(solution)/shard_map/ppermute | solution.py:793
  19.3 71.5 %collective-permute-start.2 = (f32[1792,128]{1,0:T(8,128)}, f32[1792,128]{1,0:T(8,128)}, u32[]{:S(2)}, u32[]{:S(2)}) collective-permute-start(f32[1792,128]{1,0:T(8,128)} %get-tuple-element.23), channel_id=1, source_target_pairs={{0,1},{1,2},{2,3},{3,0},{4,5},{5,6},{6,7},{7,4},{8,9},{9,10},{10,1... | collective-permute-start | bytes 2752520 | tf_op jit(solution)/shard_map/ppermute | solution.py:793
  39.9 1.2 %copy-start.1 = (f32[4,512,128]{2,1,0:T(8,128)S(1)}, f32[4,512,128]{2,1,0:T(8,128)}, u32[]{:S(2)}) copy-start(f32[4,512,128]{2,1,0:T(8,128)} %get-tuple-element.31.im_in) | copy-start | bytes 3145732
  41.2 1.2 %copy-start.2 = (f32[4,512,128]{2,1,0:T(8,128)S(1)}, f32[4,512,128]{2,1,0:T(8,128)}, u32[]{:S(2)}) copy-start(f32[4,512,128]{2,1,0:T(8,128)} %get-tuple-element.32.dg_in) | copy-start | bytes 3145732
  42.4 1.2 %copy-start.4 = (f32[128,1792]{1,0:T(8,128)S(1)}, f32[128,1792]{1,0:T(8,128)}, u32[]{:S(2)}) copy-start(f32[128,1792]{1,0:T(8,128)} %get-tuple-element.26.tf) | copy-start | bytes 2752516
  43.6 0.9 copy-start.5
  44.5 0.9 copy-start.10
  45.4 0.9 copy-start.11
  46.3 0.8 copy-start.12
  47.1 0.8 copy-start.13
  83.9 1.0 copy-start.3
  84.9 0.7 copy-start.6
  85.5 0.7 copy-start.7
  86.2 0.7 copy-start.8
  86.8 0.6 copy-start.9
  90.7 0.9 copy-start.15
  90.7 1.2 %copy-start.16 = (f32[1792,128]{1,0:T(8,128)}, f32[1792,128]{1,0:T(8,128)S(1)}, u32[]{:S(2)}) copy-start(f32[1792,128]{1,0:T(8,128)S(1)} %collective-permute-done.a0) | copy-start | bytes 2752516

commit v3 on v2

--- a/solution.py
+++ b/solution.py
@@ -198,36 +198,6 @@
     return jnp.where(keep, x[0:half], yl), jnp.where(keep, x[half:], yh)
 
 
-def pack_kernel(devs, owner_ref, met_ref, o0, o1, o2, o3, pa, pb):
-    @pl.when(pl.program_id(0) == 0)
-    def _():
-        _, leave, _ = move_rows(owner_ref[...], [devs[d] for d in range(5)], prefix_matrix())
-        pa[...] = onehot(small_row(leave, 256), 256)
-        pb[...] = onehot(small_row(swapped(leave), 256), 256)
-
-    out = pack_block(met_ref[0].reshape(NODES, E), pa[...], pb[...])
-    for ref, val in zip((o0, o1, o2, o3), out):
-        ref[...] = val
-
-
-def pack_metric(devs, owner, metric):
-    half = NODES // 2
-    return pl.pallas_call(
-        pack_kernel,
-        grid=(7,),
-        in_specs=[
-            pl.BlockSpec(memory_space=pltpu.SMEM),
-            pl.BlockSpec((1, E), lambda m: (0, 0)),
-            pl.BlockSpec((1, N, N, N, E), lambda m: (m, 0, 0, 0, 0)),
-        ],
-        out_specs=[pl.BlockSpec((half, 128), lambda m: (m, 0))] * 4,
-        out_shape=[jax.ShapeDtypeStruct((7 * half, 128), f32)] * 4,
-        scratch_shapes=[pltpu.VMEM((256, E), bf16)] * 2,
-        interpret=INTERPRET,
-        name="pack",
-    )(devs, owner, metric)
-
-
 def contract_i(src, table, put):
     for j in range(N):
         xs = [src(i, j) for i in range(N)]
@@ -261,27 +231,23 @@
     return ref[pl.ds(r * N, N), :]
 
 
-def apply_kernel(
-    devs, ids, sol, met, kmat, im_out, dg_out, key_out, tf, te, tc, md, ms,
-    vf, ve, vc, rix, ga, gb, gc, of, le, ol, acc_e,
-):
-    c = pl.program_id(0)
-
-    @pl.when(c == 0)
-    def _():
-        tri = prefix_matrix()
-        dv = [devs[d] for d in range(6)]
-        k, r = key_rows(ids[0:6], F_BLOCK, dv, 1536, None, 1664, tri)
-        key_out[0:6, :] = k
-        rix[0:6, :] = r
-        k, r = key_rows(ids[6:18], E_BLOCK, dv, 1536, 2016, 2048, tri)
-        key_out[6:18, :] = k
-        rix[6:18, :] = r
-        k, r = key_rows(ids[18:26], C_BLOCK, dv, 512, 960, 1024, tri)
-        key_out[18:26, :] = k
-        rix[18:26, :] = r
-
-    im, dg = im_out.at[0], dg_out.at[0]
+def make_keys(ids, devs, key_out, rix, tri):
+    k, r = key_rows(ids[0:6], F_BLOCK, devs, 1536, None, 1664, tri)
+    key_out[0:6, :] = k
+    rix[0:6, :] = r
+    k, r = key_rows(ids[6:18], E_BLOCK, devs, 1536, 2016, 2048, tri)
+    key_out[6:18, :] = k
+    rix[6:18, :] = r
+    k, r = key_rows(ids[18:26], C_BLOCK, devs, 512, 960, 1024, tri)
+    key_out[18:26, :] = k
+    rix[18:26, :] = r
+
+
+def apply_chunk(c, sol_all, met_all, kmat, im_all, dg_all, rix, vf, ve, vc, ga, gb, gc):
+    lanes = pl.ds(pl.multiple_of(c * 128, 128), 128)
+    sol = sol_all.at[:, :, :, lanes]
+    met = met_all.at[:, :, :, :, lanes]
+    im, dg = im_all.at[c], dg_all.at[c]
     fwd, bwd = kmat.at[0], kmat.at[1]
     half = NODES // 2
 
@@ -348,8 +314,6 @@
         dg[pl.ds((i * N + j) * N, N), :] += v
 
     contract_j(lambda i, j: met[1, i, j], SQUARED.T, add_dg_last)
-
-    lanes = pl.ds(pl.multiple_of(c * 128, 128), 128)
 
     def face(ref, f):
         if f < 2:
@@ -386,118 +350,63 @@
         vc[2:3, at] = rix[18 + q : 19 + q, lanes]
         vc[3:8, at] = jnp.zeros((5, 128), f32)
 
-    @pl.when(c == 3)
-    def _():
-        def face_block(n, carry):
-            for f in range(6):
-                of[:, f * E : (f + 1) * E] = onehot(small_row(key_out[f : f + 1, :] - n * 256, 256), 256)
-            acc = dot_nt(vf[...], of[...])
-            tf[:, pl.ds(pl.multiple_of(n * 256, 256), 256)] = sum3(acc)
-            return carry
-
-        lax.fori_loop(0, F_KEYS // 256, face_block, 0)
-
-        for e in range(12):
-            at = slice(e * E, (e + 1) * E)
-            key = key_out[6 + e : 7 + e, :]
-            hi = small_row(key >> 8, E_HI)
-            ol[:, at] = onehot(small_row(key & 255, 256), 256)
-            for g in range(4):
-                ag = slice(e * E + g * 128, e * E + (g + 1) * 128)
-                hb = jnp.broadcast_to(hi[:, g * 128 : (g + 1) * 128], (16, 128))
-                zero = jnp.zeros((16, 128), bf16)
-                parts = [ve[s * 16 : s * 16 + 16, ag] for s in range(3)]
-                for h in range(E_HI):
-                    m = hb == jnp.full((16, 128), float(h), bf16)
-                    for s in range(3):
-                        le[(s * E_HI + h) * 16 : (s * E_HI + h + 1) * 16, ag] = jnp.where(m, parts[s], zero)
-        acc_e[...] = dot_nt(le[...], ol[...])
-        for h in range(E_HI):
-            te[h] = sum(acc_e[(s * E_HI + h) * 16 : (s * E_HI + h + 1) * 16, :] for s in range(3))
-
-        full = E * 8
-        for q in range(8):
-            at = slice(q * E, (q + 1) * E)
-            ol[:, at] = onehot(small_row(key_out[18 + q : 19 + q, :] & 255, 256), 256)
-        hi = jnp.concatenate([key_out[18 + q : 19 + q, :] >> 8 for q in range(8)], axis=1)
-        x = vc[...]
-        big = jnp.concatenate(
-            [jnp.where(jnp.broadcast_to(hi, (8, full)) == h, x, 0.0) for h in range(C_HI)], axis=0
-        )
-        acc = sum3(dot_nt(stack3(big), ol[:, 0:full]))
-        for h in range(C_HI):
-            tc[h] = acc[h * 8 : (h + 1) * 8]
-
-        md[0:128, :] = tf[:, 1536:1664]
-        ms[0:128, :] = tf[:, 1664:1792]
+
+def scatter_shared(key_out, tf, te, tc, md, ms, vf, ve, vc, of, le, ol, acc_e):
+    def face_block(n, carry):
+        for f in range(6):
+            of[:, f * E : (f + 1) * E] = onehot(small_row(key_out[f : f + 1, :] - n * 256, 256), 256)
+        acc = dot_nt(vf[...], of[...])
+        tf[:, pl.ds(pl.multiple_of(n * 256, 256), 256)] = sum3(acc)
+        return carry
+
+    lax.fori_loop(0, F_KEYS // 256, face_block, 0)
+
+    for e in range(12):
+        at = slice(e * E, (e + 1) * E)
+        key = key_out[6 + e : 7 + e, :]
+        hi = small_row(key >> 8, E_HI)
+        ol[:, at] = onehot(small_row(key & 255, 256), 256)
         for g in range(4):
-            er, cr = msg_rows(g)
-            half_lanes = slice((g % 2) * 128, (g % 2) * 128 + 128)
-            md[er : er + 16, :] = te[6 + g // 2, :, half_lanes]
-            ms[er : er + 16, :] = te[8 + g // 2, :, half_lanes]
-            md[cr : cr + 8, :] = tc[2 + g // 2, :, half_lanes]
-            ms[cr : cr + 8, :] = tc[4 + g // 2, :, half_lanes]
+            ag = slice(e * E + g * 128, e * E + (g + 1) * 128)
+            hb = jnp.broadcast_to(hi[:, g * 128 : (g + 1) * 128], (16, 128))
+            zero = jnp.zeros((16, 128), bf16)
+            parts = [ve[s * 16 : s * 16 + 16, ag] for s in range(3)]
+            for h in range(E_HI):
+                m = hb == jnp.full((16, 128), float(h), bf16)
+                for s in range(3):
+                    le[(s * E_HI + h) * 16 : (s * E_HI + h + 1) * 16, ag] = jnp.where(m, parts[s], zero)
+    acc_e[...] = dot_nt(le[...], ol[...])
+    for h in range(E_HI):
+        te[h] = sum(acc_e[(s * E_HI + h) * 16 : (s * E_HI + h + 1) * 16, :] for s in range(3))
+
+    full = E * 8
+    for q in range(8):
+        at = slice(q * E, (q + 1) * E)
+        ol[:, at] = onehot(small_row(key_out[18 + q : 19 + q, :] & 255, 256), 256)
+    hi = jnp.concatenate([key_out[18 + q : 19 + q, :] >> 8 for q in range(8)], axis=1)
+    x = vc[...]
+    big = jnp.concatenate(
+        [jnp.where(jnp.broadcast_to(hi, (8, full)) == h, x, 0.0) for h in range(C_HI)], axis=0
+    )
+    acc = sum3(dot_nt(stack3(big), ol[:, 0:full]))
+    for h in range(C_HI):
+        tc[h] = acc[h * 8 : (h + 1) * 8]
+
+    md[0:128, :] = tf[:, 1536:1664]
+    ms[0:128, :] = tf[:, 1664:1792]
+    for g in range(4):
+        er, cr = msg_rows(g)
+        half_lanes = slice((g % 2) * 128, (g % 2) * 128 + 128)
+        md[er : er + 16, :] = te[6 + g // 2, :, half_lanes]
+        ms[er : er + 16, :] = te[8 + g // 2, :, half_lanes]
+        md[cr : cr + 8, :] = tc[2 + g // 2, :, half_lanes]
+        ms[cr : cr + 8, :] = tc[4 + g // 2, :, half_lanes]
 
 
 def msg_rows(g):
     if g < 3:
         return 128 + 16 * g, 176 + 8 * g
     return 200, 216
-
-
-def apply_scatter(devs, ids, solution, metric):
-    eye = np.eye(NODES // 2 // N, dtype=np.float32)
-    kmat = np.stack([np.kron(eye, TABLE), np.kron(eye, TABLE.T), np.kron(eye, SQUARED.T)])
-    chunk = lambda c: (c, 0, 0)
-    whole2 = lambda c: (0, 0)
-    whole3 = lambda c: (0, 0, 0)
-    return pl.pallas_call(
-        apply_kernel,
-        grid=(4,),
-        in_specs=[
-            pl.BlockSpec(memory_space=pltpu.SMEM),
-            pl.BlockSpec((26, E), whole2),
-            pl.BlockSpec((N, N, N, 128), lambda c: (0, 0, 0, c)),
-            pl.BlockSpec((7, N, N, N, 128), lambda c: (0, 0, 0, 0, c)),
-            pl.BlockSpec((3, 256, 256), whole3),
-        ],
-        out_specs=[
-            pl.BlockSpec((1, NODES, 128), chunk),
-            pl.BlockSpec((1, NODES, 128), chunk),
-            pl.BlockSpec((26, E), whole2),
-            pl.BlockSpec((128, F_KEYS), whole2),
-            pl.BlockSpec((E_HI, 16, 256), whole3),
-            pl.BlockSpec((C_HI, 8, 256), whole3),
-            pl.BlockSpec((MSG, 128), whole2),
-            pl.BlockSpec((MSG, 128), whole2),
-        ],
-        out_shape=[
-            jax.ShapeDtypeStruct((4, NODES, 128), f32),
-            jax.ShapeDtypeStruct((4, NODES, 128), f32),
-            jax.ShapeDtypeStruct((26, E), i32),
-            jax.ShapeDtypeStruct((128, F_KEYS), f32),
-            jax.ShapeDtypeStruct((E_HI, 16, 256), f32),
-            jax.ShapeDtypeStruct((C_HI, 8, 256), f32),
-            jax.ShapeDtypeStruct((MSG, 128), f32),
-            jax.ShapeDtypeStruct((MSG, 128), f32),
-        ],
-        scratch_shapes=[
-            pltpu.VMEM((384, 6 * E), bf16),
-            pltpu.VMEM((48, 12 * E), bf16),
-            pltpu.VMEM((8, 8 * E), f32),
-            pltpu.VMEM((26, E), f32),
-            pltpu.VMEM((NODES, 128), f32),
-            pltpu.VMEM((NODES, 128), f32),
-            pltpu.VMEM((NODES, 128), f32),
-            pltpu.VMEM((256, 6 * E), bf16),
-            pltpu.VMEM((3 * E_HI * 16, 12 * E), bf16),
-            pltpu.VMEM((256, 12 * E), bf16),
-            pltpu.VMEM((3 * E_HI * 16, 256), f32),
-        ],
-        compiler_params=pltpu.CompilerParams(vmem_limit_bytes=56 << 20),
-        interpret=INTERPRET,
-        name="apply",
-    )(devs, ids, solution, metric, kmat)
 
 
 def owner_sums(tf, te, tc, gd, gs, gboth, tf2, te2, tc2, rd, rs, rb):
@@ -633,12 +542,14 @@
 MESH = pl.DeviceIdType.MESH
 
 
-def exchange_kernel(
-    owner, keys, tf, te, tc, md, ms, im_in, dg_in, sol_in, forc_in,
+def main_kernel(
+    owner, ids, kmat_in, sol_in, forc_in, met_in,
     out, a0, a1, a2, a3,
+    met, sol, forc, kmat, im, dg, keys, rix, tf, te, tc, md, ms,
     gd, gs, gb, tf2, te2, tc2, sd, ss, sb, rd, rs, rb,
-    im, dg, sol, forc, tfs, of, gf, ge, gc, rel, p0, p1, p2, p3,
-    local_sem, send_sem, recv_sem,
+    vf, ve, vc, ga, gb2, gc2, of, le, ol, acc_e,
+    tfs, og, gf, ge, gc, rel, p0, p1, p2, p3, pa, pb,
+    load_sem, msg_send, msg_recv, move_send, move_recv,
 ):
     na, nb = lax.axis_size("dom"), lax.axis_size("sub")
     d, s = lax.axis_index("dom"), lax.axis_index("sub")
@@ -646,25 +557,60 @@
     sn, sp = lax.rem(s + 1, nb), lax.rem(s + nb - 1, nb)
     prev_dom, next_dom, prev_sub, next_sub = (dp, s), (dn, s), (d, sp), (d, sn)
     prev_both, next_both = (dp, sp), (dn, sn)
-    loads = [
-        pltpu.make_async_copy(src, dst, local_sem.at[n])
-        for n, (src, dst) in enumerate(((im_in, im), (dg_in, dg), (sol_in, sol), (forc_in, forc)))
-    ]
+    loads = [pltpu.make_async_copy(met_in.at[m], met.at[m], load_sem.at[m]) for m in range(7)]
+    loads.append(pltpu.make_async_copy(sol_in, sol, load_sem.at[7]))
+    loads.append(pltpu.make_async_copy(forc_in, forc, load_sem.at[8]))
+    loads.append(pltpu.make_async_copy(kmat_in, kmat, load_sem.at[9]))
     for copy in loads:
         copy.start()
 
     barrier = pltpu.get_barrier_semaphore()
     for peer in (prev_dom, next_dom, prev_sub, next_sub, prev_both, next_both):
         pl.semaphore_signal(barrier, inc=1, device_id=peer, device_id_type=MESH)
+
+    devs = [x * nb + y for x, y in ((d, s), prev_dom, next_dom, prev_sub, next_sub, next_both)]
+    tri = prefix_matrix()
+    make_keys(ids, devs, keys, rix, tri)
+    _, leave, _ = move_rows(owner[...], devs, tri)
+    pa[...] = onehot(small_row(leave, 256), 256)
+    pb[...] = onehot(small_row(swapped(leave), 256), 256)
     pl.semaphore_wait(barrier, 6)
 
-    def send(n, src, dst, peer):
+    def remote(src, dst, send_sem, recv_sem, peer):
         copy = pltpu.make_async_remote_copy(
-            src_ref=src, dst_ref=dst, send_sem=send_sem.at[n], recv_sem=recv_sem.at[n],
+            src_ref=src, dst_ref=dst, send_sem=send_sem, recv_sem=recv_sem,
             device_id=peer, device_id_type=MESH,
         )
         copy.start()
         return copy
+
+    half = NODES // 2
+    moves = []
+
+    def move(m, x):
+        for ref, val in zip((p0, p1, p2, p3), pack_block(x, pa[...], pb[...])):
+            ref[m] = val
+        for n, (src, dst, peer) in enumerate(
+            ((p2, a3, prev_sub), (p3, a2, next_sub), (p0, a1, prev_dom), (p1, a0, next_dom))
+        ):
+            moves.append(remote(src.at[m], dst.at[m], move_send.at[m, n], move_recv.at[m, n], peer))
+
+    for m in range(7):
+        loads[m].wait()
+        move(m, met[m].reshape(NODES, E))
+
+    loads[7].wait()
+    loads[9].wait()
+
+    def chunk(c, carry):
+        apply_chunk(c, sol, met, kmat, im, dg, rix, vf, ve, vc, ga, gb2, gc2)
+        return carry
+
+    lax.fori_loop(0, 4, chunk, 0)
+    scatter_shared(keys, tf, te, tc, md, ms, vf, ve, vc, of, le, ol, acc_e)
+
+    def send(n, src, dst, peer):
+        return remote(src, dst, msg_send.at[n], msg_recv.at[n], peer)
 
     first = [
         send(0, ms, gs, next_sub),
@@ -681,125 +627,109 @@
     ]
     for copy in second:
         copy.wait()
-    gather_shared(keys, tf2, te2, tc2, rd, rs, rb, tfs, of, gf, ge, gc)
-    for copy in loads:
+    gather_shared(keys, tf2, te2, tc2, rd, rs, rb, tfs, og, gf, ge, gc)
+    loads[8].wait()
+    place_relax(im, dg, gf, ge, gc, sol, forc, rel)
+    move(7, rel[...])
+    out[...] = rel[...].reshape(N, N, N, E)
+    for copy in moves:
         copy.wait()
-    place_relax(im, dg, gf, ge, gc, sol, forc, rel)
-    devs = [x * nb + y for x, y in ((d, s), prev_dom, next_dom, prev_sub, next_sub)]
-    _, leave, _ = move_rows(owner[...], devs, prefix_matrix())
-    pa = onehot(small_row(leave, 256), 256)
-    pb = onehot(small_row(swapped(leave), 256), 256)
-    for ref, val in zip((p0, p1, p2, p3), pack_block(rel[...], pa, pb)):
-        ref[...] = val
-    third = [
-        send(6, p2, a3, prev_sub),
-        send(7, p3, a2, next_sub),
-        send(8, p0, a1, prev_dom),
-        send(9, p1, a0, next_dom),
-    ]
-    out[...] = rel[...].reshape(N, N, N, E)
-    for copy in third:
-        copy.wait()
-
-
-def exchange_relax(owner, keys, tf, te, tc, md, ms, im, dg, solution, forcing):
+
+
+def main_call(owner, ids, solution, forcing, metric):
     half = NODES // 2
+    eye = np.eye(half // N, dtype=np.float32)
+    kmat = np.stack([np.kron(eye, TABLE), np.kron(eye, TABLE.T), np.kron(eye, SQUARED.T)])
     vm = pl.BlockSpec(memory_space=pltpu.VMEM)
     hbm = pl.BlockSpec(memory_space=pl.ANY)
+    box = pltpu.VMEM((N, N, N, E), f32)
+    planes = pltpu.VMEM((4, NODES, 128), f32)
     msg, both = pltpu.VMEM((MSG, 128), f32), pltpu.VMEM((BOTH, 128), f32)
+    work = pltpu.VMEM((NODES, 128), f32)
+    moved = pltpu.VMEM((8, half, 128), f32)
     return pl.pallas_call(
-        exchange_kernel,
-        in_specs=[vm] * 7 + [hbm] * 4,
-        out_shape=[jax.ShapeDtypeStruct((N, N, N, E), f32)] + [jax.ShapeDtypeStruct((half, 128), f32)] * 4,
+        main_kernel,
+        in_specs=[vm] * 2 + [hbm] * 4,
+        out_specs=[vm] * 5,
+        out_shape=[jax.ShapeDtypeStruct((N, N, N, E), f32)] + [jax.ShapeDtypeStruct((8, half, 128), f32)] * 4,
         scratch_shapes=[
+            pltpu.VMEM((7, N, N, N, E), f32), box, box,
+            pltpu.VMEM((3, 256, 256), f32), planes, planes,
+            pltpu.VMEM((26, E), i32),
+            pltpu.VMEM((26, E), f32),
+            pltpu.VMEM((128, F_KEYS), f32),
+            pltpu.VMEM((E_HI, 16, 256), f32),
+            pltpu.VMEM((C_HI, 8, 256), f32),
+            msg, msg,
             msg, msg, both,
             pltpu.VMEM((128, F_BLOCK), f32),
             pltpu.VMEM((E_BLOCK // 256, 16, 256), f32),
             pltpu.VMEM((C_BLOCK // 256, 8, 256), f32),
             msg, msg, both, msg, msg, both,
-            pltpu.VMEM((4, NODES, 128), f32),
-            pltpu.VMEM((4, NODES, 128), f32),
-            pltpu.VMEM((N, N, N, E), f32),
-            pltpu.VMEM((N, N, N, E), f32),
+            pltpu.VMEM((384, 6 * E), bf16),
+            pltpu.VMEM((48, 12 * E), bf16),
+            pltpu.VMEM((8, 8 * E), f32),
+            work, work, work,
+            pltpu.VMEM((256, 6 * E), bf16),
+            pltpu.VMEM((3 * E_HI * 16, 12 * E), bf16),
+            pltpu.VMEM((256, 12 * E), bf16),
+            pltpu.VMEM((3 * E_HI * 16, 256), f32),
             pltpu.VMEM((384, F_KEYS), bf16),
             pltpu.VMEM((F_KEYS, E), bf16),
             pltpu.VMEM((6, 128, E), f32),
             pltpu.VMEM((12, 16, E), f32),
             pltpu.VMEM((8, 8, E), f32),
             pltpu.VMEM((NODES, E), f32),
-            pltpu.VMEM((half, 128), f32),
-            pltpu.VMEM((half, 128), f32),
-            pltpu.VMEM((half, 128), f32),
-            pltpu.VMEM((half, 128), f32),
-            pltpu.SemaphoreType.DMA((4,)),
+            moved, moved, moved, moved,
+            pltpu.VMEM((256, E), bf16),
+            pltpu.VMEM((256, E), bf16),
             pltpu.SemaphoreType.DMA((10,)),
-            pltpu.SemaphoreType.DMA((10,)),
+            pltpu.SemaphoreType.DMA((6,)),
+            pltpu.SemaphoreType.DMA((6,)),
+            pltpu.SemaphoreType.DMA((8, 4)),
+            pltpu.SemaphoreType.DMA((8, 4)),
         ],
         compiler_params=pltpu.CompilerParams(
             vmem_limit_bytes=48 << 20, collective_id=0, has_side_effects=True
         ),
         interpret=pltpu.InterpretParams() if INTERPRET else False,
-        name="exchange",
-    )(owner, keys, tf, te, tc, md, ms, im, dg, solution, forcing)
-
-
-def land_kernel(devs, owner_ref, x_ref, a0, a1, a2, a3, out, pa, pb, dep):
-    @pl.when(pl.program_id(0) == 0)
-    def _():
-        departed, _, arrive = move_rows(owner_ref[...], [devs[d] for d in range(5)], prefix_matrix())
-        pa[...] = onehot(small_row(arrive, 256), 256)
-        pb[...] = onehot(small_row(swapped(arrive), 256), 256)
-        dep[...] = jnp.broadcast_to(jnp.where(departed, 1.0, 0.0), (8, E))
-
-    departed = dep[0:1, :] > 0.5
-    got = [a[...] for a in (a0, a1, a2, a3)]
-    shape = x_ref.shape
-    lo, hi = land_block(x_ref[...].reshape(NODES, E), got, pa[...], pb[...], departed)
-    half = shape[:-4] + (N // 2, N, N, E)
-    if len(shape) == 5:
-        out[0, 0:4] = lo.reshape(half[1:])
-        out[0, 4:8] = hi.reshape(half[1:])
-    else:
-        out[0:4] = lo.reshape(half)
-        out[4:8] = hi.reshape(half)
-
-
-def land(devs, owner, x, got, name):
-    half = NODES // 2
-    parts = x.shape[0] if x.ndim == 5 else 1
-    if x.ndim == 5:
-        spec = pl.BlockSpec((1, N, N, N, E), lambda m: (m, 0, 0, 0, 0))
-    else:
-        spec = pl.BlockSpec((N, N, N, E), lambda m: (0, 0, 0, 0))
+        name="main",
+    )(owner, ids, kmat, solution, forcing, metric)
+
+
+def land_kernel(devs, owner_ref, met_in, rel_in, a0, a1, a2, a3, met_out, rel_out, y, out_sem):
+    order = list(range(8))
+    departed, _, arrive = move_rows(owner_ref[...], [devs[d] for d in range(5)], prefix_matrix())
+    pa = onehot(small_row(arrive, 256), 256)
+    pb = onehot(small_row(swapped(arrive), 256), 256)
+    stores = []
+    for m in order:
+        x = (rel_in if m == 7 else met_in.at[m])[...].reshape(NODES, E)
+        lo, hi = land_block(x, [a[m] for a in (a0, a1, a2, a3)], pa, pb, departed)
+        y[m, 0:4] = lo.reshape(4, N, N, E)
+        y[m, 4:8] = hi.reshape(4, N, N, E)
+        stores.append(pltpu.make_async_copy(y.at[m], met_out.at[m] if m < 7 else rel_out, out_sem.at[m]))
+        stores[-1].start()
+    for copy in stores:
+        copy.wait()
+
+
+def land(devs, owner, metric, relaxed, got):
+    vm = pl.BlockSpec(memory_space=pltpu.VMEM)
+    hbm = pl.BlockSpec(memory_space=pltpu.HBM)
     return pl.pallas_call(
         land_kernel,
-        grid=(parts,),
-        in_specs=[
-            pl.BlockSpec(memory_space=pltpu.SMEM),
-            pl.BlockSpec((1, E), lambda m: (0, 0)),
-            spec,
-        ]
-        + [pl.BlockSpec((half, 128), lambda m: (m, 0))] * 4,
-        out_specs=spec,
-        out_shape=jax.ShapeDtypeStruct(x.shape, f32),
-        scratch_shapes=[pltpu.VMEM((256, E), bf16)] * 2 + [pltpu.VMEM((8, E), f32)],
+        in_specs=[pl.BlockSpec(memory_space=pltpu.SMEM)] + [vm] * 7,
+        out_specs=[hbm] * 2,
+        out_shape=[jax.ShapeDtypeStruct(metric.shape, f32), jax.ShapeDtypeStruct(relaxed.shape, f32)],
+        scratch_shapes=[
+            pltpu.VMEM((8, N, N, N, E), f32),
+            pltpu.SemaphoreType.DMA((8,)),
+        ],
+        compiler_params=pltpu.CompilerParams(vmem_limit_bytes=14 << 20),
         interpret=INTERPRET,
-        name=name,
-    )(devs, owner, x, *got)
-
-
-def shift(value, axis, steps):
-    count = lax.axis_size(axis)
-    return lax.ppermute(value, axis, [(s, (s + steps) % count) for s in range(count)])
-
-
-def exchange(sent):
-    return [
-        shift(sent[1], "dom", 1),
-        shift(sent[0], "dom", -1),
-        shift(sent[3], "sub", 1),
-        shift(sent[2], "sub", -1),
-    ]
+        name="land",
+    )(devs, owner, metric, relaxed, *got)
 
 
 def on_device(solution, forcing, metric, entity_ids, new_owner):
@@ -810,13 +740,8 @@
     devs = jnp.stack([d * b + s, db * b + s, da * b + s, d * b + sb, d * b + sa, da * b + sa]).astype(i32)
     owner = new_owner.reshape(1, E)
 
-    sent = pack_metric(devs, owner, metric)
-    arrived = exchange(sent)
-    later, *sent = lax.optimization_barrier((devs, *sent))
-    im, dg, keys, tf, te, tc, md, ms = apply_scatter(later, entity_ids, solution, metric)
-    relaxed, *moved = exchange_relax(owner, keys, tf, te, tc, md, ms, im, dg, solution, forcing)
-    moved_metric = land(devs, owner, metric, arrived, "land_metric")
-    smoothed = land(devs, owner, relaxed, moved, "land_field")
+    relaxed, *got = main_call(owner, entity_ids, solution, forcing, metric)
+    moved_metric, smoothed = land(devs, owner, metric, relaxed, got)
     return smoothed, moved_metric
 
 

time: 104 us -> 71 us (0.68)
  Pallas kernels: 80.6 us -> 66.9 us
  local copies, waits for them, and re-layouts: 13.3 us -> 3.12 us
  starting transfers between devices: 8.8 us -> 0 us
    pallas_call x5 -> x2, Pallas kernels: 80.6 us -> 66.9 us  [the longest x1 61.5 us: main_call(): pl.pallas_call(main_kernel, in_specs=[vm] * 2 + [hbm] * 4, out_specs=[vm]...]
    unnamed x34 -> x8, local copies, waits for them, and re-layouts: 12.7 us -> 3.04 us
    ppermute x4 -> x0, starting transfers between devices: 8.8 us -> none  [shift(): lax.ppermute(value, axis, [(s, (s + steps) % count) for s in range(count)])]
  transfers between devices with their start and end apart: 4 -> 0, of which waited for: 0 -> 0; matrix products, arithmetic and copies ran while one was open for 0% -> 0% of each run, Pallas kernels for 58% -> 0%
where the time goes in v3:
time: 71 us; the launch traced here: 70.9 us
  Pallas kernels  66.9 us (94%)
  local copies, waits for them, and re-layouts  3.12 us (4%)
  between operations  0.86 us (1%)
    pallas_call x1, Pallas kernels, main_call(): pl.pallas_call(main_kernel, in_specs=[vm] * 2 + [hbm] * 4, out_specs=[vm]...  61.5 us
    pallas_call x1, Pallas kernels, land(): pl.pallas_call(land_kernel, in_specs=[pl.BlockSpec(memory_space=pltpu.SME...  5.44 us
    unnamed x8, local copies, waits for them, and re-layouts  3.04 us

profile of v3, /device:TPU:0, one launch (start us, length us, event | category | flops | bytes accessed | tf_op | source)
XLA Modules:
  0.0 70.9 jit_solution(5350687266706979380)
XLA Ops:
  0.7 0.1 stack.27.devs
  0.8 0.0 copy-start
  0.8 0.0 copy-start.1
  0.8 1.3 %copy-done.1 = f32[3,256,256]{2,1,0:T(8,128)S(1)} copy-done((f32[3,256,256]{2,1,0:T(8,128)S(1)}, f32[3,256,256]{2,1,0:T(8,128)}, u32[]{:S(2)}) %copy-start.1) | copy-done | bytes 786456
  2.0 0.0 copy-start.2
  2.0 1.1 %copy-done.2 = s32[26,512]{1,0:T(8,128)S(1)} copy-done((s32[26,512]{1,0:T(8,128)S(1)}, s32[26,512]{1,0:T(8,128)}, u32[]{:S(2)}) %copy-start.2) | copy-done | bytes 53272
  3.1 0.0 copy-start.3
  3.1 0.7 copy-done.3
  3.8 61.5 %main.1 = (f32[8,8,8,512]{3,2,1,0:T(8,128)S(1)}, f32[8,256,128]{2,1,0:T(8,128)S(1)}, f32[8,256,128]{2,1,0:T(8,128)S(1)}, f32[8,256,128]{2,1,0:T(8,128)S(1)}, f32[8,256,128]{2,1,0:T(8,128)S(1)}) custom-call(s32[1,512]{1,0:T(1,128)S(1)} %bitcast.7, s32[26,512]{1,0:T(8,128)S(1)} %copy-done.2, f32[3,256,256]{2,1,0:T(8,128)S(1)} %copy-done.1, ...), custom_call_target="tpu_custom_call" | custom-call | tf_op jit(solution)/shard_map/main/pallas_call | solution.py:650
  65.3 0.0 copy-done
  65.3 5.4 %land.1 = (f32[7,8,8,8,512]{4,3,2,1,0:T(8,128)}, f32[8,8,8,512]{3,2,1,0:T(8,128)}) custom-call(s32[6]{0:T(128)S(1)} %stack.27.devs, s32[1,512]{1,0:T(1,128)S(1)} %bitcast.8, f32[7,8,8,8,512]{4,3,2,1,0:T(8,128)S(1)} %copy-done, f32[8,8,8,512]{3,2,1,0:T(8,128)S(1)} %get-tuple-element.9.rel_in, f32[8,256,128]{2,1,0:T(8,128)S(1)} %get-tuple-element.10.a0, ...), custom_call_target="tpu_custom_call" | custom-call | tf_op jit(solution)/shard_map/land/pallas_call | solution.py:720
Async XLA Ops:
  0.8 64.6 %copy-start = (f32[7,8,8,8,512]{4,3,2,1,0:T(8,128)S(1)}, f32[7,8,8,8,512]{4,3,2,1,0:T(8,128)}, u32[]{:S(2)}) copy-start(f32[7,8,8,8,512]{4,3,2,1,0:T(8,128)} %met_in.3) | copy-start | bytes 22020100
  0.8 1.3 %copy-start.1 = (f32[3,256,256]{2,1,0:T(8,128)S(1)}, f32[3,256,256]{2,1,0:T(8,128)}, u32[]{:S(2)}) copy-start(f32[3,256,256]{2,1,0:T(8,128)} %constant.48.clone.kmat_in) | copy-start | bytes 2359300
  2.0 1.1 %copy-start.2 = (s32[26,512]{1,0:T(8,128)S(1)}, s32[26,512]{1,0:T(8,128)}, u32[]{:S(2)}) copy-start(s32[26,512]{1,0:T(8,128)} %ids.1) | copy-start | bytes 159748
  3.1 0.7 copy-start.3

commit v4 on v3

v4 whole, which is shorter than its diff:
```python
import functools

import jax
import jax.numpy as jnp
import numpy as np
from jax import lax
from jax.experimental import pallas as pl
from jax.experimental.pallas import tpu as pltpu
from jax.sharding import PartitionSpec as P

N = 8
E = 512
NODES = N * N * N
EX = 4
EY = 4
EZ = 32
MOVE = 64
RELAX = 0.6
F_BLOCK, E_BLOCK, C_BLOCK = 3 * E, 3 * E, E
F_KEYS, E_KEYS, C_KEYS = 1792, 2560, 1536
E_HI, C_HI = E_KEYS // 256, C_KEYS // 256
PLANE = 48
F_ROWS = 2 * PLANE
LINES = 96
BOTH = 24
INTERPRET = False

f32, bf16, i32 = jnp.float32, jnp.bfloat16, jnp.int32


def derivative_table(order):
    count = order + 1
    points = -np.cos(np.pi * np.arange(count) / order)
    legendre = np.zeros((count, count))
    for sweep in range(80):
        legendre[:, 0] = 1.0
        legendre[:, 1] = points
        for degree in range(2, count):
            legendre[:, degree] = (
                (2 * degree - 1) * points * legendre[:, degree - 1]
                - (degree - 1) * legendre[:, degree - 2]
            ) / degree
        points = points - (points * legendre[:, order] - legendre[:, order - 1]) / (
            count * legendre[:, order]
        )
    legendre[:, 0] = 1.0
    legendre[:, 1] = points
    for degree in range(2, count):
        legendre[:, degree] = (
            (2 * degree - 1) * points * legendre[:, degree - 1]
            - (degree - 1) * legendre[:, degree - 2]
        ) / degree
    values = legendre[:, order]
    identity = np.eye(count)
    spread = points[:, None] - points[None, :] + identity
    table = values[:, None] / values[None, :] / spread
    table = table * (1.0 - identity)
    table[0, 0] = -order * count / 4.0
    table[order, order] = order * count / 4.0
    return table.astype(np.float32)


TABLE = derivative_table(N - 1)
SQUARED = TABLE * TABLE
ALONG = [float(v) for v in np.diagonal(TABLE)]


def row_of(i, j, k):
    return (i * N + j) * N + k


EDGE_ROWS = (
    [(row_of(0, a, b), N * N) for a in (0, 7) for b in (0, 7)]
    + [(row_of(a, 0, b), N) for a in (0, 7) for b in (0, 7)]
    + [(row_of(a, b, 0), 1) for a in (0, 7) for b in (0, 7)]
)
CORNER_ROWS = [row_of(a, b, c) for a in (0, 7) for b in (0, 7) for c in (0, 7)]


def split2(x):
    hi = x.astype(bf16)
    return hi, (x - hi.astype(f32)).astype(bf16)


def stack2(x):
    return jnp.concatenate(split2(x), axis=0)


def sum2(x):
    m = x.shape[0] // 2
    return x[0:m] + x[m:]


def dot_nn(a, b):
    return lax.dot_general(a, b, (((1,), (0,)), ((), ())), preferred_element_type=f32)


def dot_nt(a, b):
    return lax.dot_general(a, b, (((1,), (1,)), ((), ())), preferred_element_type=f32)


def small_row(key, count):
    ok = (key >= 0) & (key < count)
    return jnp.where(ok, key, -1).astype(f32).astype(bf16)


def iota_rows(count, lanes):
    return lax.broadcasted_iota(i32, (count, lanes), 0).astype(f32).astype(bf16)


def onehot(row, count):
    lanes = row.shape[1]
    io = iota_rows(count, 128)
    one, zero = jnp.ones((count, 128), bf16), jnp.zeros((count, 128), bf16)
    cols = [
        jnp.where(io == jnp.broadcast_to(row[:, g : g + 128], (count, 128)), one, zero)
        for g in range(0, lanes, 128)
    ]
    return cols[0] if len(cols) == 1 else jnp.concatenate(cols, axis=1)


def prefix_matrix():
    a = lax.broadcasted_iota(i32, (E, E), 0)
    b = lax.broadcasted_iota(i32, (E, E), 1)
    return jnp.where(a <= b, 1.0, 0.0).astype(bf16)


def ranks(mask, tri):
    m = mask.shape[0]
    flags = jnp.where(mask, 1.0, 0.0)
    within = dot_nn(flags.astype(bf16), tri) - 1.0
    if m > 1:
        before = jnp.zeros((1, 1), f32)
        offs = [before]
        for r in range(m - 1):
            before = before + jnp.sum(flags[r : r + 1], axis=1, keepdims=True)
            offs.append(before)
        within = within + jnp.concatenate(offs, axis=0)
    return within.astype(i32)


def move_rows(owner, devs, tri):
    own = devs[0]
    departed = owner != own
    leave = jnp.full((1, E), -1, i32)
    arrive = jnp.full((1, E), -1, i32)
    flags = [departed] + [departed & (owner == devs[d]) for d in range(1, 5)]
    stacked = jnp.concatenate([jnp.where(f, 1.0, 0.0) for f in flags] + [jnp.zeros((3, E), f32)], axis=0)
    pre = dot_nn(stacked.astype(bf16), tri)
    hole = pre[0:1] - 1.0
    start = jnp.zeros((1, 1), f32)
    for d in range(4):
        chosen = flags[d + 1]
        rank = pre[d + 1 : d + 2] - 1.0
        leave = jnp.where(chosen, d * MOVE + rank.astype(i32), leave)
        count = pre[d + 1 : d + 2, E - 1 : E]
        pos = hole - start
        inside = departed & (pos >= 0.0) & (pos < count)
        arrive = jnp.where(inside, d * MOVE + pos.astype(i32), arrive)
        start = start + count
    return departed, leave, arrive


def swapped(col):
    return jnp.where(col >= 0, col ^ MOVE, -1)


def lane_low(rows):
    return lax.broadcasted_iota(i32, (rows, 128), 1) < MOVE


def pack_block(x, pa, pb):
    half = NODES // 2
    ya = sum2(dot_nt(stack2(x[0:half]), pa))
    yb = sum2(dot_nt(stack2(x[half:]), pb))
    low = lane_low(half)
    out = []
    for g in (0, 128):
        a, b = ya[:, g : g + 128], yb[:, g : g + 128]
        out.append(jnp.where(low, a, b))
        out.append(jnp.where(low, b, a))
    return out


def land_block(x, got, pa, pb, departed, out):
    half = NODES // 2
    low = lane_low(half)
    zl, zh = [], []
    for g in (0, 2):
        zl.append(jnp.where(low, got[g + 1], got[g]))
        zh.append(jnp.where(low, got[g], got[g + 1]))
    keep = jnp.logical_not(departed)
    for at, z, p in ((slice(0, 4), zl, pb), (slice(4, 8), zh, pa)):
        y = sum2(dot_nn(stack2(jnp.concatenate(z, axis=1)), p))
        v = jnp.where(keep, x[at].reshape(half, E), y)
        out[at] = v.reshape(4, N, N, E)


def halves(table):
    t = table.astype(np.float64)
    return (t[:4, :4] + t[:4, :3:-1]) / 2, (t[:4, :4] - t[:4, :3:-1]) / 2


def combine(xs, table, odd):
    even_w, odd_w = halves(table)
    e = [xs[p] + xs[7 - p] for p in range(4)]
    o = [xs[p] - xs[7 - p] for p in range(4)]
    out = [None] * N
    for a in range(4):
        u = sum(float(even_w[a, p]) * e[p] for p in range(4))
        v = sum(float(odd_w[a, p]) * o[p] for p in range(4))
        out[a] = v + u
        out[7 - a] = v - u if odd else u - v
    return out


def contract_i(src, table, odd, put):
    for j in range(N):
        for a, v in enumerate(combine([src(i, j) for i in range(N)], table, odd)):
            put(a, j, v)


def contract_j(src, table, odd, put):
    for i in range(N):
        for b, v in enumerate(combine([src(i, j) for j in range(N)], table, odd)):
            put(i, b, v)


def key_rows(ids, block, devs, dom_base, both_base, sub_base, tri):
    rel, inside = [], []
    for d in (0, 2, 4, 5):
        r = ids - devs[d] * block
        rel.append(r)
        inside.append((r >= 0) & (r < block))
    key = jnp.where(inside[0], rel[0], -1)
    key = jnp.where(inside[1], dom_base + ranks(inside[1], tri), key)
    key = jnp.where(inside[2], sub_base + ranks(inside[2], tri), key)
    if both_base is not None:
        key = jnp.where(inside[3], both_base + ranks(inside[3], tri), key)
    row = jnp.where(inside[0], rel[0], jnp.where(inside[1], rel[1], jnp.where(inside[2], rel[2], rel[3])))
    return key, row.astype(f32)


def tile(ref, r):
    return ref[pl.ds(r * N, N), :]


def make_keys(ids, devs, key_out, rix, tri):
    k, r = key_rows(ids[0:6], F_BLOCK, devs, 1536, None, 1664, tri)
    key_out[0:6, :] = k
    rix[0:6, :] = r
    k, r = key_rows(ids[6:18], E_BLOCK, devs, 1536, 2016, 2048, tri)
    key_out[6:18, :] = k
    rix[6:18, :] = r
    k, r = key_rows(ids[18:26], C_BLOCK, devs, 512, 960, 1024, tri)
    key_out[18:26, :] = k
    rix[18:26, :] = r


def apply_chunk(c, sol_all, met_all, kmat, im_all, dg_all, rix, vf, ve, vc, ga, gb, gc):
    lanes = pl.ds(pl.multiple_of(c * 128, 128), 128)
    sol = sol_all.at[:, :, :, lanes]
    met = [m.at[:, :, :, lanes] for m in met_all]
    im, dg = im_all.at[c], dg_all.at[c]
    fwd, bwd = kmat.at[0], kmat.at[1]
    slab = N * N

    def kdot(m, x):
        return lax.dot_general(
            m, x, (((1,), (0,)), ((), ())),
            precision=lax.Precision.HIGHEST, preferred_element_type=f32,
        )

    def put_a(i, j, v):
        ga[pl.ds((i * N + j) * N, N), :] = v

    def put_b(i, j, v):
        gb[pl.ds((i * N + j) * N, N), :] = v

    contract_i(lambda i, j: sol[i, j], TABLE, True, put_a)
    contract_j(lambda i, j: sol[i, j], TABLE, True, put_b)
    for h in range(N):
        gc[h * slab : (h + 1) * slab, :] = kdot(fwd[...], sol[h].reshape(slab, 128))

    for i in range(N):
        for j in range(N):
            r = i * N + j
            a, b, t = tile(ga, r), tile(gb, r), tile(gc, r)
            m3, m4, m5 = met[3][i, j], met[4][i, j], met[5][i, j]
            ga[pl.ds(r * N, N), :] = met[0][i, j] * a + m3 * b + m4 * t
            gb[pl.ds(r * N, N), :] = m3 * a + met[1][i, j] * b + m5 * t
            gc[pl.ds(r * N, N), :] = m4 * a + m5 * b + met[2][i, j] * t

    for h in range(N):
        im[h * slab : (h + 1) * slab, :] = kdot(bwd[...], gc[h * slab : (h + 1) * slab, :])

    def add_im(i, j, v):
        im[pl.ds((i * N + j) * N, N), :] += v

    contract_i(lambda i, j: tile(ga, i * N + j), TABLE.T, True, add_im)

    def add_im_last(i, j, v):
        im[pl.ds((i * N + j) * N, N), :] += v + met[6][i, j] * sol[i, j]

    contract_j(lambda i, j: tile(gb, i * N + j), TABLE.T, True, add_im_last)

    sq = kmat.at[2]
    for h in range(N):
        dg[h * slab : (h + 1) * slab, :] = kdot(sq[...], met[2][h].reshape(slab, 128))

    def add_dg(i, j, v):
        dg[pl.ds((i * N + j) * N, N), :] += v

    contract_i(lambda i, j: met[0][i, j], SQUARED.T, False, add_dg)
    kk = lax.broadcasted_iota(i32, (N, 128), 0)
    dk = jnp.where(kk == 0, ALONG[0], jnp.where(kk == N - 1, ALONG[N - 1], 0.0))

    def add_dg_last(i, j, v):
        v = v + met[6][i, j]
        if ALONG[i] * ALONG[j] != 0.0:
            v = v + (2.0 * ALONG[i] * ALONG[j]) * met[3][i, j]
        if ALONG[i] != 0.0:
            v = v + (2.0 * ALONG[i]) * dk * met[4][i, j]
        if ALONG[j] != 0.0:
            v = v + (2.0 * ALONG[j]) * dk * met[5][i, j]
        dg[pl.ds((i * N + j) * N, N), :] += v

    contract_j(lambda i, j: met[1][i, j], SQUARED.T, False, add_dg_last)

    def face(ref, f):
        if f < 2:
            base = 8 if f == 0 else 456
            return ref[base : base + PLANE, :]
        if f < 4:
            j = 0 if f == 2 else 7
            return jnp.concatenate([ref[pl.ds((i * N + j) * N, N), :] for i in range(1, 7)], axis=0)
        return ref[pl.ds(64 if f == 4 else 71, PLANE, stride=N), :]

    top = lax.broadcasted_iota(i32, (N, 128), 0) == 0
    for f in range(6):
        at = pl.ds(pl.multiple_of(f * E + c * 128, 128), 128)
        a, b = face(im, f), face(dg, f)
        mark = jnp.broadcast_to(rix[f : f + 1, lanes], (N, 128))
        a = jnp.concatenate([jnp.where(top, mark, a[0:N]), a[N:]], axis=0)
        for s, (p, q) in enumerate(zip(split2(a), split2(b))):
            vf[s * F_ROWS : s * F_ROWS + PLANE, at] = p
            vf[s * F_ROWS + PLANE : (s + 1) * F_ROWS, at] = q
    for e in range(12):
        at = pl.ds(pl.multiple_of(e * E + c * 128, 128), 128)
        start, stride = EDGE_ROWS[e]
        rows = pl.ds(start, N) if stride == 1 else pl.ds(start, N, stride=stride)
        a, b = im[rows, :], dg[rows, :]
        mark = jnp.broadcast_to(rix[6 + e : 7 + e, lanes], (N, 128))
        x = jnp.concatenate([jnp.where(top, mark, a), b], axis=0)
        for s, p in enumerate(split2(x)):
            ve[s * 16 : s * 16 + 16, at] = p
    for q in range(8):
        at = pl.ds(pl.multiple_of(q * E + c * 128, 128), 128)
        r = CORNER_ROWS[q]
        vc[0:1, at] = im[r : r + 1, :]
        vc[1:2, at] = dg[r : r + 1, :]
        vc[2:3, at] = rix[18 + q : 19 + q, lanes]
        vc[3:8, at] = jnp.zeros((5, 128), f32)


def scatter_faces(key_out, tf, fd, fs, vf, of):
    def face_block(n, carry):
        for f in range(6):
            of[:, f * E : (f + 1) * E] = onehot(small_row(key_out[f : f + 1, :] - n * 256, 256), 256)
        acc = dot_nt(vf[...], of[...])
        tf[:, pl.ds(pl.multiple_of(n * 256, 256), 256)] = sum2(acc)
        return carry

    lax.fori_loop(0, F_KEYS // 256, face_block, 0)
    fd[...] = tf[:, 1536:1664]
    fs[...] = tf[:, 1664:1792]


def scatter_lines(key_out, te, tc, md, ms, ve, vc, le, ol, acc_e):
    for e in range(12):
        at = slice(e * E, (e + 1) * E)
        key = key_out[6 + e : 7 + e, :]
        hi = small_row(key >> 8, E_HI)
        ol[:, at] = onehot(small_row(key & 255, 256), 256)
        for g in range(4):
            ag = slice(e * E + g * 128, e * E + (g + 1) * 128)
            hb = jnp.broadcast_to(hi[:, g * 128 : (g + 1) * 128], (16, 128))
            zero = jnp.zeros((16, 128), bf16)
            parts = [ve[s * 16 : s * 16 + 16, ag] for s in range(2)]
            for h in range(E_HI):
                m = hb == jnp.full((16, 128), float(h), bf16)
                for s in range(2):
                    le[(s * E_HI + h) * 16 : (s * E_HI + h + 1) * 16, ag] = jnp.where(m, parts[s], zero)
    acc_e[...] = dot_nt(le[...], ol[...])
    for h in range(E_HI):
        te[h] = sum(acc_e[(s * E_HI + h) * 16 : (s * E_HI + h + 1) * 16, :] for s in range(2))

    full = E * 8
    for q in range(8):
        at = slice(q * E, (q + 1) * E)
        ol[:, at] = onehot(small_row(key_out[18 + q : 19 + q, :] & 255, 256), 256)
    hi = jnp.concatenate([key_out[18 + q : 19 + q, :] >> 8 for q in range(8)], axis=1)
    x = vc[...]
    big = jnp.concatenate(
        [jnp.where(jnp.broadcast_to(hi, (8, full)) == h, x, 0.0) for h in range(C_HI)], axis=0
    )
    acc = sum2(dot_nt(stack2(big), ol[:, 0:full]))
    for h in range(C_HI):
        tc[h] = acc[h * 8 : (h + 1) * 8]

    for g in range(4):
        er, cr = msg_rows(g)
        half_lanes = slice((g % 2) * 128, (g % 2) * 128 + 128)
        md[er : er + 16, :] = te[6 + g // 2, :, half_lanes]
        ms[er : er + 16, :] = te[8 + g // 2, :, half_lanes]
        md[cr : cr + 8, :] = tc[2 + g // 2, :, half_lanes]
        ms[cr : cr + 8, :] = tc[4 + g // 2, :, half_lanes]


def msg_rows(g):
    if g < 3:
        return 16 * g, 48 + 8 * g
    return 72, 88


def owner_faces(tf, gd, gs, tf2, rd, rs):
    vals = jnp.concatenate([gd[...], gs[...]], axis=1)
    key = vals[0:1, :].astype(i32)
    vs = stack2(vals)
    ret = jnp.zeros((2 * F_ROWS, 256), f32)
    for n in range(F_BLOCK // 256):
        o = onehot(small_row(key - n * 256, 256), 256)
        total = tf[:, n * 256 : (n + 1) * 256] + sum2(dot_nt(vs, o))
        tf2[:, n * 256 : (n + 1) * 256] = total
        ret = ret + dot_nn(stack2(total), o)
    ret = sum2(ret)
    rd[...] = ret[:, 0:128]
    rs[...] = ret[:, 128:256]


def owner_lines(te, tc, gd, gs, gboth, te2, tc2, rd, rs, rb):
    lane = lax.broadcasted_iota(i32, (1, 128), 1)

    def lines(rows, id_row, total_ref, total_out, his, cut, at):
        vals, keys = [], []
        for src in (gd, gs):
            for g in range(4):
                r = msg_rows(g)[at]
                v = src[r : r + rows, :]
                k = v[id_row : id_row + 1].astype(i32)
                if src is gd and g == 3:
                    k = jnp.where(lane >= cut, -1, k)
                vals.append(v)
                keys.append(k)
        r = msg_rows(3)[at] - (LINES - BOTH)
        v = gboth[r : r + rows, :]
        keys.append(jnp.where(lane < cut, -1, v[id_row : id_row + 1].astype(i32)))
        vals.append(v)
        x = jnp.concatenate(vals, axis=1)
        key = jnp.concatenate(keys, axis=1)
        hi = key >> 8
        o = onehot(small_row(key & 255, 256), 256)
        big = jnp.concatenate([jnp.where(jnp.broadcast_to(hi, x.shape) == h, x, 0.0) for h in range(his)], axis=0)
        acc = sum2(dot_nt(stack2(big), o))
        totals = jnp.concatenate([total_ref[h] for h in range(his)], axis=0) + acc
        for h in range(his):
            total_out[h] = totals[h * rows : (h + 1) * rows]
        y = sum2(dot_nn(stack2(totals), o))
        back = jnp.zeros_like(x)
        for h in range(his):
            back = jnp.where(jnp.broadcast_to(hi, x.shape) == h, y[h * rows : (h + 1) * rows], back)
        for n, dst in enumerate((rd, rs)):
            for g in range(4):
                p = msg_rows(g)[at]
                dst[p : p + rows, :] = back[:, (n * 4 + g) * 128 : (n * 4 + g + 1) * 128]
        rb[r : r + rows, :] = back[:, 1024:1152]

    lines(16, 0, te, te2, E_BLOCK // 256, 96, 0)
    lines(8, 2, tc, tc2, C_BLOCK // 256, 64, 1)


def gather_faces(keys, tf, rd, rs, tfs, of, gf):
    for ref, at in ((tf, slice(0, 1536)), (rd, slice(1536, 1664)), (rs, slice(1664, 1792))):
        for s, p in enumerate(split2(ref[...])):
            tfs[s * F_ROWS : (s + 1) * F_ROWS, at] = p

    def face_gather(f, carry):
        key = keys[pl.ds(f, 1), :]
        for n in range(F_KEYS // 256):
            of[n * 256 : (n + 1) * 256, :] = onehot(small_row(key - n * 256, 256), 256)
        gf[f] = sum2(dot_nn(tfs[...], of[...]))
        return carry

    lax.fori_loop(0, 6, face_gather, 0)


def gather_lines(keys, te, tc, rd, rs, rb, ge, gc):
    lane = lax.broadcasted_iota(i32, (1, 128), 1)

    def table(own, his, rows, at, cut):
        blocks = [own[h] for h in range(his)]
        for src in (rd, rs):
            for g in (0, 2):
                pair = []
                for q in (g, g + 1):
                    r = msg_rows(q)[at]
                    v = src[r : r + rows, :]
                    if src is rd and q == 3:
                        b = r - (LINES - BOTH)
                        v = jnp.where(jnp.broadcast_to(lane, (rows, 128)) >= cut, rb[b : b + rows, :], v)
                    pair.append(v)
                blocks.append(jnp.concatenate(pair, axis=1))
        return stack2(jnp.concatenate(blocks, axis=0))

    def line_gather(tab, first, count, his, rows, dst):
        for q in range(count):
            key = keys[first + q : first + q + 1, :]
            hi = key >> 8
            y = sum2(dot_nn(tab, onehot(small_row(key & 255, 256), 256)))
            back = jnp.zeros((rows, E), f32)
            for h in range(his):
                back = jnp.where(jnp.broadcast_to(hi, (rows, E)) == h, y[h * rows : (h + 1) * rows], back)
            dst[q] = back

    line_gather(table(te, 6, 16, 0, 96), 6, 12, E_HI, 16, ge)
    line_gather(table(tc, 2, 8, 1, 64), 18, 8, C_HI, 8, gc)

def place_relax(im, dg, gf, ge, gc, sol, forc, rel):
    for c in range(4):
        at = slice(c * 128, (c + 1) * 128)
        for ref, base in ((im.at[c], 0), (dg.at[c], 1)):
            for f in range(6):
                v = gf[f, base * PLANE : (base + 1) * PLANE, at]
                if f < 2:
                    start = 8 if f == 0 else 456
                    ref[start : start + PLANE, :] = v
                elif f < 4:
                    j = 0 if f == 2 else 7
                    for i in range(1, 7):
                        ref[pl.ds((i * N + j) * N, N), :] = v[(i - 1) * N : i * N]
                else:
                    ref[pl.ds(64 if f == 4 else 71, PLANE, stride=N), :] = v
            for e in range(12):
                start, stride = EDGE_ROWS[e]
                rows = pl.ds(start, N) if stride == 1 else pl.ds(start, N, stride=stride)
                ref[rows, :] = ge[e, base * 8 : base * 8 + 8, at]
            for q in range(8):
                r = CORNER_ROWS[q]
                ref[r : r + 1, :] = gc[q, base : base + 1, at]
        s = sol[:, :, :, at].reshape(NODES, 128)
        v = s + RELAX * (forc[:, :, :, at].reshape(NODES, 128) - im[c]) / dg[c]
        rel[:, :, :, at] = v.reshape(N, N, N, 128)

MESH = pl.DeviceIdType.MESH


def main_kernel(
    owner, ids, kmat_in, sol_in, forc_in, met_in,
    m0, m1, m2, m3, m4, m5, m6, rel, f0, f1, f2, f3,
    sol, forc, kmat, im, dg, keys, rix, tf, te, tc, fd, fs, md, ms,
    gfd, gfs, gd, gs, gb, tf2, te2, tc2, sfd, sfs, sd, ss, sb, rfd, rfs, rd, rs, rb,
    vf, ve, vc, ga, gb2, gc2, of, le, ol, acc_e,
    tfs, og, gf, ge, gc, p0, p1, p2, p3, a0, a1, a2, a3, pa, pb,
    load_sem, msg_send, msg_recv, move_send, move_recv,
):
    na, nb = lax.axis_size("dom"), lax.axis_size("sub")
    d, s = lax.axis_index("dom"), lax.axis_index("sub")
    dn, dp = lax.rem(d + 1, na), lax.rem(d + na - 1, na)
    sn, sp = lax.rem(s + 1, nb), lax.rem(s + nb - 1, nb)
    prev_dom, next_dom, prev_sub, next_sub = (dp, s), (dn, s), (d, sp), (d, sn)
    prev_both, next_both = (dp, sp), (dn, sn)
    met = (m0, m1, m2, m3, m4, m5, m6)
    loads = [pltpu.make_async_copy(met_in.at[m], met[m], load_sem.at[m]) for m in range(7)]
    loads.append(pltpu.make_async_copy(sol_in, sol, load_sem.at[7]))
    loads.append(pltpu.make_async_copy(forc_in, forc, load_sem.at[8]))
    loads.append(pltpu.make_async_copy(kmat_in, kmat, load_sem.at[9]))
    for copy in loads:
        copy.start()

    barrier = pltpu.get_barrier_semaphore()
    for peer in (prev_dom, next_dom, prev_sub, next_sub, prev_both, next_both):
        pl.semaphore_signal(barrier, inc=1, device_id=peer, device_id_type=MESH)

    devs = [x * nb + y for x, y in ((d, s), prev_dom, next_dom, prev_sub, next_sub, next_both)]
    tri = prefix_matrix()
    make_keys(ids, devs, keys, rix, tri)
    _, leave, _ = move_rows(owner[...], devs, tri)
    pa[...] = onehot(small_row(leave, 256), 256)
    pb[...] = onehot(small_row(swapped(leave), 256), 256)
    pl.semaphore_wait(barrier, 6)

    def remote(src, dst, send_sem, recv_sem, peer):
        copy = pltpu.make_async_remote_copy(
            src_ref=src, dst_ref=dst, send_sem=send_sem, recv_sem=recv_sem,
            device_id=peer, device_id_type=MESH,
        )
        copy.start()
        return copy

    half = NODES // 2
    moves = []

    def move(m, x):
        for ref, val in zip((p0, p1, p2, p3), pack_block(x, pa[...], pb[...])):
            ref[m] = val
        for n, (src, dst, last, peer) in enumerate((
            (p2, a3, f3, prev_sub), (p3, a2, f2, next_sub), (p0, a1, f1, prev_dom), (p1, a0, f0, next_dom),
        )):
            to = last if m == 7 else dst.at[m]
            moves.append(remote(src.at[m], to, move_send.at[m, n], move_recv.at[m, n], peer))

    for m in range(7):
        loads[m].wait()
        move(m, met[m][...].reshape(NODES, E))

    loads[7].wait()
    loads[9].wait()

    def chunk(c, carry):
        apply_chunk(c, sol, met, kmat, im, dg, rix, vf, ve, vc, ga, gb2, gc2)
        return carry

    lax.fori_loop(0, 4, chunk, 0)

    def send(n, src, dst, peer):
        return remote(src, dst, msg_send.at[n], msg_recv.at[n], peer)

    scatter_faces(keys, tf, fd, fs, vf, of)
    face_out = [send(0, fs, gfs, next_sub), send(1, fd, gfd, next_dom)]
    scatter_lines(keys, te, tc, md, ms, ve, vc, le, ol, acc_e)
    line_out = [
        send(2, ms, gs, next_sub),
        send(3, md, gd, next_dom),
        send(4, md.at[pl.ds(LINES - BOTH, BOTH)], gb, next_both),
    ]
    for copy in face_out:
        copy.wait()
    owner_faces(tf, gfd, gfs, tf2, sfd, sfs)
    face_back = [send(5, sfs, rfs, prev_sub), send(6, sfd, rfd, prev_dom)]
    for copy in line_out:
        copy.wait()
    owner_lines(te, tc, gd, gs, gb, te2, tc2, sd, ss, sb)
    line_back = [send(7, ss, rs, prev_sub), send(8, sd, rd, prev_dom), send(9, sb, rb, prev_both)]
    for copy in face_back:
        copy.wait()
    gather_faces(keys, tf2, rfd, rfs, tfs, og, gf)
    for copy in line_back:
        copy.wait()
    gather_lines(keys, te2, tc2, rd, rs, rb, ge, gc)
    loads[8].wait()
    place_relax(im, dg, gf, ge, gc, sol, forc, rel)
    move(7, rel[...].reshape(NODES, E))
    departed, _, arrive = move_rows(owner[...], devs, tri)
    pa[...] = onehot(small_row(arrive, 256), 256)
    pb[...] = onehot(small_row(swapped(arrive), 256), 256)
    for m in range(7):
        for copy in moves[4 * m : 4 * m + 4]:
            copy.wait()
        land_block(met[m], [a[m] for a in (a0, a1, a2, a3)], pa[...], pb[...], departed, met[m])
    for copy in moves[28:]:
        copy.wait()


def main_call(owner, ids, solution, forcing, metric):
    half = NODES // 2
    eye = np.eye(N, dtype=np.float32)
    kmat = np.stack([np.kron(eye, TABLE), np.kron(eye, TABLE.T), np.kron(eye, SQUARED.T)])
    vm = pl.BlockSpec(memory_space=pltpu.VMEM)
    hbm = pl.BlockSpec(memory_space=pl.ANY)
    box = pltpu.VMEM((N, N, N, E), f32)
    planes = pltpu.VMEM((4, NODES, 128), f32)
    face, line, both = (pltpu.VMEM((r, 128), f32) for r in (F_ROWS, LINES, BOTH))
    work = pltpu.VMEM((NODES, 128), f32)
    moved = pltpu.VMEM((8, half, 128), f32)
    came = pltpu.VMEM((7, half, 128), f32)
    return pl.pallas_call(
        main_kernel,
        in_specs=[vm] * 2 + [hbm] * 4,
        out_specs=[vm] * 12,
        out_shape=[jax.ShapeDtypeStruct((N, N, N, E), f32)] * 8
        + [jax.ShapeDtypeStruct((half, 128), f32)] * 4,
        scratch_shapes=[
            box, box,
            pltpu.VMEM((3, 64, 64), f32), planes, planes,
            pltpu.VMEM((26, E), i32),
            pltpu.VMEM((26, E), f32),
            pltpu.VMEM((F_ROWS, F_KEYS), f32),
            pltpu.VMEM((E_HI, 16, 256), f32),
            pltpu.VMEM((C_HI, 8, 256), f32),
            face, face, line, line,
            face, face, line, line, both,
            pltpu.VMEM((F_ROWS, F_BLOCK), f32),
            pltpu.VMEM((E_BLOCK // 256, 16, 256), f32),
            pltpu.VMEM((C_BLOCK // 256, 8, 256), f32),
            face, face, line, line, both,
            face, face, line, line, both,
            pltpu.VMEM((2 * F_ROWS, 6 * E), bf16),
            pltpu.VMEM((32, 12 * E), bf16),
            pltpu.VMEM((8, 8 * E), f32),
            work, work, work,
            pltpu.VMEM((256, 6 * E), bf16),
            pltpu.VMEM((2 * E_HI * 16, 12 * E), bf16),
            pltpu.VMEM((256, 12 * E), bf16),
            pltpu.VMEM((2 * E_HI * 16, 256), f32),
            pltpu.VMEM((2 * F_ROWS, F_KEYS), bf16),
            pltpu.VMEM((F_KEYS, E), bf16),
            pltpu.VMEM((6, F_ROWS, E), f32),
            pltpu.VMEM((12, 16, E), f32),
            pltpu.VMEM((8, 8, E), f32),
            moved, moved, moved, moved,
            came, came, came, came,
            pltpu.VMEM((256, E), bf16),
            pltpu.VMEM((256, E), bf16),
            pltpu.SemaphoreType.DMA((10,)),
            pltpu.SemaphoreType.DMA((10,)),
            pltpu.SemaphoreType.DMA((10,)),
            pltpu.SemaphoreType.DMA((8, 4)),
            pltpu.SemaphoreType.DMA((8, 4)),
        ],
        compiler_params=pltpu.CompilerParams(
            vmem_limit_bytes=45 << 20, collective_id=0, has_side_effects=True
        ),
        interpret=pltpu.InterpretParams() if INTERPRET else False,
        name="main",
    )(owner, ids, kmat, solution, forcing, metric)


def land_kernel(
    devs, owner_ref, m0, m1, m2, m3, m4, m5, m6, rel_in, f0, f1, f2, f3, met_out, rel_out, y, out_sem
):
    met = (m0, m1, m2, m3, m4, m5, m6)
    stores = [pltpu.make_async_copy(met[m], met_out.at[m], out_sem.at[m]) for m in range(7)]
    for copy in stores:
        copy.start()
    departed, _, arrive = move_rows(owner_ref[...], [devs[d] for d in range(5)], prefix_matrix())
    pa = onehot(small_row(arrive, 256), 256)
    pb = onehot(small_row(swapped(arrive), 256), 256)
    land_block(rel_in, [f[...] for f in (f0, f1, f2, f3)], pa, pb, departed, y)
    stores.append(pltpu.make_async_copy(y, rel_out, out_sem.at[7]))
    stores[7].start()
    for copy in stores:
        copy.wait()


def land(devs, owner, shape, blocks):
    vm = pl.BlockSpec(memory_space=pltpu.VMEM)
    hbm = pl.BlockSpec(memory_space=pltpu.HBM)
    return pl.pallas_call(
        land_kernel,
        in_specs=[pl.BlockSpec(memory_space=pltpu.SMEM)] + [vm] * 13,
        out_specs=[hbm] * 2,
        out_shape=[jax.ShapeDtypeStruct(shape, f32), jax.ShapeDtypeStruct(shape[1:], f32)],
        scratch_shapes=[
            pltpu.VMEM((N, N, N, E), f32),
            pltpu.SemaphoreType.DMA((8,)),
        ],
        compiler_params=pltpu.CompilerParams(vmem_limit_bytes=8 << 20),
        interpret=INTERPRET,
        name="land",
    )(devs, owner, *blocks)


def on_device(solution, forcing, metric, entity_ids, new_owner):
    a, b = lax.axis_size("dom"), lax.axis_size("sub")
    d, s = lax.axis_index("dom"), lax.axis_index("sub")
    da, db = (d + 1) % a, (d + a - 1) % a
    sa, sb = (s + 1) % b, (s + b - 1) % b
    devs = jnp.stack([d * b + s, db * b + s, da * b + s, d * b + sb, d * b + sa, da * b + sa]).astype(i32)
    owner = new_owner.reshape(1, E)

    blocks = main_call(owner, entity_ids, solution, forcing, metric)
    moved_metric, smoothed = land(devs, owner, metric.shape, blocks)
    return smoothed, moved_metric


def solution(mesh):
    cols = ("dom", "sub")
    placed = (
        P(None, None, None, cols),
        P(None, None, None, cols),
        P(None, None, None, None, cols),
        P(None, cols),
        P(cols),
    )
    return jax.shard_map(
        on_device,
        mesh=mesh,
        in_specs=placed,
        out_specs=(P(None, None, None, cols), P(None, None, None, None, cols)),
        check_vma=False,
    )
```

time: 71 us -> 53.6 us (0.75)
  Pallas kernels: 66.9 us -> 50 us
    pallas_call x1, Pallas kernels: 61.5 us -> 46.1 us  [main_call(): pl.pallas_call(main_kernel, in_specs=[vm] * 2 + [hbm] * 4, out_specs=[vm]...]
    pallas_call x1, Pallas kernels: 5.44 us -> 3.91 us  [land(): pl.pallas_call(land_kernel, in_specs=[pl.BlockSpec(memory_space=pltpu.SME...]
    unnamed x8 -> x6, local copies, waits for them, and re-layouts: 3.04 us -> 2.41 us
where the time goes in v4:
time: 53.6 us; the launch traced here: 53.4 us
  Pallas kernels  50 us (93%)
  local copies, waits for them, and re-layouts  2.5 us (5%)
  between operations  0.85 us (2%)
    pallas_call x1, Pallas kernels, main_call(): pl.pallas_call(main_kernel, in_specs=[vm] * 2 + [hbm] * 4, out_specs=[vm]...  46.1 us
    pallas_call x1, Pallas kernels, land(): pl.pallas_call(land_kernel, in_specs=[pl.BlockSpec(memory_space=pltpu.SME...  3.91 us
    unnamed x6, local copies, waits for them, and re-layouts  2.41 us

profile of v4, /device:TPU:0, one launch (start us, length us, event | category | flops | bytes accessed | tf_op | source)
XLA Modules:
  0.0 53.4 jit_solution(12173119755192838131)
XLA Ops:
  0.7 0.1 stack.27.devs
  0.8 0.0 copy-start
  0.8 0.9 %copy-done = f32[3,64,64]{2,1,0:T(8,128)S(1)} copy-done((f32[3,64,64]{2,1,0:T(8,128)S(1)}, f32[3,64,64]{2,1,0:T(8,128)}, u32[]{:S(2)}) %copy-start) | copy-done | bytes 49176
  1.7 0.0 copy-start.1
  1.7 0.8 %copy-done.1 = s32[26,512]{1,0:T(8,128)S(1)} copy-done((s32[26,512]{1,0:T(8,128)S(1)}, s32[26,512]{1,0:T(8,128)}, u32[]{:S(2)}) %copy-start.1) | copy-done | bytes 53272
  2.5 0.0 copy-start.2
  2.5 0.7 %copy-done.2 = s32[512]{0:T(512)S(1)} copy-done((s32[512]{0:T(512)S(1)}, s32[512]{0:T(512)}, u32[]{:S(2)}) %copy-start.2) | copy-done | bytes 2072
  3.2 46.1 %main.1 = (f32[8,8,8,512]{3,2,1,0:T(8,128)S(1)}, f32[8,8,8,512]{3,2,1,0:T(8,128)S(1)}, f32[8,8,8,512]{3,2,1,0:T(8,128)S(1)}, f32[8,8,8,512]{3,2,1,0:T(8,128)S(1)...) custom-call(s32[1,512]{1,0:T(1,128)S(1)} %bitcast.7, ...), custom_call_target="tpu_custom_call" | custom-call | tf_op jit(solution)/shard_map/main/pallas_call | solution.py:676
  49.3 3.9 %land.1 = (f32[7,8,8,8,512]{4,3,2,1,0:T(8,128)}, f32[8,8,8,512]{3,2,1,0:T(8,128)}) custom-call(s32[6]{0:T(128)S(1)} %stack.27.devs, s32[1,512]{1,0:T(1,128)S(1)} %bitcast.8, f32[8,8,8,512]{3,2,1,0:T(8,128)S(1)} %get-tuple-element.16.m0, f32[8,8,8,512]{3,2,1,0:T(8,128)S(1)} %get-tuple-element.17.m1, f32[8,8,8,512]{3,2,1,0:T(8,128)S(1)} %get-tuple-element.18.m2, ...), custom_call_target="tpu_custom_call" | custom-call | tf_op jit(solution)/shard_map/land/pallas_call | solution.py:748
Async XLA Ops:
  0.8 0.9 %copy-start = (f32[3,64,64]{2,1,0:T(8,128)S(1)}, f32[3,64,64]{2,1,0:T(8,128)}, u32[]{:S(2)}) copy-start(f32[3,64,64]{2,1,0:T(8,128)} %constant.48.clone.kmat_in) | copy-start | bytes 147460
  1.7 0.8 %copy-start.1 = (s32[26,512]{1,0:T(8,128)S(1)}, s32[26,512]{1,0:T(8,128)}, u32[]{:S(2)}) copy-start(s32[26,512]{1,0:T(8,128)} %ids.1) | copy-start | bytes 159748
  2.5 0.7 %copy-start.2 = (s32[512]{0:T(512)S(1)}, s32[512]{0:T(512)}, u32[]{:S(2)}) copy-start(s32[512]{0:T(512)} %param.10) | copy-start | bytes 6148

commit v5 on v4

--- a/solution.py
+++ b/solution.py
@@ -18,7 +18,7 @@
 RELAX = 0.6
 F_BLOCK, E_BLOCK, C_BLOCK = 3 * E, 3 * E, E
 F_KEYS, E_KEYS, C_KEYS = 1792, 2560, 1536
-E_HI, C_HI = E_KEYS // 256, C_KEYS // 256
+F_HI, E_HI, C_HI = F_KEYS // 256, E_KEYS // 256, C_KEYS // 256
 PLANE = 48
 F_ROWS = 2 * PLANE
 LINES = 96
@@ -196,6 +196,19 @@
         out[at] = v.reshape(4, N, N, E)
 
 
+def block_table(table):
+    r = lax.broadcasted_iota(i32, (N, 64), 0)
+    c = lax.broadcasted_iota(i32, (N, 64), 1)
+    tile_of = jnp.zeros((N, 64), f32)
+    low = c & 7
+    for a in range(N):
+        row = jnp.zeros((N, 64), f32)
+        for i in range(N):
+            row = jnp.where(low == i, float(table[a, i]), row)
+        tile_of = jnp.where(r == a, row, tile_of)
+    return jnp.concatenate([jnp.where(c >> 3 == b, tile_of, 0.0) for b in range(N)], axis=0)
+
+
 def halves(table):
     t = table.astype(np.float64)
     return (t[:4, :4] + t[:4, :3:-1]) / 2, (t[:4, :4] - t[:4, :3:-1]) / 2
@@ -363,15 +376,22 @@
         vc[3:8, at] = jnp.zeros((5, 128), f32)
 
 
-def scatter_faces(key_out, tf, fd, fs, vf, of):
-    def face_block(n, carry):
-        for f in range(6):
-            of[:, f * E : (f + 1) * E] = onehot(small_row(key_out[f : f + 1, :] - n * 256, 256), 256)
-        acc = dot_nt(vf[...], of[...])
-        tf[:, pl.ds(pl.multiple_of(n * 256, 256), 256)] = sum2(acc)
-        return carry
-
-    lax.fori_loop(0, F_KEYS // 256, face_block, 0)
+def scatter_faces(key_out, tf, fd, fs, vf, lf, of, acc_f):
+    rows = 2 * F_ROWS
+    zero = jnp.zeros((rows, 128), bf16)
+    for f in range(6):
+        key = key_out[f : f + 1, :]
+        hi = small_row(key >> 8, F_HI)
+        of[:, f * E : (f + 1) * E] = onehot(small_row(key & 255, 256), 256)
+        for g in range(4):
+            at = slice(f * E + g * 128, f * E + (g + 1) * 128)
+            hb = jnp.broadcast_to(hi[:, g * 128 : (g + 1) * 128], (rows, 128))
+            part = vf[:, at]
+            for h in range(F_HI):
+                lf[h * rows : (h + 1) * rows, at] = jnp.where(hb == jnp.full((rows, 128), float(h), bf16), part, zero)
+    acc_f[...] = dot_nt(lf[...], of[...])
+    for h in range(F_HI):
+        tf[:, h * 256 : (h + 1) * 256] = sum2(acc_f[h * rows : (h + 1) * rows, :])
     fd[...] = tf[:, 1536:1664]
     fs[...] = tf[:, 1664:1792]
 
@@ -555,12 +575,12 @@
 
 
 def main_kernel(
-    owner, ids, kmat_in, sol_in, forc_in, met_in,
+    owner_in, ids_in, sol_in, forc_in, met_in,
     m0, m1, m2, m3, m4, m5, m6, rel, f0, f1, f2, f3,
-    sol, forc, kmat, im, dg, keys, rix, tf, te, tc, fd, fs, md, ms,
+    owner, ids, sol, forc, kmat, im, dg, keys, rix, tf, te, tc, fd, fs, md, ms,
     gfd, gfs, gd, gs, gb, tf2, te2, tc2, sfd, sfs, sd, ss, sb, rfd, rfs, rd, rs, rb,
-    vf, ve, vc, ga, gb2, gc2, of, le, ol, acc_e,
-    tfs, og, gf, ge, gc, p0, p1, p2, p3, a0, a1, a2, a3, pa, pb,
+    vf, ve, vc, ga, gb2, gc2, lf, of, acc_f, le, ol, acc_e,
+    tfs, og, gf, ge, gc, p0, p1, p2, p3, a0, a1, a2, a3, pa, pb, pc, pd,
     load_sem, msg_send, msg_recv, move_send, move_recv,
 ):
     na, nb = lax.axis_size("dom"), lax.axis_size("sub")
@@ -573,8 +593,8 @@
     loads = [pltpu.make_async_copy(met_in.at[m], met[m], load_sem.at[m]) for m in range(7)]
     loads.append(pltpu.make_async_copy(sol_in, sol, load_sem.at[7]))
     loads.append(pltpu.make_async_copy(forc_in, forc, load_sem.at[8]))
-    loads.append(pltpu.make_async_copy(kmat_in, kmat, load_sem.at[9]))
-    for copy in loads:
+    early = [pltpu.make_async_copy(owner_in, owner, load_sem.at[9]), pltpu.make_async_copy(ids_in, ids, load_sem.at[10])]
+    for copy in early + loads:
         copy.start()
 
     barrier = pltpu.get_barrier_semaphore()
@@ -583,10 +603,14 @@
 
     devs = [x * nb + y for x, y in ((d, s), prev_dom, next_dom, prev_sub, next_sub, next_both)]
     tri = prefix_matrix()
-    make_keys(ids, devs, keys, rix, tri)
-    _, leave, _ = move_rows(owner[...], devs, tri)
+    for n, table in enumerate((TABLE, TABLE.T, SQUARED.T)):
+        kmat[n] = block_table(table)
+    for copy in early:
+        copy.wait()
+    departed, leave, arrive = move_rows(owner[...], devs, tri)
     pa[...] = onehot(small_row(leave, 256), 256)
     pb[...] = onehot(small_row(swapped(leave), 256), 256)
+    make_keys(ids, devs, keys, rix, tri)
     pl.semaphore_wait(barrier, 6)
 
     def remote(src, dst, send_sem, recv_sem, peer):
@@ -600,9 +624,11 @@
     half = NODES // 2
     moves = []
 
-    def move(m, x):
+    def fill(m, x):
         for ref, val in zip((p0, p1, p2, p3), pack_block(x, pa[...], pb[...])):
             ref[m] = val
+
+    def push(m):
         for n, (src, dst, last, peer) in enumerate((
             (p2, a3, f3, prev_sub), (p3, a2, f2, next_sub), (p0, a1, f1, prev_dom), (p1, a0, f0, next_dom),
         )):
@@ -611,10 +637,11 @@
 
     for m in range(7):
         loads[m].wait()
-        move(m, met[m][...].reshape(NODES, E))
+        fill(m, met[m][...].reshape(NODES, E))
+        if m < 5:
+            push(m)
 
     loads[7].wait()
-    loads[9].wait()
 
     def chunk(c, carry):
         apply_chunk(c, sol, met, kmat, im, dg, rix, vf, ve, vc, ga, gb2, gc2)
@@ -625,7 +652,7 @@
     def send(n, src, dst, peer):
         return remote(src, dst, msg_send.at[n], msg_recv.at[n], peer)
 
-    scatter_faces(keys, tf, fd, fs, vf, of)
+    scatter_faces(keys, tf, fd, fs, vf, lf, of, acc_f)
     face_out = [send(0, fs, gfs, next_sub), send(1, fd, gfd, next_dom)]
     scatter_lines(keys, te, tc, md, ms, ve, vc, le, ol, acc_e)
     line_out = [
@@ -633,6 +660,8 @@
         send(3, md, gd, next_dom),
         send(4, md.at[pl.ds(LINES - BOTH, BOTH)], gb, next_both),
     ]
+    pc[...] = onehot(small_row(arrive, 256), 256)
+    pd[...] = onehot(small_row(swapped(arrive), 256), 256)
     for copy in face_out:
         copy.wait()
     owner_faces(tf, gfd, gfs, tf2, sfd, sfs)
@@ -641,6 +670,8 @@
         copy.wait()
     owner_lines(te, tc, gd, gs, gb, te2, tc2, sd, ss, sb)
     line_back = [send(7, ss, rs, prev_sub), send(8, sd, rd, prev_dom), send(9, sb, rb, prev_both)]
+    for m in range(5, 7):
+        push(m)
     for copy in face_back:
         copy.wait()
     gather_faces(keys, tf2, rfd, rfs, tfs, og, gf)
@@ -649,22 +680,18 @@
     gather_lines(keys, te2, tc2, rd, rs, rb, ge, gc)
     loads[8].wait()
     place_relax(im, dg, gf, ge, gc, sol, forc, rel)
-    move(7, rel[...].reshape(NODES, E))
-    departed, _, arrive = move_rows(owner[...], devs, tri)
-    pa[...] = onehot(small_row(arrive, 256), 256)
-    pb[...] = onehot(small_row(swapped(arrive), 256), 256)
+    fill(7, rel[...].reshape(NODES, E))
+    push(7)
     for m in range(7):
         for copy in moves[4 * m : 4 * m + 4]:
             copy.wait()
-        land_block(met[m], [a[m] for a in (a0, a1, a2, a3)], pa[...], pb[...], departed, met[m])
+        land_block(met[m], [a[m] for a in (a0, a1, a2, a3)], pc[...], pd[...], departed, met[m])
     for copy in moves[28:]:
         copy.wait()
 
 
 def main_call(owner, ids, solution, forcing, metric):
     half = NODES // 2
-    eye = np.eye(N, dtype=np.float32)
-    kmat = np.stack([np.kron(eye, TABLE), np.kron(eye, TABLE.T), np.kron(eye, SQUARED.T)])
     vm = pl.BlockSpec(memory_space=pltpu.VMEM)
     hbm = pl.BlockSpec(memory_space=pl.ANY)
     box = pltpu.VMEM((N, N, N, E), f32)
@@ -675,11 +702,13 @@
     came = pltpu.VMEM((7, half, 128), f32)
     return pl.pallas_call(
         main_kernel,
-        in_specs=[vm] * 2 + [hbm] * 4,
+        in_specs=[hbm] * 5,
         out_specs=[vm] * 12,
         out_shape=[jax.ShapeDtypeStruct((N, N, N, E), f32)] * 8
         + [jax.ShapeDtypeStruct((half, 128), f32)] * 4,
         scratch_shapes=[
+            pltpu.VMEM((1, E), i32),
+            pltpu.VMEM((26, E), i32),
             box, box,
             pltpu.VMEM((3, 64, 64), f32), planes, planes,
             pltpu.VMEM((26, E), i32),
@@ -698,7 +727,9 @@
             pltpu.VMEM((32, 12 * E), bf16),
             pltpu.VMEM((8, 8 * E), f32),
             work, work, work,
+            pltpu.VMEM((2 * F_ROWS * F_HI, 6 * E), bf16),
             pltpu.VMEM((256, 6 * E), bf16),
+            pltpu.VMEM((2 * F_ROWS * F_HI, 256), f32),
             pltpu.VMEM((2 * E_HI * 16, 12 * E), bf16),
             pltpu.VMEM((256, 12 * E), bf16),
             pltpu.VMEM((2 * E_HI * 16, 256), f32),
@@ -711,18 +742,20 @@
             came, came, came, came,
             pltpu.VMEM((256, E), bf16),
             pltpu.VMEM((256, E), bf16),
-            pltpu.SemaphoreType.DMA((10,)),
+            pltpu.VMEM((256, E), bf16),
+            pltpu.VMEM((256, E), bf16),
+            pltpu.SemaphoreType.DMA((11,)),
             pltpu.SemaphoreType.DMA((10,)),
             pltpu.SemaphoreType.DMA((10,)),
             pltpu.SemaphoreType.DMA((8, 4)),
             pltpu.SemaphoreType.DMA((8, 4)),
         ],
         compiler_params=pltpu.CompilerParams(
-            vmem_limit_bytes=45 << 20, collective_id=0, has_side_effects=True
+            vmem_limit_bytes=47448064, collective_id=0, has_side_effects=True
         ),
         interpret=pltpu.InterpretParams() if INTERPRET else False,
         name="main",
-    )(owner, ids, kmat, solution, forcing, metric)
+    )(owner, ids, solution, forcing, metric)
 
 
 def land_kernel(

time: 53.6 us -> 49.9 us (0.931)
  Pallas kernels: 50 us -> 47.2 us
  local copies, waits for them, and re-layouts: 2.5 us -> 1.61 us
    pallas_call x1, Pallas kernels: 46.1 us -> 43.3 us  [main_call(): pl.pallas_call(main_kernel, in_specs=[hbm] * 5, out_specs=[vm] * 12, out_...]
    unnamed x6 -> x4, local copies, waits for them, and re-layouts: 2.41 us -> 1.52 us
where the time goes in v5:
time: 49.9 us; the launch traced here: 49.7 us
  Pallas kernels  47.2 us (95%)
  local copies, waits for them, and re-layouts  1.61 us (3%)
  between operations  0.85 us (2%)
    pallas_call x1, Pallas kernels, main_call(): pl.pallas_call(main_kernel, in_specs=[hbm] * 5, out_specs=[vm] * 12, out_...  43.3 us
    pallas_call x1, Pallas kernels, land(): pl.pallas_call(land_kernel, in_specs=[pl.BlockSpec(memory_space=pltpu.SME...  3.91 us
    unnamed x4, local copies, waits for them, and re-layouts  1.52 us

profile of v5, /device:TPU:0, one launch (start us, length us, event | category | flops | bytes accessed | tf_op | source)
XLA Modules:
  0.0 49.7 jit_solution(16759379094428006212)
XLA Ops:
  0.7 0.1 stack.27.devs
  0.8 0.0 copy-start
  0.8 0.8 %copy-done = s32[26,512]{1,0:T(8,128)S(1)} copy-done((s32[26,512]{1,0:T(8,128)S(1)}, s32[26,512]{1,0:T(8,128)}, u32[]{:S(2)}) %copy-start) | copy-done | bytes 53272
  1.6 0.0 copy-start.1
  1.6 0.7 %copy-done.1 = s32[512]{0:T(512)S(1)} copy-done((s32[512]{0:T(512)S(1)}, s32[512]{0:T(512)}, u32[]{:S(2)}) %copy-start.1) | copy-done | bytes 2072
  2.3 43.3 %main.1 = (f32[8,8,8,512]{3,2,1,0:T(8,128)S(1)}, f32[8,8,8,512]{3,2,1,0:T(8,128)S(1)}, f32[8,8,8,512]{3,2,1,0:T(8,128)S(1)}, f32[8,8,8,512]{3,2,1,0:T(8,128)S(1)...) custom-call(s32[1,512]{1,0:T(1,128)S(1)} %bitcast.7, ...), custom_call_target="tpu_custom_call" | custom-call | tf_op jit(solution)/shard_map/main/pallas_call | solution.py:703
  45.6 3.9 %land.1 = (f32[7,8,8,8,512]{4,3,2,1,0:T(8,128)}, f32[8,8,8,512]{3,2,1,0:T(8,128)}) custom-call(s32[6]{0:T(128)S(1)} %stack.27.devs, s32[1,512]{1,0:T(1,128)S(1)} %bitcast.8, f32[8,8,8,512]{3,2,1,0:T(8,128)S(1)} %get-tuple-element.16.m0, f32[8,8,8,512]{3,2,1,0:T(8,128)S(1)} %get-tuple-element.17.m1, f32[8,8,8,512]{3,2,1,0:T(8,128)S(1)} %get-tuple-element.18.m2, ...), custom_call_target="tpu_custom_call" | custom-call | tf_op jit(solution)/shard_map/land/pallas_call | solution.py:781
Async XLA Ops:
  0.8 0.8 %copy-start = (s32[26,512]{1,0:T(8,128)S(1)}, s32[26,512]{1,0:T(8,128)}, u32[]{:S(2)}) copy-start(s32[26,512]{1,0:T(8,128)} %ids_in.1) | copy-start | bytes 159748
  1.6 0.7 %copy-start.1 = (s32[512]{0:T(512)S(1)}, s32[512]{0:T(512)}, u32[]{:S(2)}) copy-start(s32[512]{0:T(512)} %param.9) | copy-start | bytes 6148

commit v6 on v5

--- a/solution.py
+++ b/solution.py
@@ -270,30 +270,39 @@
     rix[18:26, :] = r
 
 
-def apply_chunk(c, sol_all, met_all, kmat, im_all, dg_all, rix, vf, ve, vc, ga, gb, gc):
+def kdot(m, x):
+    return lax.dot_general(
+        m, x, (((1,), (0,)), ((), ())),
+        precision=lax.Precision.HIGHEST, preferred_element_type=f32,
+    )
+
+
+def gradient_chunk(c, sol_all, kmat, ga_all, gb_all, gc_all):
+    lanes = pl.ds(pl.multiple_of(c * 128, 128), 128)
+    sol = sol_all.at[:, :, :, lanes]
+    ga, gb, gc = ga_all.at[c], gb_all.at[c], gc_all.at[c]
+    slab = N * N
+
+    def put_a(i, j, v):
+        ga[pl.ds((i * N + j) * N, N), :] = v
+
+    def put_b(i, j, v):
+        gb[pl.ds((i * N + j) * N, N), :] = v
+
+    contract_i(lambda i, j: sol[i, j], TABLE, True, put_a)
+    contract_j(lambda i, j: sol[i, j], TABLE, True, put_b)
+    for h in range(N):
+        gc[h * slab : (h + 1) * slab, :] = kdot(kmat[0], sol[h].reshape(slab, 128))
+
+
+def apply_chunk(c, sol_all, met_all, kmat, im_all, dg_all, rix, vf, ve, vc, ga_all, gb_all, gc_all):
     lanes = pl.ds(pl.multiple_of(c * 128, 128), 128)
     sol = sol_all.at[:, :, :, lanes]
     met = [m.at[:, :, :, lanes] for m in met_all]
     im, dg = im_all.at[c], dg_all.at[c]
-    fwd, bwd = kmat.at[0], kmat.at[1]
+    ga, gb, gc = ga_all.at[c], gb_all.at[c], gc_all.at[c]
+    bwd = kmat.at[1]
     slab = N * N
-
-    def kdot(m, x):
-        return lax.dot_general(
-            m, x, (((1,), (0,)), ((), ())),
-            precision=lax.Precision.HIGHEST, preferred_element_type=f32,
-        )
-
-    def put_a(i, j, v):
-        ga[pl.ds((i * N + j) * N, N), :] = v
-
-    def put_b(i, j, v):
-        gb[pl.ds((i * N + j) * N, N), :] = v
-
-    contract_i(lambda i, j: sol[i, j], TABLE, True, put_a)
-    contract_j(lambda i, j: sol[i, j], TABLE, True, put_b)
-    for h in range(N):
-        gc[h * slab : (h + 1) * slab, :] = kdot(fwd[...], sol[h].reshape(slab, 128))
 
     for i in range(N):
         for j in range(N):
@@ -444,18 +453,28 @@
 
 
 def owner_faces(tf, gd, gs, tf2, rd, rs):
+    rows, his = 2 * F_ROWS, F_BLOCK // 256
     vals = jnp.concatenate([gd[...], gs[...]], axis=1)
     key = vals[0:1, :].astype(i32)
+    hi = key >> 8
+    o = onehot(small_row(key & 255, 256), 256)
     vs = stack2(vals)
-    ret = jnp.zeros((2 * F_ROWS, 256), f32)
-    for n in range(F_BLOCK // 256):
-        o = onehot(small_row(key - n * 256, 256), 256)
-        total = tf[:, n * 256 : (n + 1) * 256] + sum2(dot_nt(vs, o))
-        tf2[:, n * 256 : (n + 1) * 256] = total
-        ret = ret + dot_nn(stack2(total), o)
-    ret = sum2(ret)
-    rd[...] = ret[:, 0:128]
-    rs[...] = ret[:, 128:256]
+    hb = jnp.broadcast_to(small_row(hi, his), (rows, 256))
+    zero = jnp.zeros((rows, 256), bf16)
+    big = [jnp.where(hb == jnp.full((rows, 256), float(h), bf16), vs, zero) for h in range(his)]
+    acc = dot_nt(jnp.concatenate(big, axis=0), o)
+    parts = []
+    for h in range(his):
+        total = tf[:, h * 256 : (h + 1) * 256] + sum2(acc[h * rows : (h + 1) * rows])
+        tf2[:, h * 256 : (h + 1) * 256] = total
+        parts.append(stack2(total))
+    y = dot_nn(jnp.concatenate(parts, axis=0), o)
+    back = jnp.zeros((F_ROWS, 256), f32)
+    for h in range(his):
+        mine = jnp.broadcast_to(hi, (F_ROWS, 256)) == h
+        back = jnp.where(mine, sum2(y[h * rows : (h + 1) * rows]), back)
+    rd[...] = back[:, 0:128]
+    rs[...] = back[:, 128:256]
 
 
 def owner_lines(te, tc, gd, gs, gboth, te2, tc2, rd, rs, rb):
@@ -594,7 +613,7 @@
     loads.append(pltpu.make_async_copy(sol_in, sol, load_sem.at[7]))
     loads.append(pltpu.make_async_copy(forc_in, forc, load_sem.at[8]))
     early = [pltpu.make_async_copy(owner_in, owner, load_sem.at[9]), pltpu.make_async_copy(ids_in, ids, load_sem.at[10])]
-    for copy in early + loads:
+    for copy in early + loads[7:8] + loads[:7] + loads[8:]:
         copy.start()
 
     barrier = pltpu.get_barrier_semaphore()
@@ -622,26 +641,35 @@
         return copy
 
     half = NODES // 2
-    moves = []
+    moves = [[] for _ in range(8)]
 
     def fill(m, x):
         for ref, val in zip((p0, p1, p2, p3), pack_block(x, pa[...], pb[...])):
             ref[m] = val
 
-    def push(m):
-        for n, (src, dst, last, peer) in enumerate((
-            (p2, a3, f3, prev_sub), (p3, a2, f2, next_sub), (p0, a1, f1, prev_dom), (p1, a0, f0, next_dom),
-        )):
+    def push_sub(m):
+        for n, (src, dst, last, peer) in enumerate(((p2, a3, f3, prev_sub), (p3, a2, f2, next_sub))):
             to = last if m == 7 else dst.at[m]
-            moves.append(remote(src.at[m], to, move_send.at[m, n], move_recv.at[m, n], peer))
-
+            moves[m].append(remote(src.at[m], to, move_send.at[m, n], move_recv.at[m, n], peer))
+
+    def push_dom(m):
+        for n, (src, dst, last, peer) in enumerate(((p0, a1, f1, prev_dom), (p1, a0, f0, next_dom))):
+            to = last if m == 7 else dst.at[m]
+            moves[m].append(remote(src.at[m], to, move_send.at[m, n + 2], move_recv.at[m, n + 2], peer))
+
+    loads[7].wait()
+
+    def gradients(c, carry):
+        gradient_chunk(c, sol, kmat, ga, gb2, gc2)
+        return carry
+
+    lax.fori_loop(0, 4, gradients, 0)
     for m in range(7):
         loads[m].wait()
         fill(m, met[m][...].reshape(NODES, E))
-        if m < 5:
-            push(m)
-
-    loads[7].wait()
+        if m < 4:
+            push_sub(m)
+        push_dom(m)
 
     def chunk(c, carry):
         apply_chunk(c, sol, met, kmat, im, dg, rix, vf, ve, vc, ga, gb2, gc2)
@@ -660,6 +688,8 @@
         send(3, md, gd, next_dom),
         send(4, md.at[pl.ds(LINES - BOTH, BOTH)], gb, next_both),
     ]
+    for m in range(4, 5):
+        push_sub(m)
     pc[...] = onehot(small_row(arrive, 256), 256)
     pd[...] = onehot(small_row(swapped(arrive), 256), 256)
     for copy in face_out:
@@ -671,7 +701,7 @@
     owner_lines(te, tc, gd, gs, gb, te2, tc2, sd, ss, sb)
     line_back = [send(7, ss, rs, prev_sub), send(8, sd, rd, prev_dom), send(9, sb, rb, prev_both)]
     for m in range(5, 7):
-        push(m)
+        push_sub(m)
     for copy in face_back:
         copy.wait()
     gather_faces(keys, tf2, rfd, rfs, tfs, og, gf)
@@ -681,12 +711,13 @@
     loads[8].wait()
     place_relax(im, dg, gf, ge, gc, sol, forc, rel)
     fill(7, rel[...].reshape(NODES, E))
-    push(7)
+    push_sub(7)
+    push_dom(7)
     for m in range(7):
-        for copy in moves[4 * m : 4 * m + 4]:
+        for copy in moves[m]:
             copy.wait()
         land_block(met[m], [a[m] for a in (a0, a1, a2, a3)], pc[...], pd[...], departed, met[m])
-    for copy in moves[28:]:
+    for copy in moves[7]:
         copy.wait()
 
 
@@ -697,7 +728,6 @@
     box = pltpu.VMEM((N, N, N, E), f32)
     planes = pltpu.VMEM((4, NODES, 128), f32)
     face, line, both = (pltpu.VMEM((r, 128), f32) for r in (F_ROWS, LINES, BOTH))
-    work = pltpu.VMEM((NODES, 128), f32)
     moved = pltpu.VMEM((8, half, 128), f32)
     came = pltpu.VMEM((7, half, 128), f32)
     return pl.pallas_call(
@@ -726,7 +756,7 @@
             pltpu.VMEM((2 * F_ROWS, 6 * E), bf16),
             pltpu.VMEM((32, 12 * E), bf16),
             pltpu.VMEM((8, 8 * E), f32),
-            work, work, work,
+            planes, planes, planes,
             pltpu.VMEM((2 * F_ROWS * F_HI, 6 * E), bf16),
             pltpu.VMEM((256, 6 * E), bf16),
             pltpu.VMEM((2 * F_ROWS * F_HI, 256), f32),

time: 49.9 us -> 50 us (level)
  no operation moved by 1% of the time
where the time goes in v6:
time: 50 us; the launch traced here: 49.8 us
  Pallas kernels  47.4 us (95%)
  local copies, waits for them, and re-layouts  1.61 us (3%)
  between operations  0.85 us (2%)
    pallas_call x1, Pallas kernels, main_call(): pl.pallas_call(main_kernel, in_specs=[hbm] * 5, out_specs=[vm] * 12, out_...  43.5 us
    pallas_call x1, Pallas kernels, land(): pl.pallas_call(land_kernel, in_specs=[pl.BlockSpec(memory_space=pltpu.SME...  3.91 us
    unnamed x4, local copies, waits for them, and re-layouts  1.52 us

profile of v6, /device:TPU:0, one launch (start us, length us, event | category | flops | bytes accessed | tf_op | source)
XLA Modules:
  0.0 49.8 jit_solution(12177809386175854078)
XLA Ops:
  0.7 0.1 stack.27.devs
  0.8 0.0 copy-start
  0.8 0.8 %copy-done = s32[26,512]{1,0:T(8,128)S(1)} copy-done((s32[26,512]{1,0:T(8,128)S(1)}, s32[26,512]{1,0:T(8,128)}, u32[]{:S(2)}) %copy-start) | copy-done | bytes 53272
  1.6 0.0 copy-start.1
  1.6 0.7 %copy-done.1 = s32[512]{0:T(512)S(1)} copy-done((s32[512]{0:T(512)S(1)}, s32[512]{0:T(512)}, u32[]{:S(2)}) %copy-start.1) | copy-done | bytes 2072
  2.3 43.5 %main.1 = (f32[8,8,8,512]{3,2,1,0:T(8,128)S(1)}, f32[8,8,8,512]{3,2,1,0:T(8,128)S(1)}, f32[8,8,8,512]{3,2,1,0:T(8,128)S(1)}, f32[8,8,8,512]{3,2,1,0:T(8,128)S(1)...) custom-call(s32[1,512]{1,0:T(1,128)S(1)} %bitcast.7, ...), custom_call_target="tpu_custom_call" | custom-call | tf_op jit(solution)/shard_map/main/pallas_call | solution.py:733
  45.8 3.9 %land.1 = (f32[7,8,8,8,512]{4,3,2,1,0:T(8,128)}, f32[8,8,8,512]{3,2,1,0:T(8,128)}) custom-call(s32[6]{0:T(128)S(1)} %stack.27.devs, s32[1,512]{1,0:T(1,128)S(1)} %bitcast.8, f32[8,8,8,512]{3,2,1,0:T(8,128)S(1)} %get-tuple-element.16.m0, f32[8,8,8,512]{3,2,1,0:T(8,128)S(1)} %get-tuple-element.17.m1, f32[8,8,8,512]{3,2,1,0:T(8,128)S(1)} %get-tuple-element.18.m2, ...), custom_call_target="tpu_custom_call" | custom-call | tf_op jit(solution)/shard_map/land/pallas_call | solution.py:811
Async XLA Ops:
  0.8 0.8 %copy-start = (s32[26,512]{1,0:T(8,128)S(1)}, s32[26,512]{1,0:T(8,128)}, u32[]{:S(2)}) copy-start(s32[26,512]{1,0:T(8,128)} %ids_in.1) | copy-start | bytes 159748
  1.6 0.7 %copy-start.1 = (s32[512]{0:T(512)S(1)}, s32[512]{0:T(512)}, u32[]{:S(2)}) copy-start(s32[512]{0:T(512)} %param.9) | copy-start | bytes 6148
